TPU v7x, 32 devices: a whole 2x2x4 slice. The times are simulated.
32 devices in a mesh: groups: 2 (over x), dp: 16 (over z, y, core).
Axes of the slice: x: 2, y: 2, z: 4, core: 2. Of those that a mesh axis runs over, the one named last changes fastest.
Arguments:
- fingerprints: bfloat16 [32768, 512], P(('groups', 'dp')), parts along dimension 0, may hold values from 0 to 1
- targets: bfloat16 [32768, 128], P(('groups', 'dp')), parts along dimension 0, may hold values from -6 to 6
- landmark_index: int32 [4096], P('groups'), parts along dimension 0, may hold values from 0 to 16383, as said below
Outputs:
- rhs: float32 [4096, 128], P(('groups', 'dp')), parts along dimension 0
- panel: float32 [4096, 256], P(('groups', 'dp')), parts along dimension 0
- trailing: float32 [4096, 2048], P(('groups', 'dp')), parts along dimension 0
There are 2 independent parts, one for each index of `groups`. A program takes and returns all parts, laid end to end along the dimension named above; each array names one. Nothing has to cross between parts.
Inputs may be any that keep to these rules, and one draw needn't show every extreme that they name: `landmark_index`: distinct rows of the window; row r belongs to index r // 1024 of dp; each index of dp owns at most 256 landmarks and a quarter of them own exactly 256.
All inputs are finite; a program needn't handle non-finite values.
Results may differ from a plain program's by a relative error of at most 0.0029.
Values may be sent and summed in bfloat16 or wider, within the bound.
No kernel may reach another device: no remote copies, remote signals or barrier semaphores. Data moves between devices by JAX's collectives and lax.ppermute only.
A program may use at most 64 MiB of HBM per device.

v0:
```python
import math

import jax
import jax.numpy as jnp
from jax import lax
from jax.sharding import PartitionSpec as P

PB = 256


ridge_weight = 0.01


def sq_norms(row_block):
    wide_rows = row_block.astype(jnp.float32)
    return jnp.sum(wide_rows * wide_rows, axis=1)


def tanimoto(row_block, landmark_fps, landmark_norms):
    inner_prod = lax.dot_general(
        row_block, landmark_fps, (((1,), (1,)), ((), ())), preferred_element_type=jnp.float32
    )
    row_norms = sq_norms(row_block)
    return inner_prod / (row_norms[:, None] + landmark_norms[None, :] - inner_prod)


def local(fingerprints, targets, landmark_index):
    rows_dev = fingerprints.shape[0]
    devices = lax.axis_size("dp")
    total_rows = rows_dev * devices
    landmarks = landmark_index.shape[0]
    land_share = landmarks // devices
    position = lax.axis_index("dp")
    owner_dev = landmark_index // rows_dev
    offset = landmark_index % rows_dev
    is_mine = owner_dev == position
    capacity = 2 * land_share
    owner_onehot = (owner_dev[:, None] == jnp.arange(devices, dtype=jnp.int32)[None, :]).astype(
        jnp.int32
    )
    owner_rank = jnp.sum(jnp.cumsum(owner_onehot, axis=0) * owner_onehot, axis=1) - 1
    slot_rows = (
        jnp.zeros((capacity,), jnp.int32)
        .at[jnp.where(is_mine, owner_rank, capacity)]
        .set(offset, mode="drop")
    )
    packed = fingerprints[slot_rows]
    gathered = lax.all_gather(packed, "dp", axis=0, tiled=True)
    landmark_fps = gathered[owner_dev * capacity + owner_rank]
    landmark_norms = sq_norms(landmark_fps)
    kernel = tanimoto(fingerprints, landmark_fps, landmark_norms)
    col_total = lax.psum(jnp.sum(kernel, axis=0), "dp")
    col_mean = col_total / total_rows
    centred = (kernel - col_mean[None, :]).astype(jnp.bfloat16)
    joined = jnp.concatenate([centred, targets], axis=1)
    totals = lax.psum_scatter(
        lax.dot_general(
            centred, joined, (((0,), (0,)), ((), ())), preferred_element_type=jnp.float32
        ),
        "dp",
        scatter_dimension=0,
        tiled=True,
    )
    gram_rows = totals[:, :landmarks]
    rhs_rows = totals[:, landmarks:]
    rhs = rhs_rows / math.sqrt(ridge_weight * total_rows)
    own_fps = lax.dynamic_slice_in_dim(landmark_fps, position * land_share, land_share, 0)
    system_rows = gram_rows / (ridge_weight * total_rows) + tanimoto(
        own_fps, landmark_fps, landmark_norms
    )
    panel_width = PB
    column_block = lax.all_gather(system_rows[:, :panel_width], "dp", axis=0, tiled=True)
    corner = jnp.linalg.cholesky(column_block[:panel_width])
    panel_full = lax.linalg.triangular_solve(
        corner, column_block, left_side=False, lower=True, transpose_a=True
    )
    panel_own = lax.dynamic_slice_in_dim(panel_full, position * land_share, land_share, 0)
    trailing = system_rows - jnp.dot(panel_own, panel_full.T, precision=lax.Precision.HIGHEST)
    return (rhs, panel_own, trailing)


def solution(mesh):
    in_specs = (P(("groups", "dp"), None), P(("groups", "dp"), None), P("groups"))
    out_specs = (P(("groups", "dp"), None), P(("groups", "dp"), None), P(("groups", "dp"), None))
    return jax.shard_map(local, mesh=mesh, in_specs=in_specs, out_specs=out_specs, check_vma=False)
```

profile of v0, /device:TPU:0, one launch (start us, length us, event | category | flops | bytes accessed | tf_op | source)
XLA Modules:
  0.0 448.4 jit_solution(3361861722444120776)
XLA Ops:
  8.0 4.5 %reduce-window.6 = s32[16,16,128]{2,1,0:T(8,128)S(1)} reduce-window(s32[16,16,128]{2,1,0:T(8,128)S(1)} %fusion.11, s32[]{:T(128)} %copy.39), window={size=1x1x128 pad=0_0x0_0x127_0}, to_apply=%region_0.1 | reduce-window | flops 4161536 | bytes 262148 | tf_op jit(solution)/shard_map/reduce-window
  13.4 8.0 %scatter_custom_fusion = s32[256]{0:T(256)S(1)} fusion(s32[2048]{0:T(1024)S(1)} %get-tuple-element.32, s32[2048]{0:T(1024)S(1)} %get-tuple-element.33, s32[]{:T(128)} %copy.39), kind=kCustom, calls=%fused_computation.73 | custom fusion | bytes 1028 | tf_op jit(solution)/shard_map/scatter | solution.py:45
  21.5 3.3 gather_fusion
  24.8 1.1 copy.15
  26.2 52.0 %all-gather.6.cloned.1.call-done = bf16[4096,512]{1,0:T(8,128)(2,1)} async-done(((bf16[256,512]{1,0:T(8,128)(2,1)}), bf16[4096,512]{1,0:T(8,128)(2,1)}) %all-gather.6.cloned.1.call-update) | async-done | bytes 4194320 | tf_op jit(solution)/shard_map/all_gather | solution.py:48
  78.2 10.3 %gather_fusion.1 = bf16[2048,512]{1,0:T(8,128)(2,1)S(1)} fusion(bf16[4096,512]{1,0:T(8,128)(2,1)} %all-gather.6.cloned.1.call-done, s32[2048]{0:T(1024)S(1)} %get-tuple-element.31), kind=kCustom, calls=%fused_computation.1 | custom fusion | bytes 4202496 | tf_op jit(solution)/shard_map/gather | solution.py:49
  89.0 5.0 %fusion.30 = (f32[2048]{0:T(1024)S(1)}, f32[1024,2048]{0,1:T(8,128)}) fusion(f32[2048]{0:T(1024)S(1)} %multiply_reduce_fusion, f32[1024]{0:T(1024)S(1)} %multiply_reduce_fusion.1, bf16[2048,512]{1,0:T(8,128)(2,1)S(1)} %gather_fusion.1, bf16[1024,512]{1,0:T(8,128)(2,1)S(1)} %copy-done), kind=kOutput, calls=%fused_computation.78 | convolution fusion | flops 2155870208 | bytes 11554816 | tf_op jit(solution)/shard_map/dot_general | solution.py:20
  94.0 31.6 %psum.7 = f32[2048]{0:T(1024)S(1)} all-reduce(f32[2048]{0:T(1024)S(1)} %get-tuple-element.35), channel_id=1, replica_groups=mesh['groups'=2,'dp'=16] {'dp'}, use_global_device_ids=true, to_apply=%region_7.8 | all-reduce | flops 2048 | bytes 16384 | tf_op jit(solution)/shard_map/psum | solution.py:52
  125.6 3.9 subtract_convert_fusion
  129.5 13.4 %fusion = f32[2048,2176]{0,1:T(8,128)} fusion(bf16[1024,2048]{0,1:T(8,128)(2,1)S(1)} %subtract_convert_fusion, bf16[1024,128]{0,1:T(8,128)(2,1)S(1)} %copy.15), kind=kOutput, calls=%fused_computation.7 | convolution fusion | flops 9135718400 | bytes 22282240 | tf_op jit(solution)/shard_map/dot_general | solution.py:57
  143.3 183.7 %reduce-scatter.2.cloned.1.call-done = f32[128,2176]{0,1:T(8,128)} async-done(((f32[2048,2176]{0,1:T(8,128)}), f32[128,2176]{0,1:T(8,128)}) %reduce-scatter.2.cloned.1.call-update) | async-done | bytes 1114128 | tf_op jit(solution)/shard_map/reduce_scatter | solution.py:56
  326.9 1.9 fusion.4
  332.1 38.8 %all-gather.4.cloned.1.call-done = f32[2048,256]{0,1:T(8,128)} async-done(((f32[128,256]{0,1:T(8,128)}), f32[2048,256]{0,1:T(8,128)}) %all-gather.4.cloned.1.call-update) | async-done | bytes 2097168 | tf_op jit(solution)/shard_map/all_gather | solution.py:72
  371.0 1.1 slice.86
  373.2 11.7 %cholesky.50 = f32[128,128]{1,0:T(8,128)S(1)} custom-call(f32[128,128]{1,0:T(8,128)S(1)} %cholesky.118), custom_call_target="Cholesky" | custom-call | tf_op jit(solution)/shard_map/jit(cholesky)/cholesky | solution.py:73
  385.0 9.8 %custom-call.14 = f32[1,128,128]{1,2,0:T(8,128)S(1)} custom-call(f32[1,128,128]{2,1,0:T(8,128)S(1)} %get-tuple-element.30), custom_call_target="InvertDiagBlocksLowerTriangular" | custom-call | tf_op jit(solution)/shard_map/jit(cholesky)/cholesky | solution.py:73
  395.3 11.7 %cholesky.105 = f32[128,128]{1,0:T(8,128)S(1)} custom-call(f32[128,128]{1,0:T(8,128)S(1)} %convolution_subtract_fusion.2), custom_call_target="Cholesky" | custom-call | tf_op jit(solution)/shard_map/jit(cholesky)/cholesky | solution.py:73
  409.1 4.1 while.1
  409.9 1.4 bitcast_dynamic-update-slice_fusion.2
  411.8 1.4 bitcast_dynamic-update-slice_fusion.2
  413.2 19.7 %custom-call.15 = f32[2,128,128]{1,2,0:T(8,128)S(1)} custom-call(f32[2,128,128]{2,1,0:T(8,128)S(1)} %get-tuple-element.10), custom_call_target="InvertDiagBlocksLowerTriangular" | custom-call | tf_op jit(solution)/shard_map/triangular_solve | solution.py:74
  432.9 1.1 fusion.5
  436.2 3.6 convolution_subtract_fusion
  440.6 1.3 copy.23
  (51 shorter events, 12.6 us)
Async XLA Ops:
  7.2 18.7 %copy-start = (bf16[1024,512]{1,0:T(8,128)(2,1)S(1)}, bf16[1024,512]{1,0:T(8,128)(2,1)}, u32[]{:S(2)}) copy-start(bf16[1024,512]{1,0:T(8,128)(2,1)} %param.3) | copy-start | bytes 3145732
  7.2 71.0 %all-gather.6.cloned.1.call-start = ((), (), s32[]{:S(2)}) async-start(), calls=%async_computation.3 | async-start | bytes 4456448 | tf_op jit(solution)/shard_map/all_gather | solution.py:48
  24.8 302.2 %reduce-scatter.2.cloned.1.call-start = ((), (), s32[]{:S(2)}) async-start(), calls=%async_computation.1 | async-start | bytes 18939904 | tf_op jit(solution)/shard_map/reduce_scatter | solution.py:56
  142.9 228.1 %all-gather.4.cloned.1.call-start = ((), (), s32[]{:S(2)}) async-start(), calls=%async_computation.2 | async-start | bytes 2228224 | tf_op jit(solution)/shard_map/all_gather | solution.py:72
  328.9 1.0 copy-start.2
  371.0 61.9 %copy-start.1 = (f32[2048,256]{0,1:T(8,128)S(1)}, f32[2048,256]{0,1:T(8,128)}, u32[]{:S(2)}) copy-start(f32[2048,256]{0,1:T(8,128)} %all-gather.4.cloned.1.call-done) | copy-start | bytes 6291460
  434.0 2.2 copy-start.3
Sparse Core Ops, SparseCore 0:
  24.9 53.2 all-gather.5
  143.0 183.8 reduce-scatter.1
  330.7 40.2 all-gather.3
where the time goes:
time: 449 us; the launch traced here: 448 us
  waiting for transfers between devices  275 us (61%)
  other arithmetic  66 us (15%)
  local copies, waits for them, and re-layouts  32.8 us (7%)
  blocking collectives  31.6 us (7%)
  matrix products  27.6 us (6%)
  between operations  15.3 us (3%)
    reduce_scatter x1, waiting for transfers between devices, local(): lax.psum_scatter(lax.dot_general(centred, joined, (((0,), (0,)), ((), ())...  184 us
    all_gather x1, waiting for transfers between devices, local(): gathered = lax.all_gather(packed, 'dp', axis=0, tiled=True)  52 us
    all_gather x1, waiting for transfers between devices, local(): lax.all_gather(system_rows[:, :panel_width], 'dp', axis=0, tiled=True)  38.8 us
    another operation x6, other arithmetic, local(): corner = jnp.linalg.cholesky(column_block[:panel_width])  34 us
    psum x1, blocking collectives, local(): col_total = lax.psum(jnp.sum(kernel, axis=0), 'dp')  31.6 us
    another operation x4, other arithmetic, local(): lax.linalg.triangular_solve(corner, column_block, left_side=False, lower=...  19.7 us
    dot_general x1, matrix products, local(): lax.dot_general(centred, joined, (((0,), (0,)), ((), ())), preferred_elem...  13.4 us
    gather x1, local copies, waits for them, and re-layouts, local(): landmark_fps = gathered[owner_dev * capacity + owner_rank]  10.3 us
  transfers between devices with their start and end apart: 3, of which 3 were waited for; matrix products, arithmetic and copies ran while one was open for 1% of the time, Pallas kernels for 0%

commit v1 on v0

--- a/solution.py
+++ b/solution.py
@@ -24,7 +24,7 @@
     return inner_prod / (row_norms[:, None] + landmark_norms[None, :] - inner_prod)
 
 
-def local(fingerprints, targets, landmark_index):
+def local_any(fingerprints, targets, landmark_index):
     rows_dev = fingerprints.shape[0]
     devices = lax.axis_size("dp")
     total_rows = rows_dev * devices
@@ -79,7 +79,176 @@
     return (rhs, panel_own, trailing)
 
 
+CORE = [(i, i ^ 1) for i in range(16)]
+ROW = [(i, i ^ 2) for i in range(16)]
+
+
+def rotate(step):
+    return [(i, (i + 4 * step) % 16) for i in range(16)]
+
+
+def send(x, perm):
+    return lax.ppermute(x, "dp", perm)
+
+
+def highest(a, b):
+    return lax.dot_general(
+        a,
+        b,
+        (((0,), (0,)), ((), ())),
+        precision=lax.Precision.HIGHEST,
+        preferred_element_type=jnp.float32,
+    )
+
+
+def gram(a, b):
+    return lax.dot_general(a, b, (((0,), (0,)), ((), ())), preferred_element_type=jnp.float32)
+
+
+def gather_chips(x):
+    pair = jnp.concatenate([x, send(x, ROW)], axis=0)
+    return jnp.concatenate([pair] + [send(pair, rotate(s)) for s in (1, 2, 3)], axis=0)
+
+
+def landmarks_everywhere(fingerprints, landmark_index):
+    rows_dev = fingerprints.shape[0]
+    devices = lax.axis_size("dp")
+    landmarks = landmark_index.shape[0]
+    land_share = landmarks // devices
+    position = lax.axis_index("dp")
+    owner_dev = landmark_index // rows_dev
+    offset = landmark_index % rows_dev
+    is_mine = owner_dev == position
+    capacity = 2 * land_share
+    owner_onehot = (owner_dev[:, None] == jnp.arange(devices, dtype=jnp.int32)[None, :]).astype(
+        jnp.int32
+    )
+    owner_rank = jnp.sum(jnp.cumsum(owner_onehot, axis=0) * owner_onehot, axis=1) - 1
+    slot_rows = (
+        jnp.zeros((capacity,), jnp.int32)
+        .at[jnp.where(is_mine, owner_rank, capacity)]
+        .set(offset, mode="drop")
+    )
+    packed = fingerprints[slot_rows]
+    gathered = lax.all_gather(packed, "dp", axis=0, tiled=True)
+    return gathered[owner_dev * capacity + owner_rank]
+
+
+def local_16(fingerprints, targets, landmark_index):
+    rows_dev = fingerprints.shape[0]
+    total_rows = rows_dev * 16
+    landmarks = landmark_index.shape[0]
+    share = landmarks // 16
+    width = PB
+    position = lax.axis_index("dp")
+    core = position % 2
+    row = (position // 2) % 2
+    layer = position // 4
+    scale = 1.0 / (ridge_weight * total_rows)
+
+    fps = jnp.concatenate([fingerprints, send(fingerprints, CORE)], axis=0)
+    tgs = jnp.concatenate([targets, send(targets, CORE)], axis=0)
+    chip_rows = 2 * rows_dev
+    landmark_fps = landmarks_everywhere(fingerprints, landmark_index)
+    norms = sq_norms(landmark_fps)
+    kernel = tanimoto(fps, landmark_fps, norms)
+    mean = jnp.sum(kernel, axis=0) / chip_rows
+    centred = (kernel - mean[None, :]).astype(jnp.bfloat16)
+    target_sum = jnp.sum(tgs.astype(jnp.float32), axis=0)
+    own_cols = lax.dynamic_slice_in_dim(
+        centred.reshape(chip_rows, 8, 2, share), core, 1, axis=2
+    ).reshape(chip_rows, 8 * share)
+
+    first = gram(own_cols[:, :share], centred)
+    lead = jnp.sum(first, axis=0)
+    lead_own = lax.dynamic_slice_in_dim(lead, core * share, share, 0)
+    lead_mass = jnp.sum(lead_own)
+    usable = lead_mass > 1e-3 * jnp.sum(jnp.abs(lead_own))
+    lead_weight = jnp.where(usable, 1.0 / jnp.where(usable, lead_mass, 1.0), 0.0)
+    lead = lax.reduce_precision(lead, 8, 7).astype(jnp.bfloat16)
+
+    def lead_outer(start, right):
+        left = lax.dynamic_slice_in_dim(lead, start, share, 0)
+        return lead_weight * gram(left[None, :], right[None, :])
+
+    chip_stats = gather_chips(jnp.concatenate([mean, target_sum])[None, :])
+    means, target_sums = chip_stats[:, :landmarks], chip_stats[:, landmarks:]
+    leads = gather_chips(
+        jnp.concatenate([lead.astype(jnp.float32), jnp.broadcast_to(lead_weight, (128,))])[None, :]
+    )
+    leads, lead_weights = leads[:, :landmarks], leads[:, landmarks : landmarks + 1]
+    shift = means - jnp.mean(means, axis=0, keepdims=True)
+    left_terms = jnp.concatenate([shift * chip_rows, leads], axis=0)
+    right_terms = jnp.concatenate([shift, leads * lead_weights], axis=0)
+
+    def add_back(start):
+        return highest(lax.dynamic_slice_in_dim(left_terms, start, share, 1), right_terms)
+
+    first_rest = (first - lead_outer(core * share, lead)).astype(jnp.bfloat16)
+    quarter = share // 4
+
+    def quarter_of(q):
+        return lax.dynamic_slice_in_dim(first_rest, (q % 4) * quarter, quarter, 0)
+
+    part = quarter_of(layer).astype(jnp.float32)
+    for s in (2, 1, 3):
+        part = part + send(quarter_of(layer + s), rotate(s)).astype(jnp.float32)
+    part = part.astype(jnp.bfloat16)
+    part = part.astype(jnp.float32) + send(part, ROW).astype(jnp.float32)
+    part = part.astype(jnp.bfloat16)
+    pieces = jnp.zeros((4,) + part.shape, jnp.bfloat16)
+    pieces = lax.dynamic_update_index_in_dim(pieces, part, layer, 0)
+    for s in (2, 1, 3):
+        pieces = lax.dynamic_update_index_in_dim(
+            pieces, send(part, rotate(s)), (layer + 4 - s) % 4, 0
+        )
+    block_fps = lax.dynamic_slice_in_dim(landmark_fps, core * share, share, 0)
+    block = (pieces.reshape(share, landmarks).astype(jnp.float32) + add_back(core * share)) * scale
+    block = block + tanimoto(block_fps, landmark_fps, norms)
+    other = send(block, CORE)
+    panel_rows = lax.dynamic_slice_in_dim(
+        jnp.concatenate([block, other, block], axis=0), core * share, 2 * share, 0
+    )
+    corner = jnp.linalg.cholesky(panel_rows[:, :width])
+    factor = lax.linalg.triangular_solve(corner, panel_rows, left_side=True, lower=True)
+
+    right = jnp.concatenate([centred[:, width:], tgs], axis=1)
+    lead_right = jnp.concatenate([lead[width:], jnp.zeros((tgs.shape[1],), jnp.bfloat16)])
+
+    def row_sum(s):
+        there = (layer + s) % 4
+        left = lax.dynamic_slice_in_dim(own_cols, there * 2 * share, 2 * share, 1)
+        start = (there * 4 + core) * share
+        outer = jnp.concatenate(
+            [lead_outer(start, lead_right), lead_outer(start + 2 * share, lead_right)], axis=0
+        )
+        out = (gram(left, right) - outer).astype(jnp.bfloat16)
+        mine = lax.dynamic_slice_in_dim(out, row * share, share, 0)
+        theirs = lax.dynamic_slice_in_dim(out, (1 - row) * share, share, 0)
+        return mine.astype(jnp.float32) + send(theirs, ROW).astype(jnp.float32)
+
+    own = 0.0
+    for s in (2, 1, 3):
+        own = own + send(row_sum(s).astype(jnp.bfloat16), rotate(s)).astype(jnp.float32)
+    own = own + row_sum(0)
+    start = position * share
+    own_fps = lax.dynamic_slice_in_dim(landmark_fps, start, share, 0)
+    rest = (own[:, : landmarks - width] + add_back(start)[:, width:]) * scale + tanimoto(
+        own_fps, landmark_fps[width:], norms[width:]
+    )
+    own_shift = lax.dynamic_slice_in_dim(shift, start, share, 1)
+    rhs = (own[:, landmarks - width :] + highest(own_shift, target_sums)) / math.sqrt(
+        ridge_weight * total_rows
+    )
+    own_panel = lax.dynamic_slice_in_dim(panel_rows, start, share, 1)
+    own_factor = lax.dynamic_slice_in_dim(factor, start, share, 1)
+    system_rows = jnp.concatenate([own_panel.T, rest], axis=1)
+    trailing = system_rows - highest(own_factor, factor)
+    return (rhs, own_factor.T, trailing)
+
+
 def solution(mesh):
+    local = local_16 if mesh.shape["dp"] == 16 else local_any
     in_specs = (P(("groups", "dp"), None), P(("groups", "dp"), None), P("groups"))
     out_specs = (P(("groups", "dp"), None), P(("groups", "dp"), None), P(("groups", "dp"), None))
     return jax.shard_map(local, mesh=mesh, in_specs=in_specs, out_specs=out_specs, check_vma=False)

time: 449 us -> 389 us (0.87)
  the two profiles are of different devices: /device:TPU:0 before, /device:TPU:18 now
where the time goes in v1:
time: 389 us; the launch traced here: 384 us
  waiting for transfers between devices  121 us (31%)
  other arithmetic  83.7 us (22%)
  matrix products  76.4 us (20%)
  local copies, waits for them, and re-layouts  50.6 us (13%)
  starting transfers between devices  33.6 us (9%)
  between operations  18.4 us (5%)
    ppermute x25, waiting for transfers between devices, send(): return lax.ppermute(x, 'dp', perm)  75.4 us
    dot_general x5, matrix products, gram(): lax.dot_general(a, b, (((0,), (0,)), ((), ())), preferred_element_type=jn...  52.1 us
    all_gather x1, waiting for transfers between devices, landmarks_everywhere(): gathered = lax.all_gather(packed, 'dp', axis=0, tiled=True)  46 us
    another operation x6, other arithmetic, local_16(): corner = jnp.linalg.cholesky(panel_rows[:, :width])  34 us
    ppermute x25, starting transfers between devices, send(): return lax.ppermute(x, 'dp', perm)  33.6 us
    another operation x4, other arithmetic, local_16(): lax.linalg.triangular_solve(corner, panel_rows, left_side=True, lower=True)  22.1 us
    gather x1, local copies, waits for them, and re-layouts, landmarks_everywhere(): return gathered[owner_dev * capacity + owner_rank]  10.5 us
    scatter x1, local copies, waits for them, and re-layouts, landmarks_everywhere(): slot_rows = jnp.zeros((capacity,), jnp.int32).at[jnp.where(is_mine, owner...  8.04 us
  transfers between devices with their start and end apart: 26, of which 8 were waited for; matrix products, arithmetic and copies ran while one was open for 21% of the time, Pallas kernels for 0%

profile of v1, /device:TPU:18, one launch (start us, length us, event | category | flops | bytes accessed | tf_op | source)
XLA Modules:
  0.0 384.4 jit_solution(13063732241315012073)
XLA Ops:
  8.0 4.5 %reduce-window.6 = s32[16,16,128]{2,1,0:T(8,128)S(1)} reduce-window(s32[16,16,128]{2,1,0:T(8,128)S(1)} %fusion.32, s32[]{:T(128)} %copy.53), window={size=1x1x128 pad=0_0x0_0x127_0}, to_apply=%region_0.1 | reduce-window | flops 4161536 | bytes 262148 | tf_op jit(solution)/shard_map/reduce-window
  13.4 8.0 %scatter_custom_fusion = s32[256]{0:T(256)S(1)} fusion(s32[2048]{0:T(1024)S(1)} %get-tuple-element.50, s32[2048]{0:T(1024)S(1)} %get-tuple-element.59, s32[]{:T(128)} %copy.53), kind=kCustom, calls=%fused_computation.174 | custom fusion | bytes 1028 | tf_op jit(solution)/shard_map/scatter | solution.py:130
  21.5 3.3 gather_fusion
  29.9 46.0 %all-gather.3.cloned.1.call-done = bf16[4096,512]{1,0:T(8,128)(2,1)} async-done(((bf16[256,512]{1,0:T(8,128)(2,1)}), bf16[4096,512]{1,0:T(8,128)(2,1)}) %all-gather.3.cloned.1.call-update) | async-done | bytes 4194320 | tf_op jit(solution)/shard_map/all_gather | solution.py:133
  75.9 10.5 %gather_fusion.1 = bf16[2048,512]{1,0:T(8,128)(2,1)S(1)} fusion(bf16[4096,512]{1,0:T(8,128)(2,1)} %all-gather.3.cloned.1.call-done, s32[2048]{0:T(1024)S(1)} %get-tuple-element.49), kind=kCustom, calls=%fused_computation.1 | custom fusion | bytes 4202496 | tf_op jit(solution)/shard_map/gather | solution.py:134
  88.3 5.5 %fusion.21 = (f32[2048]{0:T(1024)S(1)}, f32[2048,2048]{0,1:T(8,128)S(1)}) fusion(f32[2048]{0:T(1024)S(1)} %multiply_reduce_fusion, f32[2048]{0:T(1024)S(1)} %multiply_reduce_fusion.1, bf16[2048,512]{1,0:T(8,128)(2,1)S(1)} %copy-done.5, bf16[2048,512]{1,0:T(8,128)(2,1)S(1)} %gather_fusion.1), kind=kOutput, calls=%fused_computation.55 | convolution fusion | flops 4311742464 | bytes 20996096 | tf_op jit(solution)/shard_map/dot_general | solution.py:20
  93.7 4.9 %subtract_convert_fusion = bf16[2048,2048]{0,1:T(8,128)(2,1)S(1)} fusion(f32[2048]{0:T(1024)S(1)} %broadcast_multiply_fusion.3, f32[2048,2048]{0,1:T(8,128)S(1)} %get-tuple-element.71, f32[2048]{0:T(1024)S(1)} %multiply_reduce_fusion, f32[2048]{0:T(1024)S(1)} %multiply_reduce_fusion.1), kind=kLoop, calls=%fused_computation.6 | loop fusion | flops 20971520 | bytes 25190400 | tf_op jit(solution)/shard_map/convert_element_type | solution.py:156
  98.6 4.3 %slice.120 = bf16[2048,1792]{0,1:T(8,128)(2,1)} slice(bf16[2048,2048]{0,1:T(8,128)(2,1)S(1)} %subtract_convert_fusion), slice={[0:2048], [256:2048]} | slice | bytes 14680064 | tf_op jit(solution)/shard_map/slice | solution.py:215
  103.3 3.9 %fusion.71 = (f32[2048]{0:T(1024)S(1)}, f32[128,2048]{1,0:T(8,128)}) fusion(bf16[2048,2048]{0,1:T(8,128)(2,1)S(1)} %subtract_convert_fusion, bf16[2048,1024]{0,1:T(8,128)(2,1)S(1)} %bitcast.70), kind=kOutput, calls=%fused_computation.183 | convolution fusion | flops 1074001920 | bytes 9969664 | tf_op jit(solution)/shard_map/dot_general | solution.py:105
  119.6 12.5 %fusion = bf16[256,1920]{1,0:T(8,128)(2,1)} fusion(f32[128,1920]{1,0:T(8,128)} %get-tuple-element.52, f32[128,1920]{1,0:T(8,128)} %get-tuple-element.51, bf16[2048,1024]{0,1:T(8,128)(2,1)S(1)} %bitcast.71, s32[]{:T(128)S(6)} %select_n.189, bf16[1024,128]{0,1:T(8,128)(2,1)} %copy-done.17, bf16[1024,128]{0,1:T(8,128)(2,1)S(1)} %copy.26, ...), kind=kOutput, calls=%fused_computation.15 | convolution fusion | flops 2038333440 | bytes 11862020 | tf_op jit(solution)/shard_map/dot_general | solution.py:105
  134.0 10.3 %fusion.1 = bf16[256,1920]{1,0:T(8,128)(2,1)} fusion(f32[128,1920]{1,0:T(8,128)S(1)} %copy-done.12, f32[128,1920]{1,0:T(8,128)S(1)} %get-tuple-element.53, bf16[2048,1024]{0,1:T(8,128)(2,1)S(1)} %bitcast.72, s32[]{:T(128)S(6)} %select_n.200, bf16[1024,128]{0,1:T(8,128)(2,1)} %copy-done.17, bf16[1024,128]{0,1:T(8,128)(2,1)S(1)} %copy.26, ...), kind=kOutput, calls=%fused_computation.16 | convolution fusion | flops 2038333440 | bytes 11862020 | tf_op jit(solution)/shard_map/dot_general | solution.py:105
  146.2 9.7 %fusion.3 = bf16[256,1920]{1,0:T(8,128)(2,1)S(1)} fusion(f32[128,1920]{1,0:T(8,128)S(1)} %get-tuple-element.58, f32[128,1920]{1,0:T(8,128)S(1)} %get-tuple-element.57, bf16[2048,1024]{0,1:T(8,128)(2,1)S(1)} %bitcast.73, s32[]{:T(128)S(6)} %select_n.208, bf16[1024,128]{0,1:T(8,128)(2,1)} %copy-done.17, bf16[1024,128]{0,1:T(8,128)(2,1)S(1)} %copy.26, ...), kind=kOutput, calls=%fused_computation.18 | convolution fusion | flops 2038333440 | bytes 11862020 | tf_op jit(solution)/shard_map/dot_general | solution.py:105
  156.8 15.7 %fusion.2 = bf16[256,1920]{1,0:T(8,128)(2,1)S(1)} fusion(f32[128,1920]{1,0:T(8,128)S(1)} %get-tuple-element.56, f32[128,1920]{1,0:T(8,128)S(1)} %get-tuple-element.55, bf16[2048,1024]{0,1:T(8,128)(2,1)S(1)} %bitcast.74, s32[]{:T(128)S(6)} %select_n.204, bf16[1024,128]{0,1:T(8,128)(2,1)S(1)} %copy-done.18, bf16[1024,128]{0,1:T(8,128)(2,1)S(1)} %copy.26, ...), kind=kOutput, calls=%fused_computation.17 | convolution fusion | flops 2038333440 | bytes 11862020 | tf_op jit(solution)/shard_map/dot_general | solution.py:105
  197.5 34.6 %collective-permute-done.16 = bf16[32,2048]{1,0:T(8,128)(2,1)S(1)} collective-permute-done((bf16[32,2048]{1,0:T(8,128)(2,1)S(1)}, bf16[32,2048]{1,0:T(8,128)(2,1)S(1)}, u32[]{:S(2)}, u32[]{:S(2)}) %collective-permute-start.16) | collective-permute-done | bytes 131104 | tf_op jit(solution)/shard_map/ppermute | solution.py:91
  241.2 4.1 %collective-permute-done.18 = bf16[32,2048]{1,0:T(8,128)(2,1)S(1)} collective-permute-done((bf16[32,2048]{1,0:T(8,128)(2,1)S(1)}, bf16[32,2048]{1,0:T(8,128)(2,1)S(1)}, u32[]{:S(2)}, u32[]{:S(2)}) %collective-permute-start.18) | collective-permute-done | bytes 131104 | tf_op jit(solution)/shard_map/ppermute | solution.py:91
  246.5 3.9 %collective-permute-done.19 = bf16[32,2048]{1,0:T(8,128)(2,1)S(1)} collective-permute-done((bf16[32,2048]{1,0:T(8,128)(2,1)S(1)}, bf16[32,2048]{1,0:T(8,128)(2,1)S(1)}, u32[]{:S(2)}, u32[]{:S(2)}) %collective-permute-start.19) | collective-permute-done | bytes 131104 | tf_op jit(solution)/shard_map/ppermute | solution.py:91
  255.5 5.0 %collective-permute-start.3 = (bf16[128,1920]{1,0:T(8,128)(2,1)S(1)}, bf16[128,1920]{1,0:T(8,128)(2,1)S(1)}, u32[]{:S(2)}, u32[]{:S(2)}) collective-permute-start(bf16[128,1920]{1,0:T(8,128)(2,1)S(1)} %add_convert_fusion.2), channel_id=1, source_target_pairs={{0,8},{1,9},{2,10},{3,11},{4,12},{5,13},{6,14},{7,15},{8,0},{9,1},... | collective-permute-start | bytes 1474568 | tf_op jit(solution)/shard_map/ppermute | solution.py:91
  266.0 17.3 %collective-permute-done.3 = bf16[128,1920]{1,0:T(8,128)(2,1)S(1)} collective-permute-done((bf16[128,1920]{1,0:T(8,128)(2,1)S(1)}, bf16[128,1920]{1,0:T(8,128)(2,1)S(1)}, u32[]{:S(2)}, u32[]{:S(2)}) %collective-permute-start.3) | collective-permute-done | bytes 491552 | tf_op jit(solution)/shard_map/ppermute | solution.py:91
  283.3 11.6 %collective-permute-done.5 = bf16[128,1920]{1,0:T(8,128)(2,1)S(1)} collective-permute-done((bf16[128,1920]{1,0:T(8,128)(2,1)S(1)}, bf16[128,1920]{1,0:T(8,128)(2,1)S(1)}, u32[]{:S(2)}, u32[]{:S(2)}) %collective-permute-start.5) | collective-permute-done | bytes 491552 | tf_op jit(solution)/shard_map/ppermute | solution.py:91
  302.0 11.7 %cholesky.50 = f32[128,128]{1,0:T(8,128)S(1)} custom-call(f32[128,128]{1,0:T(8,128)S(1)} %cholesky.118), custom_call_target="Cholesky" | custom-call | tf_op jit(solution)/shard_map/jit(cholesky)/cholesky | solution.py:212
  313.7 9.8 %custom-call.14 = f32[1,128,128]{1,2,0:T(8,128)S(1)} custom-call(f32[1,128,128]{2,1,0:T(8,128)S(1)} %get-tuple-element.48), custom_call_target="InvertDiagBlocksLowerTriangular" | custom-call | tf_op jit(solution)/shard_map/jit(cholesky)/cholesky | solution.py:212
  325.7 11.7 %cholesky.105 = f32[128,128]{1,0:T(8,128)S(1)} custom-call(f32[128,128]{1,0:T(8,128)S(1)} %convolution_subtract_fusion.4), custom_call_target="Cholesky" | custom-call | tf_op jit(solution)/shard_map/jit(cholesky)/cholesky | solution.py:212
  340.6 5.5 %while.1 = (s32[]{:T(128)}, f32[256,256]{1,0:T(8,128)S(1)}, s32[2,2]{1,0:T(2,128)S(1)}, f32[2,128,128]{2,1,0:T(8,128)}, s32[]{:T(128)}) while((s32[]{:T(128)}, f32[256,256]{1,0:T(8,128)S(1)}, s32[2,2]{1,0:T(2,128)S(1)}, f32[2,128,128]{2,1,0:T(8,128)}, s32[]{:T(128)}) %tuple.57), condition=%wide.while_cond, body=%wide.while_body.sunk | while | flops 2 | bytes 132205 | solution.py:213
  346.1 20.5 %custom-call.15 = f32[2,128,128]{1,2,0:T(8,128)S(1)} custom-call(f32[2,128,128]{2,1,0:T(8,128)} %get-tuple-element.10), custom_call_target="InvertDiagBlocksLowerTriangular" | custom-call | tf_op jit(solution)/shard_map/triangular_solve | solution.py:213
  (195 shorter events, 96.3 us)
Async XLA Ops:
  7.2 68.7 %all-gather.3.cloned.1.call-start = ((), (), s32[]{:S(2)}) async-start(), calls=%async_computation | async-start | bytes 4456448 | tf_op jit(solution)/shard_map/all_gather | solution.py:133
  108.5 65.9 %collective-permute-start.9 = (f32[1,2176]{1,0:T(1,128)}, f32[1,2176]{1,0:T(1,128)}, u32[]{:S(2)}, u32[]{:S(2)}) collective-permute-start(f32[1,2176]{1,0:T(1,128)} %broadcast_in_dim.35), channel_id=1, source_target_pairs={{0,2},{1,3},{2,0},{3,1},{4,6},{5,7},{6,4},{7,5},{8,10},{9,11},{10,... | collective-permute-start | bytes 26120 | tf_op jit(solution)/shard_map/ppermute | solution.py:91
  111.1 67.5 %collective-permute-start.20 = (f32[1,2176]{1,0:T(1,128)S(1)}, f32[1,2176]{1,0:T(1,128)S(1)}, u32[]{:S(2)}, u32[]{:S(2)}) collective-permute-start(f32[1,2176]{1,0:T(1,128)S(1)} %broadcast_in_dim.41), channel_id=1, source_target_pairs={{0,2},{1,3},{2,0},{3,1},{4,6},{5,7},{6,4},{7,5},{8,10},{9,11},{10,... | collective-permute-start | bytes 26120 | tf_op jit(solution)/shard_map/ppermute | solution.py:91
  114.9 76.0 %collective-permute-start.13 = (bf16[32,2048]{1,0:T(8,128)(2,1)}, bf16[32,2048]{1,0:T(8,128)(2,1)}, u32[]{:S(2)}, u32[]{:S(2)}) collective-permute-start(bf16[32,2048]{1,0:T(8,128)(2,1)} %get-tuple-element.40), channel_id=1, source_target_pairs={{0,8},{1,9},{2,10},{3,11},{4,12},{5,13},{6,14},{7,15},{8,0},{9,1},... | collective-permute-start | bytes 393224 | tf_op jit(solution)/shard_map/ppermute | solution.py:91
  116.0 75.5 %collective-permute-start.15 = (bf16[32,2048]{1,0:T(8,128)(2,1)}, bf16[32,2048]{1,0:T(8,128)(2,1)}, u32[]{:S(2)}, u32[]{:S(2)}) collective-permute-start(bf16[32,2048]{1,0:T(8,128)(2,1)} %get-tuple-element.41), channel_id=1, source_target_pairs={{0,12},{1,13},{2,14},{3,15},{4,0},{5,1},{6,2},{7,3},{8,4},{9,5},{1... | collective-permute-start | bytes 393224 | tf_op jit(solution)/shard_map/ppermute | solution.py:91
  175.1 5.7 %collective-permute-start.12 = (f32[2,2176]{1,0:T(2,128)S(1)}, f32[2,2176]{1,0:T(2,128)S(1)}, u32[]{:S(2)}, u32[]{:S(2)}) collective-permute-start(f32[2,2176]{1,0:T(2,128)S(1)} %pad_maximum_fusion.3), channel_id=1, source_target_pairs={{0,12},{1,13},{2,14},{3,15},{4,0},{5,1},{6,2},{7,3},{8,4},{9,5},{1... | collective-permute-start | bytes 52232 | tf_op jit(solution)/shard_map/ppermute | solution.py:91
  176.6 4.7 %collective-permute-start.11 = (f32[2,2176]{1,0:T(2,128)S(1)}, f32[2,2176]{1,0:T(2,128)S(1)}, u32[]{:S(2)}, u32[]{:S(2)}) collective-permute-start(f32[2,2176]{1,0:T(2,128)S(1)} %pad_maximum_fusion.3), channel_id=1, source_target_pairs={{0,8},{1,9},{2,10},{3,11},{4,12},{5,13},{6,14},{7,15},{8,0},{9,1},... | collective-permute-start | bytes 52232 | tf_op jit(solution)/shard_map/ppermute | solution.py:91
  178.6 5.6 %collective-permute-start.10 = (f32[2,2176]{1,0:T(2,128)S(1)}, f32[2,2176]{1,0:T(2,128)S(1)}, u32[]{:S(2)}, u32[]{:S(2)}) collective-permute-start(f32[2,2176]{1,0:T(2,128)S(1)} %pad_maximum_fusion.3), channel_id=1, source_target_pairs={{0,4},{1,5},{2,6},{3,7},{4,8},{5,9},{6,10},{7,11},{8,12},{9,13},{1... | collective-permute-start | bytes 52232 | tf_op jit(solution)/shard_map/ppermute | solution.py:91
  180.7 4.9 %collective-permute-start.23 = (f32[2,2176]{1,0:T(2,128)}, f32[2,2176]{1,0:T(2,128)S(1)}, u32[]{:S(2)}, u32[]{:S(2)}) collective-permute-start(f32[2,2176]{1,0:T(2,128)} %pad_maximum_fusion.4), channel_id=1, source_target_pairs={{0,12},{1,13},{2,14},{3,15},{4,0},{5,1},{6,2},{7,3},{8,4},{9,5},{1... | collective-permute-start | bytes 52232 | tf_op jit(solution)/shard_map/ppermute | solution.py:91
  181.2 6.4 %collective-permute-start.22 = (f32[2,2176]{1,0:T(2,128)}, f32[2,2176]{1,0:T(2,128)S(1)}, u32[]{:S(2)}, u32[]{:S(2)}) collective-permute-start(f32[2,2176]{1,0:T(2,128)} %pad_maximum_fusion.4), channel_id=1, source_target_pairs={{0,8},{1,9},{2,10},{3,11},{4,12},{5,13},{6,14},{7,15},{8,0},{9,1},... | collective-permute-start | bytes 52232 | tf_op jit(solution)/shard_map/ppermute | solution.py:91
  184.2 4.1 %collective-permute-start.21 = (f32[2,2176]{1,0:T(2,128)}, f32[2,2176]{1,0:T(2,128)}, u32[]{:S(2)}, u32[]{:S(2)}) collective-permute-start(f32[2,2176]{1,0:T(2,128)} %pad_maximum_fusion.4), channel_id=1, source_target_pairs={{0,4},{1,5},{2,6},{3,7},{4,8},{5,9},{6,10},{7,11},{8,12},{9,13},{1... | collective-permute-start | bytes 52232 | tf_op jit(solution)/shard_map/ppermute | solution.py:91
  185.6 7.3 %collective-permute-start.14 = (bf16[32,2048]{1,0:T(8,128)(2,1)S(1)}, bf16[32,2048]{1,0:T(8,128)(2,1)}, u32[]{:S(2)}, u32[]{:S(2)}) collective-permute-start(bf16[32,2048]{1,0:T(8,128)(2,1)S(1)} %get-tuple-element.42), channel_id=1, source_target_pairs={{0,4},{1,5},{2,6},{3,7},{4,8},{5,9},{6,10},{7,11},{8,12},{9,13},{1... | collective-permute-start | bytes 393224 | tf_op jit(solution)/shard_map/ppermute | solution.py:91
  187.7 66.4 %collective-permute-start.2 = (bf16[128,1920]{1,0:T(8,128)(2,1)}, bf16[128,1920]{1,0:T(8,128)(2,1)}, u32[]{:S(2)}, u32[]{:S(2)}) collective-permute-start(bf16[128,1920]{1,0:T(8,128)(2,1)} %constant_dynamic-slice_fusion.9), channel_id=1, source_target_pairs={{0,2},{1,3},{2,0},{3,1},{4,6},{5,7},{6,4},{7,5},{8,10},{9,11},{10,... | collective-permute-start | bytes 1474568 | tf_op jit(solution)/shard_map/ppermute | solution.py:91
  188.3 72.3 %collective-permute-start.4 = (bf16[128,1920]{1,0:T(8,128)(2,1)}, bf16[128,1920]{1,0:T(8,128)(2,1)}, u32[]{:S(2)}, u32[]{:S(2)}) collective-permute-start(bf16[128,1920]{1,0:T(8,128)(2,1)} %constant_dynamic-slice_fusion.8), channel_id=1, source_target_pairs={{0,2},{1,3},{2,0},{3,1},{4,6},{5,7},{6,4},{7,5},{8,10},{9,11},{10,... | collective-permute-start | bytes 1474568 | tf_op jit(solution)/shard_map/ppermute | solution.py:91
  190.9 71.1 %collective-permute-start.6 = (bf16[128,1920]{1,0:T(8,128)(2,1)}, bf16[128,1920]{1,0:T(8,128)(2,1)}, u32[]{:S(2)}, u32[]{:S(2)}) collective-permute-start(bf16[128,1920]{1,0:T(8,128)(2,1)} %constant_dynamic-slice_fusion.7), channel_id=1, source_target_pairs={{0,2},{1,3},{2,0},{3,1},{4,6},{5,7},{6,4},{7,5},{8,10},{9,11},{10,... | collective-permute-start | bytes 1474568 | tf_op jit(solution)/shard_map/ppermute | solution.py:91
  191.5 74.5 %collective-permute-start.8 = (bf16[128,1920]{1,0:T(8,128)(2,1)}, bf16[128,1920]{1,0:T(8,128)(2,1)}, u32[]{:S(2)}, u32[]{:S(2)}) collective-permute-start(bf16[128,1920]{1,0:T(8,128)(2,1)} %constant_dynamic-slice_fusion.6), channel_id=1, source_target_pairs={{0,2},{1,3},{2,0},{3,1},{4,6},{5,7},{6,4},{7,5},{8,10},{9,11},{10,... | collective-permute-start | bytes 1474568 | tf_op jit(solution)/shard_map/ppermute | solution.py:91
  194.1 38.0 %collective-permute-start.16 = (bf16[32,2048]{1,0:T(8,128)(2,1)S(1)}, bf16[32,2048]{1,0:T(8,128)(2,1)S(1)}, u32[]{:S(2)}, u32[]{:S(2)}) collective-permute-start(bf16[32,2048]{1,0:T(8,128)(2,1)S(1)} %add_convert_fusion.4), channel_id=1, source_target_pairs={{0,2},{1,3},{2,0},{3,1},{4,6},{5,7},{6,4},{7,5},{8,10},{9,11},{10,... | collective-permute-start | bytes 393224 | tf_op jit(solution)/shard_map/ppermute | solution.py:91
  232.2 6.7 %collective-permute-start.17 = (bf16[32,2048]{1,0:T(8,128)(2,1)S(1)}, bf16[32,2048]{1,0:T(8,128)(2,1)S(1)}, u32[]{:S(2)}, u32[]{:S(2)}) collective-permute-start(bf16[32,2048]{1,0:T(8,128)(2,1)S(1)} %get-tuple-element.35), channel_id=1, source_target_pairs={{0,8},{1,9},{2,10},{3,11},{4,12},{5,13},{6,14},{7,15},{8,0},{9,1},... | collective-permute-start | bytes 393224 | tf_op jit(solution)/shard_map/ppermute | solution.py:91
  238.9 6.4 %collective-permute-start.18 = (bf16[32,2048]{1,0:T(8,128)(2,1)S(1)}, bf16[32,2048]{1,0:T(8,128)(2,1)S(1)}, u32[]{:S(2)}, u32[]{:S(2)}) collective-permute-start(bf16[32,2048]{1,0:T(8,128)(2,1)S(1)} %get-tuple-element.35), channel_id=1, source_target_pairs={{0,4},{1,5},{2,6},{3,7},{4,8},{5,9},{6,10},{7,11},{8,12},{9,13},{1... | collective-permute-start | bytes 393224 | tf_op jit(solution)/shard_map/ppermute | solution.py:91
  245.3 5.1 %collective-permute-start.19 = (bf16[32,2048]{1,0:T(8,128)(2,1)S(1)}, bf16[32,2048]{1,0:T(8,128)(2,1)S(1)}, u32[]{:S(2)}, u32[]{:S(2)}) collective-permute-start(bf16[32,2048]{1,0:T(8,128)(2,1)S(1)} %get-tuple-element.35), channel_id=1, source_target_pairs={{0,12},{1,13},{2,14},{3,15},{4,0},{5,1},{6,2},{7,3},{8,4},{9,5},{1... | collective-permute-start | bytes 393224 | tf_op jit(solution)/shard_map/ppermute | solution.py:91
  255.5 27.8 %collective-permute-start.3 = (bf16[128,1920]{1,0:T(8,128)(2,1)S(1)}, bf16[128,1920]{1,0:T(8,128)(2,1)S(1)}, u32[]{:S(2)}, u32[]{:S(2)}) collective-permute-start(bf16[128,1920]{1,0:T(8,128)(2,1)S(1)} %add_convert_fusion.2), channel_id=1, source_target_pairs={{0,8},{1,9},{2,10},{3,11},{4,12},{5,13},{6,14},{7,15},{8,0},{9,1},... | collective-permute-start | bytes 1474568 | tf_op jit(solution)/shard_map/ppermute | solution.py:91
  261.9 33.0 %collective-permute-start.5 = (bf16[128,1920]{1,0:T(8,128)(2,1)S(1)}, bf16[128,1920]{1,0:T(8,128)(2,1)S(1)}, u32[]{:S(2)}, u32[]{:S(2)}) collective-permute-start(bf16[128,1920]{1,0:T(8,128)(2,1)S(1)} %add_convert_fusion.1), channel_id=1, source_target_pairs={{0,4},{1,5},{2,6},{3,7},{4,8},{5,9},{6,10},{7,11},{8,12},{9,13},{1... | collective-permute-start | bytes 1474568 | tf_op jit(solution)/shard_map/ppermute | solution.py:91
  263.3 31.6 %collective-permute-start.7 = (bf16[128,1920]{1,0:T(8,128)(2,1)S(1)}, bf16[128,1920]{1,0:T(8,128)(2,1)S(1)}, u32[]{:S(2)}, u32[]{:S(2)}) collective-permute-start(bf16[128,1920]{1,0:T(8,128)(2,1)S(1)} %add_convert_fusion), channel_id=1, source_target_pairs={{0,12},{1,13},{2,14},{3,15},{4,0},{5,1},{6,2},{7,3},{8,4},{9,5},{1... | collective-permute-start | bytes 1474568 | tf_op jit(solution)/shard_map/ppermute | solution.py:91
  265.9 33.0 %collective-permute-start.24 = (f32[128,2048]{0,1:T(8,128)S(1)}, f32[128,2048]{0,1:T(8,128)S(1)}, u32[]{:S(2)}, u32[]{:S(2)}) collective-permute-start(f32[128,2048]{0,1:T(8,128)S(1)} %fusion.12), channel_id=1, source_target_pairs={{0,1},{1,0},{2,3},{3,2},{4,5},{5,4},{6,7},{7,6},{8,9},{9,8},{10,11... | collective-permute-start | bytes 3145736 | tf_op jit(solution)/shard_map/ppermute | solution.py:91
  (31 other events, 535.3 us)
Sparse Core Ops, SparseCore 0:
  24.9 50.9 all-gather.2

commit v2 on v1

--- a/solution.py
+++ b/solution.py
@@ -1,8 +1,11 @@
+import functools
 import math
 
 import jax
 import jax.numpy as jnp
 from jax import lax
+from jax.experimental import pallas as pl
+from jax.experimental.pallas import tpu as pltpu
 from jax.sharding import PartitionSpec as P
 
 PB = 256
@@ -81,6 +84,11 @@
 
 CORE = [(i, i ^ 1) for i in range(16)]
 ROW = [(i, i ^ 2) for i in range(16)]
+NEAR = [(i, i ^ 4) for i in range(16)]
+FAR = [(i, i ^ 8) for i in range(16)]
+LANES = 128
+TILE = 256
+VMEM_BYTES = 56 * 2**20
 
 
 def rotate(step):
@@ -101,13 +109,199 @@
     )
 
 
-def gram(a, b):
-    return lax.dot_general(a, b, (((0,), (0,)), ((), ())), preferred_element_type=jnp.float32)
+def dot_nt(a, b):
+    return lax.dot_general(a, b, (((1,), (1,)), ((), ())), preferred_element_type=jnp.float32)
+
+
+def dot_nn(a, b):
+    return lax.dot_general(a, b, (((1,), (0,)), ((), ())), preferred_element_type=jnp.float32)
 
 
 def gather_chips(x):
     pair = jnp.concatenate([x, send(x, ROW)], axis=0)
     return jnp.concatenate([pair] + [send(pair, rotate(s)) for s in (1, 2, 3)], axis=0)
+
+
+def vmem(count):
+    return [pl.BlockSpec(memory_space=pltpu.VMEM)] * count
+
+
+def spread(row_vector):
+    return jnp.broadcast_to(row_vector, (LANES, LANES)).T
+
+
+def stage_body(
+    core_ref, land_ref, fps_ref, norms_ref, tgs_ref,
+    ct_ref, mean_ref, rhs_ref, rest_ref, lead_ref, column_ref, weight_ref,
+    cent_ref, first_ref,
+):
+    step = pl.program_id(0)
+    rows = fps_ref.shape[0]
+    base = pl.multiple_of(step * TILE, TILE)
+    block = pl.multiple_of(core_ref[0] * LANES, LANES)
+    tile = land_ref[...]
+    wide = tile.astype(jnp.float32)
+    land_norms = jnp.sum(wide * wide, axis=1, keepdims=True)
+    inner = dot_nt(tile, fps_ref[...])
+    kernel = inner / (norms_ref[...] + land_norms - inner)
+    mean = jnp.sum(kernel, axis=1, keepdims=True) * (1.0 / rows)
+    cent = kernel - mean
+    cent_ref[...] = cent
+    ct_ref[pl.ds(base, TILE), :] = cent.astype(jnp.bfloat16)
+    mean_ref[:, pl.ds(base, TILE)] = jnp.broadcast_to(mean, (TILE, LANES)).T[:1, :]
+    own = cent_ref[pl.ds(block, LANES), :]
+    high = own.astype(jnp.bfloat16)
+    low = (own - high.astype(jnp.float32)).astype(jnp.bfloat16)
+    rhs_ref[step] = dot_nn(high, tgs_ref[...]) + dot_nn(low, tgs_ref[...])
+    first_ref[:, pl.ds(base, TILE)] = dot_nt(
+        ct_ref[pl.ds(block, LANES), :], ct_ref[pl.ds(base, TILE), :]
+    )
+
+    @pl.when(step == pl.num_programs(0) - 1)
+    def _():
+        lead = jnp.sum(first_ref[...], axis=0, keepdims=True)
+        lead_ref[...] = lead
+        lead_own = lead_ref[:, pl.ds(block, LANES)]
+        mass = jnp.sum(lead_own, axis=1, keepdims=True)
+        size = jnp.sum(jnp.abs(lead_own), axis=1, keepdims=True)
+        usable = mass > 1e-3 * size
+        weight = jnp.where(usable, 1.0 / jnp.where(usable, mass, 1.0), 0.0)
+        weight_ref[...] = jnp.broadcast_to(weight, (1, LANES))
+        mine = spread(lead_own) * weight
+        for j in range(lead.shape[1] // LANES):
+            cols = slice(j * LANES, (j + 1) * LANES)
+            part = lead[:, cols]
+            column_ref[cols, :] = spread(part) * weight
+            rest_ref[:, cols] = (first_ref[:, cols] - mine * part).astype(jnp.bfloat16)
+
+
+def stage(core, landmark_fps, fps, norms, tgs):
+    rows, length = fps.shape
+    landmarks = landmark_fps.shape[0]
+    steps = landmarks // TILE
+    f32 = jnp.float32
+
+    def whole(shape):
+        return pl.BlockSpec(shape, lambda i, c: (0,) * len(shape))
+
+    outs = [
+        ((landmarks, rows), jnp.bfloat16),
+        ((1, landmarks), f32),
+        ((steps, LANES, LANES), f32),
+        ((LANES, landmarks), jnp.bfloat16),
+        ((1, landmarks), f32),
+        ((landmarks, LANES), f32),
+        ((1, LANES), f32),
+    ]
+    return pl.pallas_call(
+        stage_body,
+        grid_spec=pltpu.PrefetchScalarGridSpec(
+            num_scalar_prefetch=1,
+            grid=(steps,),
+            in_specs=[
+                pl.BlockSpec((TILE, length), lambda i, c: (i, 0)),
+                whole(fps.shape),
+                whole(norms.shape),
+                whole(tgs.shape),
+            ],
+            out_specs=[whole(s) for s, _ in outs],
+            scratch_shapes=[
+                pltpu.VMEM((TILE, rows), f32),
+                pltpu.VMEM((LANES, landmarks), f32),
+            ],
+        ),
+        out_shape=[jax.ShapeDtypeStruct(s, d) for s, d in outs],
+        compiler_params=pltpu.CompilerParams(vmem_limit_bytes=VMEM_BYTES),
+        name="stage",
+    )(core, landmark_fps, fps, norms, tgs)
+
+
+def pieces_body(at_ref, ct_ref, lead_ref, column_ref, rhs_ref, *refs):
+    outs, left_ref = refs[:-1], refs[-1]
+    count = len(outs)
+    for p in range(count):
+        at = pl.multiple_of(at_ref[p], LANES)
+        left_ref[p * LANES : (p + 1) * LANES, :] = ct_ref[pl.ds(at, LANES), :]
+    for t in range(1, ct_ref.shape[0] // TILE):
+        got = dot_nt(left_ref[...], ct_ref[t * TILE : (t + 1) * TILE, :])
+        for p, out in enumerate(outs):
+            at = pl.multiple_of(at_ref[p], LANES)
+            column = column_ref[pl.ds(at, LANES), :]
+            for h in range(TILE // LANES):
+                lo = t * TILE + h * LANES
+                part = got[p * LANES : (p + 1) * LANES, h * LANES : (h + 1) * LANES]
+                part = part - column * lead_ref[:, lo : lo + LANES]
+                out[:, lo - TILE : lo - TILE + LANES] = part.astype(out.dtype)
+    for p, out in enumerate(outs):
+        out[:, ct_ref.shape[0] - TILE :] = rhs_ref[at_ref[p] // TILE].astype(out.dtype)
+
+
+def pieces(starts, ct, lead, column, rhs_part):
+    width = ct.shape[0] - TILE + LANES
+    outs = [jnp.float32, jnp.bfloat16] * (len(starts) // 2)
+    return pl.pallas_call(
+        pieces_body,
+        in_specs=[pl.BlockSpec(memory_space=pltpu.SMEM)] + vmem(4),
+        out_specs=vmem(len(outs)),
+        out_shape=[jax.ShapeDtypeStruct((LANES, width), d) for d in outs],
+        scratch_shapes=[pltpu.VMEM((len(outs) * LANES, ct.shape[1]), jnp.bfloat16)],
+        compiler_params=pltpu.CompilerParams(vmem_limit_bytes=VMEM_BYTES),
+        name="pieces",
+    )(jnp.stack(starts).astype(jnp.int32), ct, lead, column, rhs_part)
+
+
+CHOL = 32
+
+
+def exact_dot(a, b, dims=((1,), (0,))):
+    return lax.dot_general(
+        a, b, (dims, ((), ())), precision=lax.Precision.HIGHEST, preferred_element_type=jnp.float32
+    )
+
+
+def factor_body(blocks, state_ref, out_ref):
+    size = state_ref.shape[0]
+    out_ref[...] = state_ref[...]
+    sub = lax.broadcasted_iota(jnp.int32, (CHOL, LANES), 0)
+    lane = lax.broadcasted_iota(jnp.int32, (CHOL, LANES), 1)
+    for b in blocks:
+        lo, hi = b * CHOL, (b + 1) * CHOL
+        diag = out_ref[lo:hi, lo:hi]
+        work = jnp.concatenate(
+            [
+                diag,
+                (sub == lane)[:, :CHOL].astype(jnp.float32),
+                jnp.zeros((CHOL, LANES - 2 * CHOL), jnp.float32),
+            ],
+            axis=1,
+        )
+
+        def eliminate(k, x):
+            col = jnp.sum(jnp.where(lane == k, x, 0.0), axis=1, keepdims=True)
+            row = jnp.sum(jnp.where(sub == k, x, 0.0), axis=0, keepdims=True)
+            pivot = jnp.sum(jnp.where(lane[:1] == k, row, 0.0), axis=1, keepdims=True)
+            return x - jnp.where(sub > k, col, 0.0) * (row / pivot)
+
+        work = lax.fori_loop(0, CHOL, eliminate, work)
+        pivots = jnp.sum(jnp.where(sub == lane, work, 0.0), axis=1, keepdims=True)
+        inverse = work[:, CHOL : 2 * CHOL] / jnp.sqrt(pivots)
+        done = exact_dot(inverse, out_ref[lo:hi, :])
+        out_ref[lo:hi, :] = done
+        if hi < size:
+            out_ref[hi:, :] = out_ref[hi:, :] - exact_dot(
+                done[:, hi:size], done, ((0,), (0,))
+            )
+
+
+def eliminate_blocks(state, blocks):
+    return pl.pallas_call(
+        functools.partial(factor_body, blocks),
+        in_specs=vmem(1),
+        out_specs=vmem(1)[0],
+        out_shape=jax.ShapeDtypeStruct(state.shape, jnp.float32),
+        compiler_params=pltpu.CompilerParams(vmem_limit_bytes=VMEM_BYTES),
+        name="factor",
+    )(state)
 
 
 def landmarks_everywhere(fingerprints, landmark_index):
@@ -151,40 +345,22 @@
     chip_rows = 2 * rows_dev
     landmark_fps = landmarks_everywhere(fingerprints, landmark_index)
     norms = sq_norms(landmark_fps)
-    kernel = tanimoto(fps, landmark_fps, norms)
-    mean = jnp.sum(kernel, axis=0) / chip_rows
-    centred = (kernel - mean[None, :]).astype(jnp.bfloat16)
-    target_sum = jnp.sum(tgs.astype(jnp.float32), axis=0)
-    own_cols = lax.dynamic_slice_in_dim(
-        centred.reshape(chip_rows, 8, 2, share), core, 1, axis=2
-    ).reshape(chip_rows, 8 * share)
-
-    first = gram(own_cols[:, :share], centred)
-    lead = jnp.sum(first, axis=0)
-    lead_own = lax.dynamic_slice_in_dim(lead, core * share, share, 0)
-    lead_mass = jnp.sum(lead_own)
-    usable = lead_mass > 1e-3 * jnp.sum(jnp.abs(lead_own))
-    lead_weight = jnp.where(usable, 1.0 / jnp.where(usable, lead_mass, 1.0), 0.0)
-    lead = lax.reduce_precision(lead, 8, 7).astype(jnp.bfloat16)
-
-    def lead_outer(start, right):
-        left = lax.dynamic_slice_in_dim(lead, start, share, 0)
-        return lead_weight * gram(left[None, :], right[None, :])
-
-    chip_stats = gather_chips(jnp.concatenate([mean, target_sum])[None, :])
-    means, target_sums = chip_stats[:, :landmarks], chip_stats[:, landmarks:]
-    leads = gather_chips(
-        jnp.concatenate([lead.astype(jnp.float32), jnp.broadcast_to(lead_weight, (128,))])[None, :]
-    )
-    leads, lead_weights = leads[:, :landmarks], leads[:, landmarks : landmarks + 1]
-    shift = means - jnp.mean(means, axis=0, keepdims=True)
-    left_terms = jnp.concatenate([shift * chip_rows, leads], axis=0)
-    right_terms = jnp.concatenate([shift, leads * lead_weights], axis=0)
-
-    def add_back(start):
-        return highest(lax.dynamic_slice_in_dim(left_terms, start, share, 1), right_terms)
-
-    first_rest = (first - lead_outer(core * share, lead)).astype(jnp.bfloat16)
+    target_sum = jnp.sum(tgs.astype(jnp.float32), axis=0, keepdims=True)
+    ct, mean, rhs_part, first_rest, lead, column, weight = stage(
+        jnp.reshape(core, (1,)), landmark_fps, fps, sq_norms(fps)[None, :], tgs
+    )
+
+    def reduced_pieces(masks):
+        starts = []
+        for m in masks:
+            there = ((layer ^ m) * 4 + core) * share
+            starts += [there + row * 2 * share, there + (1 - row) * 2 * share]
+        got = pieces(starts, ct, lead, column, rhs_part)
+        return [(got[2 * p], got[2 * p + 1]) for p in range(len(masks))]
+
+    def row_sum(pair):
+        return pair[0] + send(pair[1], ROW).astype(jnp.float32)
+
     quarter = share // 4
 
     def quarter_of(q):
@@ -196,41 +372,44 @@
     part = part.astype(jnp.bfloat16)
     part = part.astype(jnp.float32) + send(part, ROW).astype(jnp.float32)
     part = part.astype(jnp.bfloat16)
-    pieces = jnp.zeros((4,) + part.shape, jnp.bfloat16)
-    pieces = lax.dynamic_update_index_in_dim(pieces, part, layer, 0)
+    quarters = jnp.zeros((4,) + part.shape, jnp.bfloat16)
+    quarters = lax.dynamic_update_index_in_dim(quarters, part, layer, 0)
     for s in (2, 1, 3):
-        pieces = lax.dynamic_update_index_in_dim(
-            pieces, send(part, rotate(s)), (layer + 4 - s) % 4, 0
+        quarters = lax.dynamic_update_index_in_dim(
+            quarters, send(part, rotate(s)), (layer + 4 - s) % 4, 0
         )
+
+    three, two = reduced_pieces((3, 2))
+    one, zero = reduced_pieces((1, 0))
+    three = row_sum(three).astype(jnp.bfloat16)
+    two = row_sum(two) + send(three, NEAR).astype(jnp.float32)
+    two = two.astype(jnp.bfloat16)
+    one = row_sum(one).astype(jnp.bfloat16)
+    own = row_sum(zero) + send(one, NEAR).astype(jnp.float32) + send(two, FAR).astype(jnp.float32)
+
+    stats = gather_chips(jnp.concatenate([mean, target_sum, lead, weight], axis=1))
+    means, target_sums = stats[:, :landmarks], stats[:, landmarks : landmarks + LANES]
+    leads = stats[:, landmarks + LANES : 2 * landmarks + LANES]
+    lead_weights = stats[:, 2 * landmarks + LANES : 2 * landmarks + LANES + 1]
+    shift = means - jnp.mean(means, axis=0, keepdims=True)
+    left_terms = jnp.concatenate([shift * chip_rows, leads], axis=0)
+    right_terms = jnp.concatenate([shift, leads * lead_weights], axis=0)
+
+    def add_back(start):
+        return highest(lax.dynamic_slice_in_dim(left_terms, start, share, 1), right_terms)
+
     block_fps = lax.dynamic_slice_in_dim(landmark_fps, core * share, share, 0)
-    block = (pieces.reshape(share, landmarks).astype(jnp.float32) + add_back(core * share)) * scale
+    block = (quarters.reshape(share, landmarks).astype(jnp.float32) + add_back(core * share)) * scale
     block = block + tanimoto(block_fps, landmark_fps, norms)
     other = send(block, CORE)
     panel_rows = lax.dynamic_slice_in_dim(
         jnp.concatenate([block, other, block], axis=0), core * share, 2 * share, 0
     )
-    corner = jnp.linalg.cholesky(panel_rows[:, :width])
-    factor = lax.linalg.triangular_solve(corner, panel_rows, left_side=True, lower=True)
-
-    right = jnp.concatenate([centred[:, width:], tgs], axis=1)
-    lead_right = jnp.concatenate([lead[width:], jnp.zeros((tgs.shape[1],), jnp.bfloat16)])
-
-    def row_sum(s):
-        there = (layer + s) % 4
-        left = lax.dynamic_slice_in_dim(own_cols, there * 2 * share, 2 * share, 1)
-        start = (there * 4 + core) * share
-        outer = jnp.concatenate(
-            [lead_outer(start, lead_right), lead_outer(start + 2 * share, lead_right)], axis=0
-        )
-        out = (gram(left, right) - outer).astype(jnp.bfloat16)
-        mine = lax.dynamic_slice_in_dim(out, row * share, share, 0)
-        theirs = lax.dynamic_slice_in_dim(out, (1 - row) * share, share, 0)
-        return mine.astype(jnp.float32) + send(theirs, ROW).astype(jnp.float32)
-
-    own = 0.0
-    for s in (2, 1, 3):
-        own = own + send(row_sum(s).astype(jnp.bfloat16), rotate(s)).astype(jnp.float32)
-    own = own + row_sum(0)
+    state = jnp.concatenate([panel_rows[:, :width], jnp.eye(width, dtype=jnp.float32)], axis=1)
+    for b in range(0, width // CHOL, 2):
+        state = eliminate_blocks(state, (b, b + 1))
+    factor = exact_dot(state[:, width:], panel_rows)
+
     start = position * share
     own_fps = lax.dynamic_slice_in_dim(landmark_fps, start, share, 0)
     rest = (own[:, : landmarks - width] + add_back(start)[:, width:]) * scale + tanimoto(

time: 389 us -> 293 us (0.75)
  the two profiles are of different devices: /device:TPU:18 before, /device:TPU:0 now
where the time goes in v2:
time: 293 us
  waiting for transfers between devices  117 us (40%)
  Pallas kernels  82.3 us (28%)
  local copies, waits for them, and re-layouts  29.6 us (10%)
  starting transfers between devices  20.2 us (7%)
  other arithmetic  17.2 us (6%)
  between operations  14.6 us (5%)
  matrix products  11.9 us (4%)
    ppermute x21, waiting for transfers between devices, send(): return lax.ppermute(x, 'dp', perm)  69.5 us
    all_gather x1, waiting for transfers between devices, landmarks_everywhere(): gathered = lax.all_gather(packed, 'dp', axis=0, tiled=True)  47.4 us
    pallas_call x4, Pallas kernels, eliminate_blocks(): pl.pallas_call(functools.partial(factor_body, blocks), in_specs=vmem(1),...  38.9 us
    pallas_call x1, Pallas kernels, stage(): pl.pallas_call(stage_body, grid_spec=pltpu.PrefetchScalarGridSpec(num_sca...  24.6 us
    ppermute x21, starting transfers between devices, send(): return lax.ppermute(x, 'dp', perm)  20.2 us
    pallas_call x2, Pallas kernels, pieces(): pl.pallas_call(pieces_body, in_specs=[pl.BlockSpec(memory_space=pltpu.SME...  18.8 us
    gather x1, local copies, waits for them, and re-layouts, landmarks_everywhere(): return gathered[owner_dev * capacity + owner_rank]  10.3 us
    scatter x1, local copies, waits for them, and re-layouts, landmarks_everywhere(): slot_rows = jnp.zeros((capacity,), jnp.int32).at[jnp.where(is_mine, owner...  8.04 us
  transfers between devices with their start and end apart: 22, of which 11 were waited for; matrix products, arithmetic and copies ran while one was open for 7% of the time, Pallas kernels for 16%

profile of v2, /device:TPU:0, one launch (start us, length us, event | category | flops | bytes accessed | tf_op | source)
XLA Modules:
  0.0 292.6 jit_solution(4640303934861231110)
XLA Ops:
  8.1 4.5 %reduce-window.6 = s32[16,16,128]{2,1,0:T(8,128)S(1)} reduce-window(s32[16,16,128]{2,1,0:T(8,128)S(1)} %fusion.22, s32[]{:T(128)} %constant.147.clone.1), window={size=1x1x128 pad=0_0x0_0x127_0}, to_apply=%region_0.1 | reduce-window | flops 4161536 | bytes 262148 | tf_op jit(solution)/shard_map/reduce-window
  13.4 8.0 %scatter_custom_fusion = s32[256]{0:T(256)S(1)} fusion(s32[2048]{0:T(1024)S(1)} %get-tuple-element.53, s32[2048]{0:T(1024)S(1)} %get-tuple-element.54, s32[]{:T(128)} %constant.147.clone.1), kind=kCustom, calls=%fused_computation.106 | custom fusion | bytes 1028 | tf_op jit(solution)/shard_map/scatter | solution.py:324
  29.4 47.4 %all-gather.3.cloned.1.call-done = bf16[4096,512]{1,0:T(8,128)(2,1)} async-done(((bf16[256,512]{1,0:T(8,128)(2,1)}), bf16[4096,512]{1,0:T(8,128)(2,1)}) %all-gather.3.cloned.1.call-update) | async-done | bytes 4194320 | tf_op jit(solution)/shard_map/all_gather | solution.py:327
  76.8 10.3 %gather_fusion.1 = bf16[2048,512]{1,0:T(8,128)(2,1)S(1)} fusion(bf16[4096,512]{1,0:T(8,128)(2,1)} %all-gather.3.cloned.1.call-done, s32[2048]{0:T(1024)S(1)} %get-tuple-element.52), kind=kCustom, calls=%fused_computation.1 | custom fusion | bytes 4202496 | tf_op jit(solution)/shard_map/gather | solution.py:328
  88.5 24.6 %stage.1 = (bf16[2048,2048]{1,0:T(8,128)(2,1)}, f32[1,2048]{1,0:T(1,128)}, f32[8,128,128]{2,1,0:T(8,128)}, bf16[128,2048]{1,0:T(8,128)(2,1)}, f32[1,2048]{1,0:T(...) custom-call(s32[1]{0:T(128)} %bitcast.4.core_ref, bf16[2048,512]{1,0:T(8,128)(2,1)} %copy-done, ...), custom_call_target="tpu_custom_call" | custom-call | tf_op jit(solution)/shard_map/stage/pallas_call | solution.py:196
  113.1 9.5 %pieces.3 = (f32[128,1920]{1,0:T(8,128)}, bf16[128,1920]{1,0:T(8,128)(2,1)}, f32[128,1920]{1,0:T(8,128)}, bf16[128,1920]{1,0:T(8,128)(2,1)}) custom-call(s32[4]{0:T(128)} %get-tuple-element.57.at_ref, bf16[2048,2048]{1,0:T(8,128)(2,1)} %get-tuple-element.18.ct_ref, f32[1,2048]{1,0:T(1,128)} %get-tuple-element.19.lead_ref, ...), custom_call_target="tpu_custom_call" | custom-call | tf_op jit(solution)/shard_map/pieces/pallas_call | solution.py:242
  127.1 20.0 %collective-permute-done.9 = f32[1,4352]{1,0:T(1,128)S(1)} collective-permute-done((f32[1,4352]{1,0:T(1,128)S(1)}, f32[1,4352]{1,0:T(1,128)S(1)}, u32[]{:S(2)}, u32[]{:S(2)}) %collective-permute-start.9) | collective-permute-done | bytes 17440 | tf_op jit(solution)/shard_map/ppermute | solution.py:99
  149.6 2.3 collective-permute-start.12
  151.9 9.3 %pieces.2 = (f32[128,1920]{1,0:T(8,128)}, bf16[128,1920]{1,0:T(8,128)(2,1)}, f32[128,1920]{1,0:T(8,128)}, bf16[128,1920]{1,0:T(8,128)(2,1)}) custom-call(s32[4]{0:T(128)} %get-tuple-element.56.at_ref, bf16[2048,2048]{1,0:T(8,128)(2,1)} %get-tuple-element.18.ct_ref, f32[1,2048]{1,0:T(1,128)} %get-tuple-element.19.lead_ref, ...), custom_call_target="tpu_custom_call" | custom-call | tf_op jit(solution)/shard_map/pieces/pallas_call | solution.py:242
  167.3 3.6 %collective-permute-done.15 = bf16[32,2048]{1,0:T(8,128)(2,1)} collective-permute-done((bf16[32,2048]{1,0:T(8,128)(2,1)S(1)}, bf16[32,2048]{1,0:T(8,128)(2,1)}, u32[]{:S(2)}, u32[]{:S(2)}) %collective-permute-start.15) | collective-permute-done | bytes 131104 | tf_op jit(solution)/shard_map/ppermute | solution.py:99
  173.0 2.1 collective-permute-done.13
  176.9 15.0 %collective-permute-done.16 = bf16[32,2048]{1,0:T(8,128)(2,1)S(1)} collective-permute-done((bf16[32,2048]{1,0:T(8,128)(2,1)S(1)}, bf16[32,2048]{1,0:T(8,128)(2,1)S(1)}, u32[]{:S(2)}, u32[]{:S(2)}) %collective-permute-start.16) | collective-permute-done | bytes 131104 | tf_op jit(solution)/shard_map/ppermute | solution.py:99
  195.8 5.0 %collective-permute-done.17 = bf16[32,2048]{1,0:T(8,128)(2,1)S(1)} collective-permute-done((bf16[32,2048]{1,0:T(8,128)(2,1)S(1)}, bf16[32,2048]{1,0:T(8,128)(2,1)S(1)}, u32[]{:S(2)}, u32[]{:S(2)}) %collective-permute-start.17) | collective-permute-done | bytes 131104 | tf_op jit(solution)/shard_map/ppermute | solution.py:99
  201.3 6.3 %collective-permute-done.18 = bf16[32,2048]{1,0:T(8,128)(2,1)S(1)} collective-permute-done((bf16[32,2048]{1,0:T(8,128)(2,1)S(1)}, bf16[32,2048]{1,0:T(8,128)(2,1)S(1)}, u32[]{:S(2)}, u32[]{:S(2)}) %collective-permute-start.18) | collective-permute-done | bytes 131104 | tf_op jit(solution)/shard_map/ppermute | solution.py:99
  208.6 3.9 %collective-permute-done.19 = bf16[32,2048]{1,0:T(8,128)(2,1)S(1)} collective-permute-done((bf16[32,2048]{1,0:T(8,128)(2,1)S(1)}, bf16[32,2048]{1,0:T(8,128)(2,1)S(1)}, u32[]{:S(2)}, u32[]{:S(2)}) %collective-permute-start.19) | collective-permute-done | bytes 131104 | tf_op jit(solution)/shard_map/ppermute | solution.py:99
  216.2 2.0 collective-permute-start.4
  218.2 11.1 %collective-permute-done.7 = bf16[128,1920]{1,0:T(8,128)(2,1)S(1)} collective-permute-done((bf16[128,1920]{1,0:T(8,128)(2,1)S(1)}, bf16[128,1920]{1,0:T(8,128)(2,1)S(1)}, u32[]{:S(2)}, u32[]{:S(2)}) %collective-permute-start.7) | collective-permute-done | bytes 491552 | tf_op jit(solution)/shard_map/ppermute | solution.py:99
  229.3 2.0 add_convert_fusion
  234.1 10.3 %factor.4.state_ref = f32[256,512]{1,0:T(8,128)} custom-call(f32[256,512]{1,0:T(8,128)} %pad_maximum_fusion.1.state_ref), custom_call_target="tpu_custom_call" | custom-call | tf_op jit(solution)/shard_map/factor/pallas_call | solution.py:297
  244.4 9.8 %factor.5.state_ref = f32[256,512]{1,0:T(8,128)} custom-call(f32[256,512]{1,0:T(8,128)} %factor.4.state_ref), custom_call_target="tpu_custom_call" | custom-call | tf_op jit(solution)/shard_map/factor/pallas_call | solution.py:297
  254.2 9.6 %factor.6.state_ref = f32[256,512]{1,0:T(8,128)} custom-call(f32[256,512]{1,0:T(8,128)} %factor.5.state_ref), custom_call_target="tpu_custom_call" | custom-call | tf_op jit(solution)/shard_map/factor/pallas_call | solution.py:297
  263.8 9.2 %factor.7 = f32[256,512]{1,0:T(8,128)} custom-call(f32[256,512]{1,0:T(8,128)} %factor.6.state_ref), custom_call_target="tpu_custom_call" | custom-call | tf_op jit(solution)/shard_map/factor/pallas_call | solution.py:297
  273.0 2.9 %fusion = f32[256,2048]{1,0:T(8,128)S(1)} fusion(f32[384,2048]{1,0:T(8,128)S(1)} %pad_maximum_fusion, s32[]{:T(128)S(6)} %select_n.131, f32[256,512]{1,0:T(8,128)} %factor.7), kind=kOutput, calls=%fused_computation.7 | convolution fusion | flops 1610612736 | bytes 4456452 | tf_op jit(solution)/shard_map/dot_general | solution.py:257
  283.5 2.2 convolution_subtract_fusion
  (134 shorter events, 46.9 us)
Async XLA Ops:
  7.2 69.6 %all-gather.3.cloned.1.call-start = ((), (), s32[]{:S(2)}) async-start(), calls=%async_computation | async-start | bytes 4456448 | tf_op jit(solution)/shard_map/all_gather | solution.py:327
  23.4 3.5 %collective-permute-start = (bf16[1024,512]{1,0:T(8,128)(2,1)S(1)}, bf16[1024,512]{1,0:T(8,128)(2,1)S(1)}, u32[]{:S(2)}, u32[]{:S(2)}) collective-permute-start(bf16[1024,512]{1,0:T(8,128)(2,1)S(1)} %copy-done.4), channel_id=1, source_target_pairs={{0,1},{1,0},{2,3},{3,2},{4,5},{5,4},{6,7},{7,6},{8,9},{9,8},{10,11... | collective-permute-start | bytes 3145736 | tf_op jit(solution)/shard_map/ppermute | solution.py:99
  23.9 2.7 collective-permute-start.1
  87.6 73.7 %copy-start.18 = (f32[2048]{0:T(1024)}, f32[2048]{0:T(1024)S(1)}, u32[]{:S(2)}) copy-start(f32[2048]{0:T(1024)S(1)} %multiply_reduce_fusion) | copy-start | bytes 24580
  122.6 91.4 %collective-permute-start.6 = (bf16[128,1920]{1,0:T(8,128)(2,1)}, bf16[128,1920]{1,0:T(8,128)(2,1)}, u32[]{:S(2)}, u32[]{:S(2)}) collective-permute-start(bf16[128,1920]{1,0:T(8,128)(2,1)} %get-tuple-element.29), channel_id=1, source_target_pairs={{0,2},{1,3},{2,0},{3,1},{4,6},{5,7},{6,4},{7,5},{8,10},{9,11},{10,... | collective-permute-start | bytes 1474568 | tf_op jit(solution)/shard_map/ppermute | solution.py:99
  123.2 95.0 %collective-permute-start.5 = (bf16[128,1920]{1,0:T(8,128)(2,1)}, bf16[128,1920]{1,0:T(8,128)(2,1)}, u32[]{:S(2)}, u32[]{:S(2)}) collective-permute-start(bf16[128,1920]{1,0:T(8,128)(2,1)} %get-tuple-element.27), channel_id=1, source_target_pairs={{0,2},{1,3},{2,0},{3,1},{4,6},{5,7},{6,4},{7,5},{8,10},{9,11},{10,... | collective-permute-start | bytes 1474568 | tf_op jit(solution)/shard_map/ppermute | solution.py:99
  124.7 22.4 %collective-permute-start.9 = (f32[1,4352]{1,0:T(1,128)S(1)}, f32[1,4352]{1,0:T(1,128)S(1)}, u32[]{:S(2)}, u32[]{:S(2)}) collective-permute-start(f32[1,4352]{1,0:T(1,128)S(1)} %pad_maximum_fusion.3), channel_id=1, source_target_pairs={{0,2},{1,3},{2,0},{3,1},{4,6},{5,7},{6,4},{7,5},{8,10},{9,11},{10,... | collective-permute-start | bytes 52232 | tf_op jit(solution)/shard_map/ppermute | solution.py:99
  147.1 15.4 %collective-permute-start.10 = (f32[2,4352]{1,0:T(2,128)S(1)}, f32[2,4352]{1,0:T(2,128)S(1)}, u32[]{:S(2)}, u32[]{:S(2)}) collective-permute-start(f32[2,4352]{1,0:T(2,128)S(1)} %pad_maximum_fusion.2), channel_id=1, source_target_pairs={{0,4},{1,5},{2,6},{3,7},{4,8},{5,9},{6,10},{7,11},{8,12},{9,13},{1... | collective-permute-start | bytes 104456 | tf_op jit(solution)/shard_map/ppermute | solution.py:99
  148.7 15.0 %collective-permute-start.11 = (f32[2,4352]{1,0:T(2,128)S(1)}, f32[2,4352]{1,0:T(2,128)S(1)}, u32[]{:S(2)}, u32[]{:S(2)}) collective-permute-start(f32[2,4352]{1,0:T(2,128)S(1)} %pad_maximum_fusion.2), channel_id=1, source_target_pairs={{0,8},{1,9},{2,10},{3,11},{4,12},{5,13},{6,14},{7,15},{8,0},{9,1},... | collective-permute-start | bytes 104456 | tf_op jit(solution)/shard_map/ppermute | solution.py:99
  149.6 14.9 %collective-permute-start.12 = (f32[2,4352]{1,0:T(2,128)S(1)}, f32[2,4352]{1,0:T(2,128)S(1)}, u32[]{:S(2)}, u32[]{:S(2)}) collective-permute-start(f32[2,4352]{1,0:T(2,128)S(1)} %pad_maximum_fusion.2), channel_id=1, source_target_pairs={{0,12},{1,13},{2,14},{3,15},{4,0},{5,1},{6,2},{7,3},{8,4},{9,5},{1... | collective-permute-start | bytes 104456 | tf_op jit(solution)/shard_map/ppermute | solution.py:99
  162.5 8.5 %collective-permute-start.15 = (bf16[32,2048]{1,0:T(8,128)(2,1)S(1)}, bf16[32,2048]{1,0:T(8,128)(2,1)}, u32[]{:S(2)}, u32[]{:S(2)}) collective-permute-start(bf16[32,2048]{1,0:T(8,128)(2,1)S(1)} %get-tuple-element.46), channel_id=1, source_target_pairs={{0,12},{1,13},{2,14},{3,15},{4,0},{5,1},{6,2},{7,3},{8,4},{9,5},{1... | collective-permute-start | bytes 393224 | tf_op jit(solution)/shard_map/ppermute | solution.py:99
  163.7 8.5 %collective-permute-start.14 = (bf16[32,2048]{1,0:T(8,128)(2,1)S(1)}, bf16[32,2048]{1,0:T(8,128)(2,1)}, u32[]{:S(2)}, u32[]{:S(2)}) collective-permute-start(bf16[32,2048]{1,0:T(8,128)(2,1)S(1)} %get-tuple-element.47), channel_id=1, source_target_pairs={{0,4},{1,5},{2,6},{3,7},{4,8},{5,9},{6,10},{7,11},{8,12},{9,13},{1... | collective-permute-start | bytes 393224 | tf_op jit(solution)/shard_map/ppermute | solution.py:99
  165.1 10.0 %collective-permute-start.13 = (bf16[32,2048]{1,0:T(8,128)(2,1)S(1)}, bf16[32,2048]{1,0:T(8,128)(2,1)}, u32[]{:S(2)}, u32[]{:S(2)}) collective-permute-start(bf16[32,2048]{1,0:T(8,128)(2,1)S(1)} %get-tuple-element.45), channel_id=1, source_target_pairs={{0,8},{1,9},{2,10},{3,11},{4,12},{5,13},{6,14},{7,15},{8,0},{9,1},... | collective-permute-start | bytes 393224 | tf_op jit(solution)/shard_map/ppermute | solution.py:99
  167.2 45.4 %copy-start.8 = (f32[128,2048]{1,0:T(8,128)S(1)}, f32[128,2048]{1,0:T(8,128)}, u32[]{:S(2)}) copy-start(f32[128,2048]{1,0:T(8,128)} %fusion.25) | copy-start | bytes 3145732
  171.0 44.3 %collective-permute-start.3 = (bf16[128,1920]{1,0:T(8,128)(2,1)}, bf16[128,1920]{1,0:T(8,128)(2,1)S(1)}, u32[]{:S(2)}, u32[]{:S(2)}) collective-permute-start(bf16[128,1920]{1,0:T(8,128)(2,1)} %get-tuple-element.25), channel_id=1, source_target_pairs={{0,2},{1,3},{2,0},{3,1},{4,6},{5,7},{6,4},{7,5},{8,10},{9,11},{10,... | collective-permute-start | bytes 1474568 | tf_op jit(solution)/shard_map/ppermute | solution.py:99
  172.2 107.1 %collective-permute-start.2 = (bf16[128,1920]{1,0:T(8,128)(2,1)}, bf16[128,1920]{1,0:T(8,128)(2,1)}, u32[]{:S(2)}, u32[]{:S(2)}) collective-permute-start(bf16[128,1920]{1,0:T(8,128)(2,1)} %get-tuple-element.23), channel_id=1, source_target_pairs={{0,2},{1,3},{2,0},{3,1},{4,6},{5,7},{6,4},{7,5},{8,10},{9,11},{10,... | collective-permute-start | bytes 1474568 | tf_op jit(solution)/shard_map/ppermute | solution.py:99
  176.2 15.7 %collective-permute-start.16 = (bf16[32,2048]{1,0:T(8,128)(2,1)S(1)}, bf16[32,2048]{1,0:T(8,128)(2,1)S(1)}, u32[]{:S(2)}, u32[]{:S(2)}) collective-permute-start(bf16[32,2048]{1,0:T(8,128)(2,1)S(1)} %add_convert_fusion.4), channel_id=1, source_target_pairs={{0,2},{1,3},{2,0},{3,1},{4,6},{5,7},{6,4},{7,5},{8,10},{9,11},{10,... | collective-permute-start | bytes 393224 | tf_op jit(solution)/shard_map/ppermute | solution.py:99
  192.0 8.7 %collective-permute-start.17 = (bf16[32,2048]{1,0:T(8,128)(2,1)S(1)}, bf16[32,2048]{1,0:T(8,128)(2,1)S(1)}, u32[]{:S(2)}, u32[]{:S(2)}) collective-permute-start(bf16[32,2048]{1,0:T(8,128)(2,1)S(1)} %get-tuple-element.44), channel_id=1, source_target_pairs={{0,8},{1,9},{2,10},{3,11},{4,12},{5,13},{6,14},{7,15},{8,0},{9,1},... | collective-permute-start | bytes 393224 | tf_op jit(solution)/shard_map/ppermute | solution.py:99
  200.8 6.8 %collective-permute-start.18 = (bf16[32,2048]{1,0:T(8,128)(2,1)S(1)}, bf16[32,2048]{1,0:T(8,128)(2,1)S(1)}, u32[]{:S(2)}, u32[]{:S(2)}) collective-permute-start(bf16[32,2048]{1,0:T(8,128)(2,1)S(1)} %get-tuple-element.44), channel_id=1, source_target_pairs={{0,4},{1,5},{2,6},{3,7},{4,8},{5,9},{6,10},{7,11},{8,12},{9,13},{1... | collective-permute-start | bytes 393224 | tf_op jit(solution)/shard_map/ppermute | solution.py:99
  207.6 5.0 %collective-permute-start.19 = (bf16[32,2048]{1,0:T(8,128)(2,1)S(1)}, bf16[32,2048]{1,0:T(8,128)(2,1)S(1)}, u32[]{:S(2)}, u32[]{:S(2)}) collective-permute-start(bf16[32,2048]{1,0:T(8,128)(2,1)S(1)} %get-tuple-element.44), channel_id=1, source_target_pairs={{0,12},{1,13},{2,14},{3,15},{4,0},{5,1},{6,2},{7,3},{8,4},{9,5},{1... | collective-permute-start | bytes 393224 | tf_op jit(solution)/shard_map/ppermute | solution.py:99
  213.9 18.9 %collective-permute-start.20 = (f32[128,2048]{1,0:T(8,128)S(1)}, f32[128,2048]{1,0:T(8,128)S(1)}, u32[]{:S(2)}, u32[]{:S(2)}) collective-permute-start(f32[128,2048]{1,0:T(8,128)S(1)} %fusion.6), channel_id=1, source_target_pairs={{0,1},{1,0},{2,3},{3,2},{4,5},{5,4},{6,7},{7,6},{8,9},{9,8},{10,11... | collective-permute-start | bytes 3145736 | tf_op jit(solution)/shard_map/ppermute | solution.py:99
  215.2 14.1 %collective-permute-start.7 = (bf16[128,1920]{1,0:T(8,128)(2,1)S(1)}, bf16[128,1920]{1,0:T(8,128)(2,1)S(1)}, u32[]{:S(2)}, u32[]{:S(2)}) collective-permute-start(bf16[128,1920]{1,0:T(8,128)(2,1)S(1)} %add_convert_fusion.1), channel_id=1, source_target_pairs={{0,4},{1,5},{2,6},{3,7},{4,0},{5,1},{6,2},{7,3},{8,12},{9,13},{10,... | collective-permute-start | bytes 1474568 | tf_op jit(solution)/shard_map/ppermute | solution.py:99
  216.2 63.2 %collective-permute-start.4 = (bf16[128,1920]{1,0:T(8,128)(2,1)}, bf16[128,1920]{1,0:T(8,128)(2,1)}, u32[]{:S(2)}, u32[]{:S(2)}) collective-permute-start(bf16[128,1920]{1,0:T(8,128)(2,1)} %add_convert_fusion.2), channel_id=1, source_target_pairs={{0,4},{1,5},{2,6},{3,7},{4,0},{5,1},{6,2},{7,3},{8,12},{9,13},{10,... | collective-permute-start | bytes 1474568 | tf_op jit(solution)/shard_map/ppermute | solution.py:99
  231.3 48.0 %collective-permute-start.8 = (bf16[128,1920]{1,0:T(8,128)(2,1)}, bf16[128,1920]{1,0:T(8,128)(2,1)}, u32[]{:S(2)}, u32[]{:S(2)}) collective-permute-start(bf16[128,1920]{1,0:T(8,128)(2,1)} %add_convert_fusion), channel_id=1, source_target_pairs={{0,8},{1,9},{2,10},{3,11},{4,12},{5,13},{6,14},{7,15},{8,0},{9,1},... | collective-permute-start | bytes 1474568 | tf_op jit(solution)/shard_map/ppermute | solution.py:99
  (23 other events, 280.5 us)
Sparse Core Ops, SparseCore 0:
  23.5 53.2 all-gather.2

commit v3 on v2

--- a/solution.py
+++ b/solution.py
@@ -142,12 +142,17 @@
     tile = land_ref[...]
     wide = tile.astype(jnp.float32)
     land_norms = jnp.sum(wide * wide, axis=1, keepdims=True)
-    inner = dot_nt(tile, fps_ref[...])
-    kernel = inner / (norms_ref[...] + land_norms - inner)
-    mean = jnp.sum(kernel, axis=1, keepdims=True) * (1.0 / rows)
-    cent = kernel - mean
-    cent_ref[...] = cent
-    ct_ref[pl.ds(base, TILE), :] = cent.astype(jnp.bfloat16)
+    total = jnp.zeros((TILE, 1), jnp.float32)
+    for n in range(0, rows, TILE):
+        inner = dot_nt(tile, fps_ref[n : n + TILE, :])
+        kernel = inner / (norms_ref[:, n : n + TILE] + land_norms - inner)
+        cent_ref[:, n : n + TILE] = kernel
+        total = total + jnp.sum(kernel, axis=1, keepdims=True)
+    mean = total * (1.0 / rows)
+    for n in range(0, rows, TILE):
+        cent = cent_ref[:, n : n + TILE] - mean
+        cent_ref[:, n : n + TILE] = cent
+        ct_ref[pl.ds(base, TILE), n : n + TILE] = cent.astype(jnp.bfloat16)
     mean_ref[:, pl.ds(base, TILE)] = jnp.broadcast_to(mean, (TILE, LANES)).T[:1, :]
     own = cent_ref[pl.ds(block, LANES), :]
     high = own.astype(jnp.bfloat16)
@@ -223,15 +228,19 @@
         at = pl.multiple_of(at_ref[p], LANES)
         left_ref[p * LANES : (p + 1) * LANES, :] = ct_ref[pl.ds(at, LANES), :]
     for t in range(1, ct_ref.shape[0] // TILE):
-        got = dot_nt(left_ref[...], ct_ref[t * TILE : (t + 1) * TILE, :])
-        for p, out in enumerate(outs):
-            at = pl.multiple_of(at_ref[p], LANES)
-            column = column_ref[pl.ds(at, LANES), :]
-            for h in range(TILE // LANES):
-                lo = t * TILE + h * LANES
-                part = got[p * LANES : (p + 1) * LANES, h * LANES : (h + 1) * LANES]
-                part = part - column * lead_ref[:, lo : lo + LANES]
-                out[:, lo - TILE : lo - TILE + LANES] = part.astype(out.dtype)
+        for q in range(0, count, 2):
+            got = dot_nt(
+                left_ref[q * LANES : (q + 2) * LANES, :], ct_ref[t * TILE : (t + 1) * TILE, :]
+            )
+            for p in (q, q + 1):
+                out = outs[p]
+                at = pl.multiple_of(at_ref[p], LANES)
+                column = column_ref[pl.ds(at, LANES), :]
+                for h in range(TILE // LANES):
+                    lo = t * TILE + h * LANES
+                    part = got[(p - q) * LANES : (p - q + 1) * LANES, h * LANES : (h + 1) * LANES]
+                    part = part - column * lead_ref[:, lo : lo + LANES]
+                    out[:, lo - TILE : lo - TILE + LANES] = part.astype(out.dtype)
     for p, out in enumerate(outs):
         out[:, ct_ref.shape[0] - TILE :] = rhs_ref[at_ref[p] // TILE].astype(out.dtype)
 
@@ -276,20 +285,19 @@
             axis=1,
         )
 
-        def eliminate(k, x):
-            col = jnp.sum(jnp.where(lane == k, x, 0.0), axis=1, keepdims=True)
-            row = jnp.sum(jnp.where(sub == k, x, 0.0), axis=0, keepdims=True)
-            pivot = jnp.sum(jnp.where(lane[:1] == k, row, 0.0), axis=1, keepdims=True)
-            return x - jnp.where(sub > k, col, 0.0) * (row / pivot)
-
-        work = lax.fori_loop(0, CHOL, eliminate, work)
+        for k in range(CHOL):
+            col = jnp.broadcast_to(work[:, k : k + 1], work.shape)
+            row = work[k : k + 1, :] / col[k : k + 1, :]
+            work = work - jnp.where(sub > k, col, 0.0) * row
         pivots = jnp.sum(jnp.where(sub == lane, work, 0.0), axis=1, keepdims=True)
         inverse = work[:, CHOL : 2 * CHOL] / jnp.sqrt(pivots)
         done = exact_dot(inverse, out_ref[lo:hi, :])
         out_ref[lo:hi, :] = done
         if hi < size:
-            out_ref[hi:, :] = out_ref[hi:, :] - exact_dot(
-                done[:, hi:size], done, ((0,), (0,))
+            left = hi // LANES * LANES
+            cols = slice(left, size + -(-hi // LANES) * LANES)
+            out_ref[hi:, cols] = out_ref[hi:, cols] - exact_dot(
+                done[:, hi:size], done[:, cols], ((0,), (0,))
             )
 
 
@@ -304,28 +312,117 @@
     )(state)
 
 
+def pack_body(at_ref, index_ref, fps_ref, packed_ref, slots_ref, key_ref, pick_ref):
+    rows, landmarks = fps_ref.shape[0], index_ref.shape[1]
+    capacity = packed_ref.shape[0]
+    f32 = jnp.float32
+    index = index_ref[...].astype(f32)
+    owner = jnp.floor(index * (1.0 / rows))
+    key_ref[1:2, :] = index - owner * rows
+    device = lax.broadcasted_iota(jnp.int32, (16, TILE), 0).astype(f32)
+    before = lax.broadcasted_iota(jnp.int32, (TILE, TILE), 0)
+    before = (before < lax.broadcasted_iota(jnp.int32, (TILE, TILE), 1)).astype(jnp.bfloat16)
+    owners = [owner[:, n : n + TILE] for n in range(0, landmarks, TILE)]
+    owned = [(device == o).astype(f32) for o in owners]
+    within = dot_nn(jnp.concatenate(owned, axis=0).astype(jnp.bfloat16), before)
+    ahead = jnp.zeros((16, 1), f32)
+    slot_in = lax.broadcasted_iota(jnp.int32, (capacity, TILE), 0).astype(f32)
+    for b, o in enumerate(owners):
+        counts = within[b * 16 : (b + 1) * 16, :] + ahead
+        rank = jnp.sum(owned[b] * counts, axis=0, keepdims=True)
+        ahead = ahead + jnp.sum(owned[b], axis=1, keepdims=True)
+        slot = o * capacity + rank
+        for h in range(0, TILE, LANES):
+            lo = b * TILE + h
+            slots_ref[lo : lo + LANES, :] = spread(slot[:, h : h + LANES])
+        key = jnp.where(o == at_ref[0].astype(f32), rank, -1.0)
+        pick_ref[:, b * TILE : (b + 1) * TILE] = (slot_in == key).astype(jnp.bfloat16)
+    packed = jnp.zeros(packed_ref.shape, f32)
+    for r in range(0, rows, TILE):
+        row_in = lax.broadcasted_iota(jnp.int32, (TILE, landmarks), 0).astype(f32) + r
+        here = (row_in == key_ref[1:2, :]).astype(jnp.bfloat16)
+        chosen = dot_nt(pick_ref[...], here).astype(jnp.bfloat16)
+        packed = packed + dot_nn(chosen, fps_ref[r : r + TILE, :])
+    packed_ref[...] = packed.astype(jnp.bfloat16)
+
+
+def pack(position, landmark_index, fingerprints):
+    landmarks = landmark_index.shape[0]
+    capacity = landmarks // 8
+    return pl.pallas_call(
+        pack_body,
+        in_specs=[pl.BlockSpec(memory_space=pltpu.SMEM)] + vmem(2),
+        out_specs=vmem(2),
+        out_shape=[
+            jax.ShapeDtypeStruct((capacity, fingerprints.shape[1]), jnp.bfloat16),
+            jax.ShapeDtypeStruct((landmarks, LANES), jnp.float32),
+        ],
+        scratch_shapes=[
+            pltpu.VMEM((8, landmarks), jnp.float32),
+            pltpu.VMEM((capacity, landmarks), jnp.bfloat16),
+        ],
+        compiler_params=pltpu.CompilerParams(vmem_limit_bytes=VMEM_BYTES),
+        name="pack",
+    )(jnp.reshape(position, (1,)), landmark_index[None, :], fingerprints)
+
+
+def place_body(count, base_ref, slots_ref, *refs):
+    chunks, before, out_ref = refs[:count], refs[count:-1], refs[-1]
+    slots = slots_ref[...]
+    lane = lax.broadcasted_iota(jnp.int32, slots.shape, 1).astype(jnp.float32)
+    got = before[0][...].astype(jnp.float32) if before else jnp.zeros(out_ref.shape, jnp.float32)
+    for n, chunk in enumerate(chunks):
+        inside = slots - base_ref[n].astype(jnp.float32)
+        chosen = jnp.concatenate(
+            [
+                (inside == lane + h).astype(jnp.float32)
+                for h in range(0, chunk.shape[0], LANES)
+            ],
+            axis=1,
+        )
+        got = got + dot_nn(chosen.astype(jnp.bfloat16), chunk[...])
+    out_ref[...] = got.astype(jnp.bfloat16)
+
+
+def place(owners, chunks, slots, before=None):
+    capacity, length = chunks[0].shape
+    landmarks = slots.shape[0]
+    tile = pl.BlockSpec((TILE, length), lambda i: (i, 0))
+    extra = [] if before is None else [before]
+    return pl.pallas_call(
+        functools.partial(place_body, len(chunks)),
+        grid=(landmarks // TILE,),
+        in_specs=[
+            pl.BlockSpec(memory_space=pltpu.SMEM),
+            pl.BlockSpec((TILE, LANES), lambda i: (i, 0)),
+        ]
+        + [pl.BlockSpec((capacity, length), lambda i: (0, 0))] * len(chunks)
+        + [tile] * len(extra),
+        out_specs=tile,
+        out_shape=jax.ShapeDtypeStruct((landmarks, length), jnp.bfloat16),
+        compiler_params=pltpu.CompilerParams(vmem_limit_bytes=VMEM_BYTES),
+        name="place",
+    )((jnp.stack(owners) * capacity).astype(jnp.int32), slots, *chunks, *extra)
+
+
 def landmarks_everywhere(fingerprints, landmark_index):
-    rows_dev = fingerprints.shape[0]
-    devices = lax.axis_size("dp")
-    landmarks = landmark_index.shape[0]
-    land_share = landmarks // devices
     position = lax.axis_index("dp")
-    owner_dev = landmark_index // rows_dev
-    offset = landmark_index % rows_dev
-    is_mine = owner_dev == position
-    capacity = 2 * land_share
-    owner_onehot = (owner_dev[:, None] == jnp.arange(devices, dtype=jnp.int32)[None, :]).astype(
-        jnp.int32
-    )
-    owner_rank = jnp.sum(jnp.cumsum(owner_onehot, axis=0) * owner_onehot, axis=1) - 1
-    slot_rows = (
-        jnp.zeros((capacity,), jnp.int32)
-        .at[jnp.where(is_mine, owner_rank, capacity)]
-        .set(offset, mode="drop")
-    )
-    packed = fingerprints[slot_rows]
-    gathered = lax.all_gather(packed, "dp", axis=0, tiled=True)
-    return gathered[owner_dev * capacity + owner_rank]
+    packed, slots = pack(position, landmark_index, fingerprints)
+    held = {0: packed}
+    for perm, mask in ((FAR, 8), (NEAR, 4), (ROW, 2)):
+        held[mask] = send(packed, perm)
+    held[12] = send(held[8], NEAR)
+    held[6] = send(held[4], ROW)
+    held[10] = send(held[8], ROW)
+    held[14] = send(held[12], ROW)
+    result = None
+    for masks in ((0, 2, 4, 8), (6, 12, 10), (14,)):
+        owners, chunks = [], []
+        for m in masks:
+            owners += [position ^ m, position ^ m ^ 1]
+            chunks += [held[m], send(held[m], CORE)]
+        result = place(owners, chunks, slots, result)
+    return result
 
 
 def local_16(fingerprints, targets, landmark_index):
@@ -361,6 +458,39 @@
     def row_sum(pair):
         return pair[0] + send(pair[1], ROW).astype(jnp.float32)
 
+    stats = gather_chips(jnp.concatenate([mean, target_sum, lead, weight], axis=1))
+    means, target_sums = stats[:, :landmarks], stats[:, landmarks : landmarks + LANES]
+    leads = stats[:, landmarks + LANES : 2 * landmarks + LANES]
+    lead_weights = stats[:, 2 * landmarks + LANES : 2 * landmarks + LANES + 1]
+    shift = means - jnp.mean(means, axis=0, keepdims=True)
+    left_terms = jnp.concatenate([shift * chip_rows, leads], axis=0)
+    right_terms = jnp.concatenate([shift, leads * lead_weights], axis=0)
+
+    def system_part(sums, start, cols):
+        rows_fps = lax.dynamic_slice_in_dim(landmark_fps, start, share, 0)
+        terms = lax.dynamic_slice_in_dim(left_terms, start, share, 1)
+        return (sums + highest(terms, right_terms[:, cols])) * scale + tanimoto(
+            rows_fps, landmark_fps[cols], norms[cols]
+        )
+
+    def both_blocks(block):
+        other = send(block, CORE)
+        return lax.dynamic_slice_in_dim(
+            jnp.concatenate([block, other, block], axis=0), core * share, 2 * share, 0
+        )
+
+    panel_cols, other_cols = slice(0, width), slice(width, landmarks)
+    corner = first_rest[:, panel_cols]
+    corner = corner.astype(jnp.float32) + send(corner, ROW).astype(jnp.float32)
+    half = corner.astype(jnp.bfloat16)
+    for s in (2, 1, 3):
+        corner = corner + send(half, rotate(s)).astype(jnp.float32)
+    corner = both_blocks(system_part(corner, core * share, panel_cols))
+    state = jnp.concatenate([corner, jnp.eye(width, dtype=jnp.float32)], axis=1)
+    for b in range(0, width // CHOL, 2):
+        state = eliminate_blocks(state, (b, b + 1))
+
+    first_rest = first_rest[:, other_cols]
     quarter = share // 4
 
     def quarter_of(q):
@@ -378,6 +508,11 @@
         quarters = lax.dynamic_update_index_in_dim(
             quarters, send(part, rotate(s)), (layer + 4 - s) % 4, 0
         )
+    block = system_part(
+        quarters.reshape(share, landmarks - width).astype(jnp.float32), core * share, other_cols
+    )
+    panel_rows = jnp.concatenate([corner, both_blocks(block)], axis=1)
+    factor = exact_dot(state[:, width:], panel_rows)
 
     three, two = reduced_pieces((3, 2))
     one, zero = reduced_pieces((1, 0))
@@ -387,34 +522,8 @@
     one = row_sum(one).astype(jnp.bfloat16)
     own = row_sum(zero) + send(one, NEAR).astype(jnp.float32) + send(two, FAR).astype(jnp.float32)
 
-    stats = gather_chips(jnp.concatenate([mean, target_sum, lead, weight], axis=1))
-    means, target_sums = stats[:, :landmarks], stats[:, landmarks : landmarks + LANES]
-    leads = stats[:, landmarks + LANES : 2 * landmarks + LANES]
-    lead_weights = stats[:, 2 * landmarks + LANES : 2 * landmarks + LANES + 1]
-    shift = means - jnp.mean(means, axis=0, keepdims=True)
-    left_terms = jnp.concatenate([shift * chip_rows, leads], axis=0)
-    right_terms = jnp.concatenate([shift, leads * lead_weights], axis=0)
-
-    def add_back(start):
-        return highest(lax.dynamic_slice_in_dim(left_terms, start, share, 1), right_terms)
-
-    block_fps = lax.dynamic_slice_in_dim(landmark_fps, core * share, share, 0)
-    block = (quarters.reshape(share, landmarks).astype(jnp.float32) + add_back(core * share)) * scale
-    block = block + tanimoto(block_fps, landmark_fps, norms)
-    other = send(block, CORE)
-    panel_rows = lax.dynamic_slice_in_dim(
-        jnp.concatenate([block, other, block], axis=0), core * share, 2 * share, 0
-    )
-    state = jnp.concatenate([panel_rows[:, :width], jnp.eye(width, dtype=jnp.float32)], axis=1)
-    for b in range(0, width // CHOL, 2):
-        state = eliminate_blocks(state, (b, b + 1))
-    factor = exact_dot(state[:, width:], panel_rows)
-
     start = position * share
-    own_fps = lax.dynamic_slice_in_dim(landmark_fps, start, share, 0)
-    rest = (own[:, : landmarks - width] + add_back(start)[:, width:]) * scale + tanimoto(
-        own_fps, landmark_fps[width:], norms[width:]
-    )
+    rest = system_part(own[:, : landmarks - width], start, other_cols)
     own_shift = lax.dynamic_slice_in_dim(shift, start, share, 1)
     rhs = (own[:, landmarks - width :] + highest(own_shift, target_sums)) / math.sqrt(
         ridge_weight * total_rows

time: 293 us -> 301 us (1.027)
  Pallas kernels: 82.3 us -> 108 us
  waiting for transfers between devices: 117 us -> 96.6 us
  starting transfers between devices: 20.2 us -> 37.9 us
  between operations: 14.6 us -> 1.12 us
  local copies, waits for them, and re-layouts: 29.6 us -> 17.2 us
  other arithmetic: 17.2 us -> 23.1 us
  matrix products: 11.9 us -> 15.6 us
    all_gather x1 -> x0, waiting for transfers between devices: 47.4 us -> none  [landmarks_everywhere(): gathered = lax.all_gather(packed, 'dp', axis=0, tiled=True)]
    pallas_call x0 -> x4, Pallas kernels: none -> 29.6 us  [the longest x3 24.8 us: place(): pl.pallas_call(functools.partial(place_body, len(chunks)), grid=(landmark...]
    ppermute x21 -> x41, waiting for transfers between devices: 69.5 us -> 96.6 us  [send(): return lax.ppermute(x, 'dp', perm)]
    ppermute x21 -> x41, starting transfers between devices: 20.2 us -> 37.9 us  [send(): return lax.ppermute(x, 'dp', perm)]
    gather x2 -> x0, local copies, waits for them, and re-layouts: 12.2 us -> none  [the longest x1 10.3 us: landmarks_everywhere(): return gathered[owner_dev * capacity + owner_rank]]
    scatter x1 -> x0, local copies, waits for them, and re-layouts: 8.04 us -> none  [landmarks_everywhere(): slot_rows = jnp.zeros((capacity,), jnp.int32).at[jnp.where(is_mine, owner...]
    another operation x3 -> x0, other arithmetic: 4.82 us -> none
    pallas_call x4, Pallas kernels: 38.9 us -> 34.5 us  [eliminate_blocks(): pl.pallas_call(functools.partial(factor_body, blocks), in_specs=vmem(1),...]
  transfers between devices with their start and end apart: 22 -> 41, of which waited for: 11 -> 15; matrix products, arithmetic and copies ran while one was open for 7% -> 15% of each run, Pallas kernels for 16% -> 21%
where the time goes in v3:
time: 301 us; the launch traced here: 299 us
  Pallas kernels  108 us (36%)
  waiting for transfers between devices  96.6 us (32%)
  starting transfers between devices  37.9 us (13%)
  other arithmetic  23.1 us (8%)
  local copies, waits for them, and re-layouts  17.2 us (6%)
  matrix products  15.6 us (5%)
    ppermute x41, waiting for transfers between devices, send(): return lax.ppermute(x, 'dp', perm)  96.6 us
    ppermute x41, starting transfers between devices, send(): return lax.ppermute(x, 'dp', perm)  37.9 us
    pallas_call x4, Pallas kernels, eliminate_blocks(): pl.pallas_call(functools.partial(factor_body, blocks), in_specs=vmem(1),...  34.5 us
    pallas_call x1, Pallas kernels, stage(): pl.pallas_call(stage_body, grid_spec=pltpu.PrefetchScalarGridSpec(num_sca...  24.8 us
    pallas_call x3, Pallas kernels, place(): pl.pallas_call(functools.partial(place_body, len(chunks)), grid=(landmark...  24.8 us
    pallas_call x2, Pallas kernels, pieces(): pl.pallas_call(pieces_body, in_specs=[pl.BlockSpec(memory_space=pltpu.SME...  18.8 us
    dot_general x5, matrix products, highest(): lax.dot_general(a, b, (((0,), (0,)), ((), ())), precision=lax.Precision.H...  8.72 us
  transfers between devices with their start and end apart: 41, of which 15 were waited for; matrix products, arithmetic and copies ran while one was open for 15% of the time, Pallas kernels for 21%

profile of v3, /device:TPU:0, one launch (start us, length us, event | category | flops | bytes accessed | tf_op | source)
XLA Modules:
  0.0 299.4 jit_solution(12970545261502815725)
XLA Ops:
  0.7 4.8 %pack.1 = (bf16[256,512]{1,0:T(8,128)(2,1)}, f32[2048,128]{1,0:T(8,128)}) custom-call(s32[1]{0:T(128)} %bitcast.7.at_ref, s32[1,2048]{1,0:T(1,128)} %bitcast.45, bf16[1024,512]{1,0:T(8,128)(2,1)} %fps_ref.1), custom_call_target="tpu_custom_call" | custom-call | tf_op jit(solution)/shard_map/pack/pallas_call | solution.py:352
  5.5 4.0 %collective-permute-start = (bf16[256,512]{1,0:T(8,128)(2,1)}, bf16[256,512]{1,0:T(8,128)(2,1)}, u32[]{:S(2)}, u32[]{:S(2)}) collective-permute-start(bf16[256,512]{1,0:T(8,128)(2,1)} %get-tuple-element.21.refs_0_), channel_id=1, source_target_pairs={{0,8},{1,9},{2,10},{3,11},{4,12},{5,13},{6,14},{7,15},{8,0},{9,1},... | collective-permute-start | bytes 786440 | tf_op jit(solution)/shard_map/ppermute | solution.py:99
  14.6 7.3 %collective-permute-done.refs_6_ = bf16[256,512]{1,0:T(8,128)(2,1)} collective-permute-done((bf16[256,512]{1,0:T(8,128)(2,1)}, bf16[256,512]{1,0:T(8,128)(2,1)}, u32[]{:S(2)}, u32[]{:S(2)}) %collective-permute-start) | collective-permute-done | bytes 262176 | tf_op jit(solution)/shard_map/ppermute | solution.py:99
  26.9 3.9 %collective-permute-done.1.refs_2_ = bf16[256,512]{1,0:T(8,128)(2,1)S(1)} collective-permute-done((bf16[256,512]{1,0:T(8,128)(2,1)}, bf16[256,512]{1,0:T(8,128)(2,1)S(1)}, u32[]{:S(2)}, u32[]{:S(2)}) %collective-permute-start.1) | collective-permute-done | bytes 262176 | tf_op jit(solution)/shard_map/ppermute | solution.py:99
  42.5 9.0 %place.3.refs_6_ = bf16[2048,512]{1,0:T(8,128)(2,1)} custom-call(s32[8]{0:T(128)} %broadcast_multiply_fusion.3.base_ref, f32[2048,128]{1,0:T(8,128)} %get-tuple-element.20.slots_ref, bf16[256,512]{1,0:T(8,128)(2,1)} %get-tuple-element.21.refs_0_, bf16[256,512]{1,0:T(8,128)(2,1)} %collective-permute-done.10.refs_1_, ...), custom_call_target="tpu_custom_call" | custom-call | tf_op jit(solution)/shard_map/place/pallas_call | solution.py:392
  52.8 8.6 %place.4.refs_2_ = bf16[2048,512]{1,0:T(8,128)(2,1)} custom-call(s32[6]{0:T(128)} %broadcast_multiply_fusion.4.base_ref, f32[2048,128]{1,0:T(8,128)} %get-tuple-element.20.slots_ref, bf16[256,512]{1,0:T(8,128)(2,1)} %copy-done.16, bf16[256,512]{1,0:T(8,128)(2,1)} %collective-permute-done.6.refs_1_, bf16[256,512]{1,0:T(8,128)(2,1)} %copy-done.15, ...), custom_call_target="tpu_custom_call" | custom-call | tf_op jit(solution)/shard_map/place/pallas_call | solution.py:392
  64.7 7.2 %place.5.land_ref = bf16[2048,512]{1,0:T(8,128)(2,1)} custom-call(s32[2]{0:T(128)} %add_multiply_fusion.base_ref, f32[2048,128]{1,0:T(8,128)} %get-tuple-element.20.slots_ref, bf16[256,512]{1,0:T(8,128)(2,1)} %copy-done.18, bf16[256,512]{1,0:T(8,128)(2,1)} %copy-done.20, bf16[2048,512]{1,0:T(8,128)(2,1)} %place.4.refs_2_), custom_call_target="tpu_custom_call" | custom-call | tf_op jit(solution)/shard_map/place/pallas_call | solution.py:392
  74.0 24.8 %stage.1 = (bf16[2048,2048]{1,0:T(8,128)(2,1)}, f32[1,2048]{1,0:T(1,128)}, f32[8,128,128]{2,1,0:T(8,128)}, bf16[128,2048]{1,0:T(8,128)(2,1)}, f32[1,2048]{1,0:T(...) custom-call(s32[1]{0:T(128)} %bitcast.4.core_ref, bf16[2048,512]{1,0:T(8,128)(2,1)} %place.5.land_ref, ...), custom_call_target="tpu_custom_call" | custom-call | tf_op jit(solution)/shard_map/stage/pallas_call | solution.py:201
  98.9 9.5 %pieces.3 = (f32[128,1920]{1,0:T(8,128)}, bf16[128,1920]{1,0:T(8,128)(2,1)}, f32[128,1920]{1,0:T(8,128)}, bf16[128,1920]{1,0:T(8,128)(2,1)}) custom-call(s32[4]{0:T(128)} %get-tuple-element.57.at_ref, bf16[2048,2048]{1,0:T(8,128)(2,1)} %get-tuple-element.22.ct_ref, f32[1,2048]{1,0:T(1,128)} %get-tuple-element.23.lead_ref, ...), custom_call_target="tpu_custom_call" | custom-call | tf_op jit(solution)/shard_map/pieces/pallas_call | solution.py:251
  112.7 19.9 %collective-permute-done.24 = f32[1,4352]{1,0:T(1,128)S(1)} collective-permute-done((f32[1,4352]{1,0:T(1,128)S(1)}, f32[1,4352]{1,0:T(1,128)S(1)}, u32[]{:S(2)}, u32[]{:S(2)}) %collective-permute-start.24) | collective-permute-done | bytes 17440 | tf_op jit(solution)/shard_map/ppermute | solution.py:99
  137.0 2.6 collective-permute-start.27
  141.0 9.3 %pieces.2 = (f32[128,1920]{1,0:T(8,128)}, bf16[128,1920]{1,0:T(8,128)(2,1)}, f32[128,1920]{1,0:T(8,128)}, bf16[128,1920]{1,0:T(8,128)(2,1)}) custom-call(s32[4]{0:T(128)} %get-tuple-element.56.at_ref, bf16[2048,2048]{1,0:T(8,128)(2,1)} %get-tuple-element.22.ct_ref, f32[1,2048]{1,0:T(1,128)} %get-tuple-element.23.lead_ref, ...), custom_call_target="tpu_custom_call" | custom-call | tf_op jit(solution)/shard_map/pieces/pallas_call | solution.py:251
  166.9 5.2 %collective-permute-done.33 = bf16[32,1792]{1,0:T(8,128)(2,1)S(1)} collective-permute-done((bf16[32,1792]{1,0:T(8,128)(2,1)S(1)}, bf16[32,1792]{1,0:T(8,128)(2,1)S(1)}, u32[]{:S(2)}, u32[]{:S(2)}) %collective-permute-start.33) | collective-permute-done | bytes 114720 | tf_op jit(solution)/shard_map/ppermute | solution.py:99
  180.3 13.8 %collective-permute-done.36 = bf16[32,1792]{1,0:T(8,128)(2,1)S(1)} collective-permute-done((bf16[32,1792]{1,0:T(8,128)(2,1)S(1)}, bf16[32,1792]{1,0:T(8,128)(2,1)S(1)}, u32[]{:S(2)}, u32[]{:S(2)}) %collective-permute-start.36) | collective-permute-done | bytes 114720 | tf_op jit(solution)/shard_map/ppermute | solution.py:99
  195.5 2.6 collective-permute-start.37
  200.2 9.0 %factor.4.state_ref = f32[256,512]{1,0:T(8,128)} custom-call(f32[256,512]{1,0:T(8,128)} %pad_maximum_fusion.2.state_ref), custom_call_target="tpu_custom_call" | custom-call | tf_op jit(solution)/shard_map/factor/pallas_call | solution.py:305
  209.2 8.7 %factor.5.state_ref = f32[256,512]{1,0:T(8,128)} custom-call(f32[256,512]{1,0:T(8,128)} %factor.4.state_ref), custom_call_target="tpu_custom_call" | custom-call | tf_op jit(solution)/shard_map/factor/pallas_call | solution.py:305
  217.9 8.6 %factor.6.state_ref = f32[256,512]{1,0:T(8,128)} custom-call(f32[256,512]{1,0:T(8,128)} %factor.5.state_ref), custom_call_target="tpu_custom_call" | custom-call | tf_op jit(solution)/shard_map/factor/pallas_call | solution.py:305
  226.5 8.2 %factor.7 = f32[256,512]{1,0:T(8,128)} custom-call(f32[256,512]{1,0:T(8,128)} %factor.6.state_ref), custom_call_target="tpu_custom_call" | custom-call | tf_op jit(solution)/shard_map/factor/pallas_call | solution.py:305
  235.9 5.8 %collective-permute-done.38 = bf16[32,1792]{1,0:T(8,128)(2,1)S(1)} collective-permute-done((bf16[32,1792]{1,0:T(8,128)(2,1)}, bf16[32,1792]{1,0:T(8,128)(2,1)S(1)}, u32[]{:S(2)}, u32[]{:S(2)}) %collective-permute-start.38) | collective-permute-done | bytes 114720 | tf_op jit(solution)/shard_map/ppermute | solution.py:99
  242.3 4.3 %collective-permute-done.39 = bf16[32,1792]{1,0:T(8,128)(2,1)S(1)} collective-permute-done((bf16[32,1792]{1,0:T(8,128)(2,1)}, bf16[32,1792]{1,0:T(8,128)(2,1)S(1)}, u32[]{:S(2)}, u32[]{:S(2)}) %collective-permute-start.39) | collective-permute-done | bytes 114720 | tf_op jit(solution)/shard_map/ppermute | solution.py:99
  257.7 10.1 %collective-permute-done.22 = bf16[128,1920]{1,0:T(8,128)(2,1)S(1)} collective-permute-done((bf16[128,1920]{1,0:T(8,128)(2,1)S(1)}, bf16[128,1920]{1,0:T(8,128)(2,1)S(1)}, u32[]{:S(2)}, u32[]{:S(2)}) %collective-permute-start.22) | collective-permute-done | bytes 491552 | tf_op jit(solution)/shard_map/ppermute | solution.py:99
  275.4 8.6 %collective-permute-done.19 = bf16[128,1920]{1,0:T(8,128)(2,1)} collective-permute-done((bf16[128,1920]{1,0:T(8,128)(2,1)}, bf16[128,1920]{1,0:T(8,128)(2,1)}, u32[]{:S(2)}, u32[]{:S(2)}) %collective-permute-start.19) | collective-permute-done | bytes 491552 | tf_op jit(solution)/shard_map/ppermute | solution.py:99
  283.9 9.7 %collective-permute-done.23 = bf16[128,1920]{1,0:T(8,128)(2,1)} collective-permute-done((bf16[128,1920]{1,0:T(8,128)(2,1)}, bf16[128,1920]{1,0:T(8,128)(2,1)}, u32[]{:S(2)}, u32[]{:S(2)}) %collective-permute-start.23) | collective-permute-done | bytes 491552 | tf_op jit(solution)/shard_map/ppermute | solution.py:99
  (184 shorter events, 92.7 us)
Async XLA Ops:
  5.5 16.4 %collective-permute-start = (bf16[256,512]{1,0:T(8,128)(2,1)}, bf16[256,512]{1,0:T(8,128)(2,1)}, u32[]{:S(2)}, u32[]{:S(2)}) collective-permute-start(bf16[256,512]{1,0:T(8,128)(2,1)} %get-tuple-element.21.refs_0_), channel_id=1, source_target_pairs={{0,8},{1,9},{2,10},{3,11},{4,12},{5,13},{6,14},{7,15},{8,0},{9,1},... | collective-permute-start | bytes 786440 | tf_op jit(solution)/shard_map/ppermute | solution.py:99
  9.5 12.5 %collective-permute-start.4 = (bf16[256,512]{1,0:T(8,128)(2,1)}, bf16[256,512]{1,0:T(8,128)(2,1)}, u32[]{:S(2)}, u32[]{:S(2)}) collective-permute-start(bf16[256,512]{1,0:T(8,128)(2,1)} %get-tuple-element.21.refs_0_), channel_id=1, source_target_pairs={{0,4},{1,5},{2,6},{3,7},{4,0},{5,1},{6,2},{7,3},{8,12},{9,13},{10,... | collective-permute-start | bytes 786440 | tf_op jit(solution)/shard_map/ppermute | solution.py:99
  11.1 12.4 %collective-permute-start.10 = (bf16[256,512]{1,0:T(8,128)(2,1)}, bf16[256,512]{1,0:T(8,128)(2,1)}, u32[]{:S(2)}, u32[]{:S(2)}) collective-permute-start(bf16[256,512]{1,0:T(8,128)(2,1)} %get-tuple-element.21.refs_0_), channel_id=1, source_target_pairs={{0,1},{1,0},{2,3},{3,2},{4,5},{5,4},{6,7},{7,6},{8,9},{9,8},{10,11... | collective-permute-start | bytes 786440 | tf_op jit(solution)/shard_map/ppermute | solution.py:99
  11.1 15.3 %collective-permute-start.11 = (bf16[256,512]{1,0:T(8,128)(2,1)}, bf16[256,512]{1,0:T(8,128)(2,1)}, u32[]{:S(2)}, u32[]{:S(2)}) collective-permute-start(bf16[256,512]{1,0:T(8,128)(2,1)} %get-tuple-element.21.refs_0_), channel_id=1, source_target_pairs={{0,2},{1,3},{2,0},{3,1},{4,6},{5,7},{6,4},{7,5},{8,10},{9,11},{10,... | collective-permute-start | bytes 786440 | tf_op jit(solution)/shard_map/ppermute | solution.py:99
  12.6 48.8 %collective-permute-start.15 = (bf16[1024,512]{1,0:T(8,128)(2,1)}, bf16[1024,512]{1,0:T(8,128)(2,1)}, u32[]{:S(2)}, u32[]{:S(2)}) collective-permute-start(bf16[1024,512]{1,0:T(8,128)(2,1)} %fps_ref.1), channel_id=1, source_target_pairs={{0,1},{1,0},{2,3},{3,2},{4,5},{5,4},{6,7},{7,6},{8,9},{9,8},{10,11... | collective-permute-start | bytes 3145736 | tf_op jit(solution)/shard_map/ppermute | solution.py:99
  36.7 14.8 %collective-permute-start.2 = (bf16[256,512]{1,0:T(8,128)(2,1)S(1)}, bf16[256,512]{1,0:T(8,128)(2,1)S(1)}, u32[]{:S(2)}, u32[]{:S(2)}) collective-permute-start(bf16[256,512]{1,0:T(8,128)(2,1)S(1)} %collective-permute-done.1.refs_2_), channel_id=1, source_target_pairs={{0,2},{1,3},{2,0},{3,1},{4,6},{5,7},{6,4},{7,5},{8,10},{9,11},{10,... | collective-permute-start | bytes 786440 | tf_op jit(solution)/shard_map/ppermute | solution.py:99
  38.3 13.8 %collective-permute-start.7 = (bf16[256,512]{1,0:T(8,128)(2,1)S(1)}, bf16[256,512]{1,0:T(8,128)(2,1)S(1)}, u32[]{:S(2)}, u32[]{:S(2)}) collective-permute-start(bf16[256,512]{1,0:T(8,128)(2,1)S(1)} %collective-permute-done.1.refs_2_), channel_id=1, source_target_pairs={{0,1},{1,0},{2,3},{3,2},{4,5},{5,4},{6,7},{7,6},{8,9},{9,8},{10,11... | collective-permute-start | bytes 786440 | tf_op jit(solution)/shard_map/ppermute | solution.py:99
  38.3 13.8 %collective-permute-start.6 = (bf16[256,512]{1,0:T(8,128)(2,1)S(1)}, bf16[256,512]{1,0:T(8,128)(2,1)}, u32[]{:S(2)}, u32[]{:S(2)}) collective-permute-start(bf16[256,512]{1,0:T(8,128)(2,1)S(1)} %collective-permute-done.5.refs_0_), channel_id=1, source_target_pairs={{0,1},{1,0},{2,3},{3,2},{4,5},{5,4},{6,7},{7,6},{8,9},{9,8},{10,11... | collective-permute-start | bytes 786440 | tf_op jit(solution)/shard_map/ppermute | solution.py:99
  38.8 13.3 %collective-permute-start.9 = (bf16[256,512]{1,0:T(8,128)(2,1)S(1)}, bf16[256,512]{1,0:T(8,128)(2,1)}, u32[]{:S(2)}, u32[]{:S(2)}) collective-permute-start(bf16[256,512]{1,0:T(8,128)(2,1)S(1)} %collective-permute-done.8.refs_4_), channel_id=1, source_target_pairs={{0,1},{1,0},{2,3},{3,2},{4,5},{5,4},{6,7},{7,6},{8,9},{9,8},{10,11... | collective-permute-start | bytes 786440 | tf_op jit(solution)/shard_map/ppermute | solution.py:99
  108.4 144.0 %collective-permute-start.21 = (bf16[128,1920]{1,0:T(8,128)(2,1)}, bf16[128,1920]{1,0:T(8,128)(2,1)}, u32[]{:S(2)}, u32[]{:S(2)}) collective-permute-start(bf16[128,1920]{1,0:T(8,128)(2,1)} %get-tuple-element.33), channel_id=1, source_target_pairs={{0,2},{1,3},{2,0},{3,1},{4,6},{5,7},{6,4},{7,5},{8,10},{9,11},{10,... | collective-permute-start | bytes 1474568 | tf_op jit(solution)/shard_map/ppermute | solution.py:99
  108.8 148.8 %collective-permute-start.20 = (bf16[128,1920]{1,0:T(8,128)(2,1)}, bf16[128,1920]{1,0:T(8,128)(2,1)}, u32[]{:S(2)}, u32[]{:S(2)}) collective-permute-start(bf16[128,1920]{1,0:T(8,128)(2,1)} %get-tuple-element.31), channel_id=1, source_target_pairs={{0,2},{1,3},{2,0},{3,1},{4,6},{5,7},{6,4},{7,5},{8,10},{9,11},{10,... | collective-permute-start | bytes 1474568 | tf_op jit(solution)/shard_map/ppermute | solution.py:99
  110.4 22.3 %collective-permute-start.24 = (f32[1,4352]{1,0:T(1,128)S(1)}, f32[1,4352]{1,0:T(1,128)S(1)}, u32[]{:S(2)}, u32[]{:S(2)}) collective-permute-start(f32[1,4352]{1,0:T(1,128)S(1)} %pad_maximum_fusion.7), channel_id=1, source_target_pairs={{0,2},{1,3},{2,0},{3,1},{4,6},{5,7},{6,4},{7,5},{8,10},{9,11},{10,... | collective-permute-start | bytes 52232 | tf_op jit(solution)/shard_map/ppermute | solution.py:99
  133.3 18.5 %collective-permute-start.25 = (f32[2,4352]{1,0:T(2,128)}, f32[2,4352]{1,0:T(2,128)}, u32[]{:S(2)}, u32[]{:S(2)}) collective-permute-start(f32[2,4352]{1,0:T(2,128)} %pad_maximum_fusion.6), channel_id=1, source_target_pairs={{0,4},{1,5},{2,6},{3,7},{4,8},{5,9},{6,10},{7,11},{8,12},{9,13},{1... | collective-permute-start | bytes 104456 | tf_op jit(solution)/shard_map/ppermute | solution.py:99
  134.8 17.6 %collective-permute-start.26 = (f32[2,4352]{1,0:T(2,128)}, f32[2,4352]{1,0:T(2,128)}, u32[]{:S(2)}, u32[]{:S(2)}) collective-permute-start(f32[2,4352]{1,0:T(2,128)} %pad_maximum_fusion.6), channel_id=1, source_target_pairs={{0,8},{1,9},{2,10},{3,11},{4,12},{5,13},{6,14},{7,15},{8,0},{9,1},... | collective-permute-start | bytes 104456 | tf_op jit(solution)/shard_map/ppermute | solution.py:99
  137.0 15.3 %collective-permute-start.27 = (f32[2,4352]{1,0:T(2,128)}, f32[2,4352]{1,0:T(2,128)}, u32[]{:S(2)}, u32[]{:S(2)}) collective-permute-start(f32[2,4352]{1,0:T(2,128)} %pad_maximum_fusion.6), channel_id=1, source_target_pairs={{0,12},{1,13},{2,14},{3,15},{4,0},{5,1},{6,2},{7,3},{8,4},{9,5},{1... | collective-permute-start | bytes 104456 | tf_op jit(solution)/shard_map/ppermute | solution.py:99
  152.4 14.4 %collective-permute-start.34 = (bf16[32,1792]{1,0:T(8,128)(2,1)}, bf16[32,1792]{1,0:T(8,128)(2,1)}, u32[]{:S(2)}, u32[]{:S(2)}) collective-permute-start(bf16[32,1792]{1,0:T(8,128)(2,1)} %get-tuple-element.51), channel_id=1, source_target_pairs={{0,4},{1,5},{2,6},{3,7},{4,8},{5,9},{6,10},{7,11},{8,12},{9,13},{1... | collective-permute-start | bytes 344072 | tf_op jit(solution)/shard_map/ppermute | solution.py:99
  173.1 80.6 %collective-permute-start.18 = (bf16[128,1920]{1,0:T(8,128)(2,1)}, bf16[128,1920]{1,0:T(8,128)(2,1)}, u32[]{:S(2)}, u32[]{:S(2)}) collective-permute-start(bf16[128,1920]{1,0:T(8,128)(2,1)} %get-tuple-element.29), channel_id=1, source_target_pairs={{0,2},{1,3},{2,0},{3,1},{4,6},{5,7},{6,4},{7,5},{8,10},{9,11},{10,... | collective-permute-start | bytes 1474568 | tf_op jit(solution)/shard_map/ppermute | solution.py:99
  174.7 100.6 %collective-permute-start.17 = (bf16[128,1920]{1,0:T(8,128)(2,1)}, bf16[128,1920]{1,0:T(8,128)(2,1)}, u32[]{:S(2)}, u32[]{:S(2)}) collective-permute-start(bf16[128,1920]{1,0:T(8,128)(2,1)} %get-tuple-element.27), channel_id=1, source_target_pairs={{0,2},{1,3},{2,0},{3,1},{4,6},{5,7},{6,4},{7,5},{8,10},{9,11},{10,... | collective-permute-start | bytes 1474568 | tf_op jit(solution)/shard_map/ppermute | solution.py:99
  177.6 16.5 %collective-permute-start.36 = (bf16[32,1792]{1,0:T(8,128)(2,1)S(1)}, bf16[32,1792]{1,0:T(8,128)(2,1)S(1)}, u32[]{:S(2)}, u32[]{:S(2)}) collective-permute-start(bf16[32,1792]{1,0:T(8,128)(2,1)S(1)} %add_convert_fusion.4), channel_id=1, source_target_pairs={{0,2},{1,3},{2,0},{3,1},{4,6},{5,7},{6,4},{7,5},{8,10},{9,11},{10,... | collective-permute-start | bytes 344072 | tf_op jit(solution)/shard_map/ppermute | solution.py:99
  195.5 39.2 %collective-permute-start.37 = (bf16[32,1792]{1,0:T(8,128)(2,1)}, bf16[32,1792]{1,0:T(8,128)(2,1)}, u32[]{:S(2)}, u32[]{:S(2)}) collective-permute-start(bf16[32,1792]{1,0:T(8,128)(2,1)} %get-tuple-element.46), channel_id=1, source_target_pairs={{0,8},{1,9},{2,10},{3,11},{4,12},{5,13},{6,14},{7,15},{8,0},{9,1},... | collective-permute-start | bytes 344072 | tf_op jit(solution)/shard_map/ppermute | solution.py:99
  252.3 18.5 %collective-permute-start.40 = (f32[128,1792]{0,1:T(8,128)S(1)}, f32[128,1792]{0,1:T(8,128)S(1)}, u32[]{:S(2)}, u32[]{:S(2)}) collective-permute-start(f32[128,1792]{0,1:T(8,128)S(1)} %fusion.11), channel_id=1, source_target_pairs={{0,1},{1,0},{2,3},{3,2},{4,5},{5,4},{6,7},{7,6},{8,9},{9,8},{10,11... | collective-permute-start | bytes 2752520 | tf_op jit(solution)/shard_map/ppermute | solution.py:99
  253.7 14.1 %collective-permute-start.22 = (bf16[128,1920]{1,0:T(8,128)(2,1)S(1)}, bf16[128,1920]{1,0:T(8,128)(2,1)S(1)}, u32[]{:S(2)}, u32[]{:S(2)}) collective-permute-start(bf16[128,1920]{1,0:T(8,128)(2,1)S(1)} %add_convert_fusion.1), channel_id=1, source_target_pairs={{0,4},{1,5},{2,6},{3,7},{4,0},{5,1},{6,2},{7,3},{8,12},{9,13},{10,... | collective-permute-start | bytes 1474568 | tf_op jit(solution)/shard_map/ppermute | solution.py:99
  255.6 28.3 %collective-permute-start.19 = (bf16[128,1920]{1,0:T(8,128)(2,1)}, bf16[128,1920]{1,0:T(8,128)(2,1)}, u32[]{:S(2)}, u32[]{:S(2)}) collective-permute-start(bf16[128,1920]{1,0:T(8,128)(2,1)} %add_convert_fusion.2), channel_id=1, source_target_pairs={{0,4},{1,5},{2,6},{3,7},{4,0},{5,1},{6,2},{7,3},{8,12},{9,13},{10,... | collective-permute-start | bytes 1474568 | tf_op jit(solution)/shard_map/ppermute | solution.py:99
  269.7 23.9 %collective-permute-start.23 = (bf16[128,1920]{1,0:T(8,128)(2,1)}, bf16[128,1920]{1,0:T(8,128)(2,1)}, u32[]{:S(2)}, u32[]{:S(2)}) collective-permute-start(bf16[128,1920]{1,0:T(8,128)(2,1)} %add_convert_fusion), channel_id=1, source_target_pairs={{0,8},{1,9},{2,10},{3,11},{4,12},{5,13},{6,14},{7,15},{8,0},{9,1},... | collective-permute-start | bytes 1474568 | tf_op jit(solution)/shard_map/ppermute | solution.py:99
  (46 other events, 521.4 us)

commit v4 on v3

--- a/solution.py
+++ b/solution.py
@@ -88,11 +88,7 @@
 FAR = [(i, i ^ 8) for i in range(16)]
 LANES = 128
 TILE = 256
-VMEM_BYTES = 56 * 2**20
-
-
-def rotate(step):
-    return [(i, (i + 4 * step) % 16) for i in range(16)]
+MIB = 2**20
 
 
 def send(x, perm):
@@ -117,9 +113,8 @@
     return lax.dot_general(a, b, (((1,), (0,)), ((), ())), preferred_element_type=jnp.float32)
 
 
-def gather_chips(x):
-    pair = jnp.concatenate([x, send(x, ROW)], axis=0)
-    return jnp.concatenate([pair] + [send(pair, rotate(s)) for s in (1, 2, 3)], axis=0)
+def after(x, *earlier):
+    return lax.optimization_barrier((x,) + earlier)[0]
 
 
 def vmem(count):
@@ -132,8 +127,8 @@
 
 def stage_body(
     core_ref, land_ref, fps_ref, norms_ref, tgs_ref,
-    ct_ref, mean_ref, rhs_ref, rest_ref, lead_ref, column_ref, weight_ref,
-    cent_ref, first_ref,
+    ct_ref, rhs_ref, rest_ref, message_ref, lead_ref, column_ref,
+    cent_ref, first_ref, left_ref, low_ref, mean_ref,
 ):
     step = pl.program_id(0)
     rows = fps_ref.shape[0]
@@ -151,16 +146,20 @@
     mean = total * (1.0 / rows)
     for n in range(0, rows, TILE):
         cent = cent_ref[:, n : n + TILE] - mean
-        cent_ref[:, n : n + TILE] = cent
-        ct_ref[pl.ds(base, TILE), n : n + TILE] = cent.astype(jnp.bfloat16)
+        high = cent.astype(jnp.bfloat16)
+        ct_ref[:, n : n + TILE] = high
+        low_ref[:, n : n + TILE] = (cent - high.astype(jnp.float32)).astype(jnp.bfloat16)
     mean_ref[:, pl.ds(base, TILE)] = jnp.broadcast_to(mean, (TILE, LANES)).T[:1, :]
-    own = cent_ref[pl.ds(block, LANES), :]
-    high = own.astype(jnp.bfloat16)
-    low = (own - high.astype(jnp.float32)).astype(jnp.bfloat16)
-    rhs_ref[step] = dot_nn(high, tgs_ref[...]) + dot_nn(low, tgs_ref[...])
-    first_ref[:, pl.ds(base, TILE)] = dot_nt(
-        ct_ref[pl.ds(block, LANES), :], ct_ref[pl.ds(base, TILE), :]
-    )
+
+    @pl.when(step == 0)
+    def _():
+        left_ref[:LANES, :] = ct_ref[pl.ds(block, LANES), :]
+        left_ref[LANES:, :] = tgs_ref[...]
+
+    both = dot_nt(left_ref[...], ct_ref[...])
+    first_ref[:, pl.ds(base, TILE)] = both[:LANES, :]
+    cent_ref[:LANES, :TILE] = both[LANES:, :] + dot_nt(left_ref[LANES:, :], low_ref[...])
+    rhs_ref[step] = cent_ref[:LANES, pl.ds(block, LANES)].T
 
     @pl.when(step == pl.num_programs(0) - 1)
     def _():
@@ -171,32 +170,45 @@
         size = jnp.sum(jnp.abs(lead_own), axis=1, keepdims=True)
         usable = mass > 1e-3 * size
         weight = jnp.where(usable, 1.0 / jnp.where(usable, mass, 1.0), 0.0)
-        weight_ref[...] = jnp.broadcast_to(weight, (1, LANES))
         mine = spread(lead_own) * weight
         for j in range(lead.shape[1] // LANES):
             cols = slice(j * LANES, (j + 1) * LANES)
             part = lead[:, cols]
             column_ref[cols, :] = spread(part) * weight
-            rest_ref[:, cols] = (first_ref[:, cols] - mine * part).astype(jnp.bfloat16)
+            rest = first_ref[:, cols] - mine * part
+            if j < TILE // LANES:
+                message_ref[:LANES, cols] = rest
+            else:
+                rest_ref[:, slice(cols.start - TILE, cols.stop - TILE)] = rest.astype(jnp.bfloat16)
+        message_ref[LANES:, :] = jnp.zeros((message_ref.shape[0] - LANES, TILE), jnp.float32)
+        for j in range(lead.shape[1] // TILE):
+            cols = slice(j * TILE, (j + 1) * TILE)
+            message_ref[LANES + j : LANES + j + 1, :] = mean_ref[:, cols]
+            message_ref[LANES + 8 + j : LANES + 9 + j, :] = lead[:, cols]
+        at = LANES + 16
+        message_ref[at : at + 1, :LANES] = jnp.broadcast_to(weight, (1, LANES))
+        sums = jnp.sum(tgs_ref[...].astype(jnp.float32), axis=1, keepdims=True)
+        message_ref[at : at + 1, LANES:] = jnp.broadcast_to(sums, (LANES, LANES)).T[:1, :]
+
+
+STATS = 24
 
 
 def stage(core, landmark_fps, fps, norms, tgs):
     rows, length = fps.shape
     landmarks = landmark_fps.shape[0]
     steps = landmarks // TILE
-    f32 = jnp.float32
+    f32, bf16 = jnp.float32, jnp.bfloat16
 
     def whole(shape):
         return pl.BlockSpec(shape, lambda i, c: (0,) * len(shape))
 
     outs = [
-        ((landmarks, rows), jnp.bfloat16),
-        ((1, landmarks), f32),
         ((steps, LANES, LANES), f32),
-        ((LANES, landmarks), jnp.bfloat16),
+        ((LANES, landmarks - TILE), bf16),
+        ((LANES + STATS, TILE), f32),
         ((1, landmarks), f32),
         ((landmarks, LANES), f32),
-        ((1, LANES), f32),
     ]
     return pl.pallas_call(
         stage_body,
@@ -209,52 +221,63 @@
                 whole(norms.shape),
                 whole(tgs.shape),
             ],
-            out_specs=[whole(s) for s, _ in outs],
+            out_specs=[pl.BlockSpec((TILE, rows), lambda i, c: (i, 0))]
+            + [whole(s) for s, _ in outs],
             scratch_shapes=[
                 pltpu.VMEM((TILE, rows), f32),
                 pltpu.VMEM((LANES, landmarks), f32),
+                pltpu.VMEM((2 * LANES, rows), bf16),
+                pltpu.VMEM((TILE, rows), bf16),
+                pltpu.VMEM((1, landmarks), f32),
             ],
         ),
-        out_shape=[jax.ShapeDtypeStruct(s, d) for s, d in outs],
-        compiler_params=pltpu.CompilerParams(vmem_limit_bytes=VMEM_BYTES),
+        out_shape=[jax.ShapeDtypeStruct((landmarks, rows), bf16)]
+        + [jax.ShapeDtypeStruct(s, d) for s, d in outs],
+        compiler_params=pltpu.CompilerParams(vmem_limit_bytes=28 * MIB),
         name="stage",
     )(core, landmark_fps, fps, norms, tgs)
 
 
-def pieces_body(at_ref, ct_ref, lead_ref, column_ref, rhs_ref, *refs):
-    outs, left_ref = refs[:-1], refs[-1]
-    count = len(outs)
+def pieces_body(at_ref, ct_ref, lead_ref, column_ref, rhs_ref, mine_ref, theirs_ref, left_ref):
+    count = left_ref.shape[0] // LANES
     for p in range(count):
         at = pl.multiple_of(at_ref[p], LANES)
         left_ref[p * LANES : (p + 1) * LANES, :] = ct_ref[pl.ds(at, LANES), :]
+
+    def store(p, cols, value):
+        out = (mine_ref, theirs_ref)[p % 2]
+        out[p // 2 * LANES : (p // 2 + 1) * LANES, cols] = value.astype(out.dtype)
+
     for t in range(1, ct_ref.shape[0] // TILE):
         for q in range(0, count, 2):
             got = dot_nt(
                 left_ref[q * LANES : (q + 2) * LANES, :], ct_ref[t * TILE : (t + 1) * TILE, :]
             )
             for p in (q, q + 1):
-                out = outs[p]
                 at = pl.multiple_of(at_ref[p], LANES)
                 column = column_ref[pl.ds(at, LANES), :]
                 for h in range(TILE // LANES):
                     lo = t * TILE + h * LANES
                     part = got[(p - q) * LANES : (p - q + 1) * LANES, h * LANES : (h + 1) * LANES]
                     part = part - column * lead_ref[:, lo : lo + LANES]
-                    out[:, lo - TILE : lo - TILE + LANES] = part.astype(out.dtype)
-    for p, out in enumerate(outs):
-        out[:, ct_ref.shape[0] - TILE :] = rhs_ref[at_ref[p] // TILE].astype(out.dtype)
+                    store(p, slice(lo - TILE, lo - TILE + LANES), part)
+    for p in range(count):
+        lo = ct_ref.shape[0] - TILE
+        store(p, slice(lo, lo + LANES), rhs_ref[at_ref[p] // TILE])
 
 
 def pieces(starts, ct, lead, column, rhs_part):
-    width = ct.shape[0] - TILE + LANES
-    outs = [jnp.float32, jnp.bfloat16] * (len(starts) // 2)
+    shape = (len(starts) // 2 * LANES, ct.shape[0] - TILE + LANES)
     return pl.pallas_call(
         pieces_body,
         in_specs=[pl.BlockSpec(memory_space=pltpu.SMEM)] + vmem(4),
-        out_specs=vmem(len(outs)),
-        out_shape=[jax.ShapeDtypeStruct((LANES, width), d) for d in outs],
-        scratch_shapes=[pltpu.VMEM((len(outs) * LANES, ct.shape[1]), jnp.bfloat16)],
-        compiler_params=pltpu.CompilerParams(vmem_limit_bytes=VMEM_BYTES),
+        out_specs=vmem(2),
+        out_shape=[
+            jax.ShapeDtypeStruct(shape, jnp.float32),
+            jax.ShapeDtypeStruct(shape, jnp.bfloat16),
+        ],
+        scratch_shapes=[pltpu.VMEM((2 * shape[0], ct.shape[1]), jnp.bfloat16)],
+        compiler_params=pltpu.CompilerParams(vmem_limit_bytes=28 * MIB),
         name="pieces",
     )(jnp.stack(starts).astype(jnp.int32), ct, lead, column, rhs_part)
 
@@ -307,7 +330,7 @@
         in_specs=vmem(1),
         out_specs=vmem(1)[0],
         out_shape=jax.ShapeDtypeStruct(state.shape, jnp.float32),
-        compiler_params=pltpu.CompilerParams(vmem_limit_bytes=VMEM_BYTES),
+        compiler_params=pltpu.CompilerParams(vmem_limit_bytes=28 * MIB),
         name="factor",
     )(state)
 
@@ -361,7 +384,7 @@
             pltpu.VMEM((8, landmarks), jnp.float32),
             pltpu.VMEM((capacity, landmarks), jnp.bfloat16),
         ],
-        compiler_params=pltpu.CompilerParams(vmem_limit_bytes=VMEM_BYTES),
+        compiler_params=pltpu.CompilerParams(vmem_limit_bytes=28 * MIB),
         name="pack",
     )(jnp.reshape(position, (1,)), landmark_index[None, :], fingerprints)
 
@@ -400,7 +423,7 @@
         + [tile] * len(extra),
         out_specs=tile,
         out_shape=jax.ShapeDtypeStruct((landmarks, length), jnp.bfloat16),
-        compiler_params=pltpu.CompilerParams(vmem_limit_bytes=VMEM_BYTES),
+        compiler_params=pltpu.CompilerParams(vmem_limit_bytes=28 * MIB),
         name="place",
     )((jnp.stack(owners) * capacity).astype(jnp.int32), slots, *chunks, *extra)
 
@@ -442,26 +465,50 @@
     chip_rows = 2 * rows_dev
     landmark_fps = landmarks_everywhere(fingerprints, landmark_index)
     norms = sq_norms(landmark_fps)
-    target_sum = jnp.sum(tgs.astype(jnp.float32), axis=0, keepdims=True)
-    ct, mean, rhs_part, first_rest, lead, column, weight = stage(
-        jnp.reshape(core, (1,)), landmark_fps, fps, sq_norms(fps)[None, :], tgs
-    )
-
-    def reduced_pieces(masks):
+    ct, rhs_part, rest_rows, message, lead, column = stage(
+        jnp.reshape(core, (1,)), landmark_fps, fps, sq_norms(fps)[None, :], tgs.T
+    )
+    panel_cols, other_cols = slice(0, width), slice(width, landmarks)
+    f32, bf16 = jnp.float32, jnp.bfloat16
+
+    def gram_rows(masks, ct):
         starts = []
         for m in masks:
             there = ((layer ^ m) * 4 + core) * share
             starts += [there + row * 2 * share, there + (1 - row) * 2 * share]
-        got = pieces(starts, ct, lead, column, rhs_part)
-        return [(got[2 * p], got[2 * p + 1]) for p in range(len(masks))]
-
-    def row_sum(pair):
-        return pair[0] + send(pair[1], ROW).astype(jnp.float32)
-
-    stats = gather_chips(jnp.concatenate([mean, target_sum, lead, weight], axis=1))
-    means, target_sums = stats[:, :landmarks], stats[:, landmarks : landmarks + LANES]
-    leads = stats[:, landmarks + LANES : 2 * landmarks + LANES]
-    lead_weights = stats[:, 2 * landmarks + LANES : 2 * landmarks + LANES + 1]
+        return pieces(starts, ct, lead, column, rhs_part)
+
+    mine_32, theirs_32 = gram_rows((3, 2), ct)
+    other_32 = send(theirs_32, ROW)
+
+    def halves(x, high):
+        return lax.dynamic_slice_in_dim(x, high * (x.shape[0] // 2), x.shape[0] // 2, 0)
+
+    near, far = layer % 2, layer // 2
+    message_row = send(message, ROW)
+    other_near = send(halves(rest_rows, 1 - near), NEAR)
+
+    mine_10, theirs_10 = gram_rows((1, 0), ct)
+    other_10 = send(theirs_10, ROW)
+
+    def merge(x, y):
+        return jnp.concatenate([x[:share] + y[:share], x[share:], y[share:]], axis=0)
+
+    message = merge(message, after(message_row, mine_10))
+    message = merge(message, send(message, NEAR))
+    part = halves(rest_rows, near).astype(f32) + other_near.astype(f32)
+    part_bf = part.astype(bf16)
+    message_far = send(message, FAR)
+    part = halves(part, far) + send(halves(part_bf, 1 - far), FAR).astype(f32)
+    part = part.astype(bf16)
+    message = merge(message, message_far)
+    part = (part.astype(f32) + send(part, ROW).astype(f32)).astype(bf16)
+    part_far = send(part, FAR)
+
+    stats = message[share:].reshape(8, STATS, TILE)
+    means = stats[:, :8].reshape(8, landmarks)
+    leads = stats[:, 8:16].reshape(8, landmarks)
+    lead_weights, target_sums = stats[:, 16, :1], stats[:, 16, LANES:]
     shift = means - jnp.mean(means, axis=0, keepdims=True)
     left_terms = jnp.concatenate([shift * chip_rows, leads], axis=0)
     right_terms = jnp.concatenate([shift, leads * lead_weights], axis=0)
@@ -473,55 +520,39 @@
             rows_fps, landmark_fps[cols], norms[cols]
         )
 
+    def in_order(x, other, high):
+        size = x.shape[0]
+        return lax.dynamic_slice_in_dim(
+            jnp.concatenate([x, other, x], axis=0), high * size, 2 * size, 0
+        )
+
     def both_blocks(block):
-        other = send(block, CORE)
-        return lax.dynamic_slice_in_dim(
-            jnp.concatenate([block, other, block], axis=0), core * share, 2 * share, 0
-        )
-
-    panel_cols, other_cols = slice(0, width), slice(width, landmarks)
-    corner = first_rest[:, panel_cols]
-    corner = corner.astype(jnp.float32) + send(corner, ROW).astype(jnp.float32)
-    half = corner.astype(jnp.bfloat16)
-    for s in (2, 1, 3):
-        corner = corner + send(half, rotate(s)).astype(jnp.float32)
-    corner = both_blocks(system_part(corner, core * share, panel_cols))
-    state = jnp.concatenate([corner, jnp.eye(width, dtype=jnp.float32)], axis=1)
-    for b in range(0, width // CHOL, 2):
-        state = eliminate_blocks(state, (b, b + 1))
-
-    first_rest = first_rest[:, other_cols]
-    quarter = share // 4
-
-    def quarter_of(q):
-        return lax.dynamic_slice_in_dim(first_rest, (q % 4) * quarter, quarter, 0)
-
-    part = quarter_of(layer).astype(jnp.float32)
-    for s in (2, 1, 3):
-        part = part + send(quarter_of(layer + s), rotate(s)).astype(jnp.float32)
-    part = part.astype(jnp.bfloat16)
-    part = part.astype(jnp.float32) + send(part, ROW).astype(jnp.float32)
-    part = part.astype(jnp.bfloat16)
-    quarters = jnp.zeros((4,) + part.shape, jnp.bfloat16)
-    quarters = lax.dynamic_update_index_in_dim(quarters, part, layer, 0)
-    for s in (2, 1, 3):
-        quarters = lax.dynamic_update_index_in_dim(
-            quarters, send(part, rotate(s)), (layer + 4 - s) % 4, 0
-        )
-    block = system_part(
-        quarters.reshape(share, landmarks - width).astype(jnp.float32), core * share, other_cols
-    )
-    panel_rows = jnp.concatenate([corner, both_blocks(block)], axis=1)
+        return in_order(block, send(block, CORE), core)
+
+    corner = both_blocks(system_part(message[:share], core * share, panel_cols))
+    state = jnp.concatenate([corner, jnp.eye(width, dtype=f32)], axis=1)
+
+    sums_32 = mine_32 + other_32.astype(f32)
+    three = sums_32[:share].astype(bf16)
+    other_two = send(three, NEAR)
+    calls = [(b, b + 1) for b in range(0, width // CHOL, 2)]
+    state = eliminate_blocks(after(state, three, part_far), calls[0])
+    part = in_order(part, part_far, far)
+    part_near = send(part, NEAR)
+    two = (sums_32[share:] + other_two.astype(f32)).astype(bf16)
+    state = eliminate_blocks(after(state, two, part), calls[1])
+    got_two = send(two, FAR)
+    sums_10 = mine_10 + other_10.astype(f32)
+    one = sums_10[:share].astype(bf16)
+    got_one = send(one, NEAR)
+    state = eliminate_blocks(after(state, one), calls[2])
+    part = in_order(part, part_near, near)
+    block = both_blocks(system_part(part.astype(f32), core * share, other_cols))
+    state = eliminate_blocks(after(state, block), calls[3])
+    panel_rows = jnp.concatenate([corner, block], axis=1)
     factor = exact_dot(state[:, width:], panel_rows)
 
-    three, two = reduced_pieces((3, 2))
-    one, zero = reduced_pieces((1, 0))
-    three = row_sum(three).astype(jnp.bfloat16)
-    two = row_sum(two) + send(three, NEAR).astype(jnp.float32)
-    two = two.astype(jnp.bfloat16)
-    one = row_sum(one).astype(jnp.bfloat16)
-    own = row_sum(zero) + send(one, NEAR).astype(jnp.float32) + send(two, FAR).astype(jnp.float32)
-
+    own = sums_10[share:] + got_one.astype(f32) + got_two.astype(f32)
     start = position * share
     rest = system_part(own[:, : landmarks - width], start, other_cols)
     own_shift = lax.dynamic_slice_in_dim(shift, start, share, 1)

time: 301 us -> 238 us (0.79)
  Pallas kernels: 108 us -> 83 us
  waiting for transfers between devices: 96.6 us -> 74.1 us
  starting transfers between devices: 37.9 us -> 28.7 us
  other arithmetic: 23.1 us -> 14.6 us
  local copies, waits for them, and re-layouts: 17.2 us -> 20.7 us
    ppermute x41 -> x32, waiting for transfers between devices: 96.6 us -> 74.1 us  [send(): return lax.ppermute(x, 'dp', perm)]
    ppermute x41 -> x32, starting transfers between devices: 37.9 us -> 28.7 us  [send(): return lax.ppermute(x, 'dp', perm)]
    unnamed x59 -> x49, local copies, waits for them, and re-layouts: 5.34 us -> 14.2 us
    pallas_call x2, Pallas kernels: 18.8 us -> 10.9 us  [pieces(): pl.pallas_call(pieces_body, in_specs=[pl.BlockSpec(memory_space=pltpu.SME...]
    pallas_call x3, Pallas kernels: 24.8 us -> 17 us  [place(): pl.pallas_call(functools.partial(place_body, len(chunks)), grid=(landmark...]
    pallas_call x4, Pallas kernels: 34.5 us -> 27 us  [eliminate_blocks(): pl.pallas_call(functools.partial(factor_body, blocks), in_specs=vmem(1),...]
    convert_element_type x7 -> x4, other arithmetic: 8.76 us -> 2.01 us  [the longest x1 0.86 us: local_16(): two = (sums_32[share:] + other_two.astype(f32)).astype(bf16)]
    add x1 -> x6, other arithmetic: 1.55 us -> 6.57 us  [the longest x1 1.56 us: local_16(): sums_32 = mine_32 + other_32.astype(f32)]
  transfers between devices with their start and end apart: 41 -> 32, of which waited for: 15 -> 10; matrix products, arithmetic and copies ran while one was open for 15% -> 15% of each run, Pallas kernels for 21% -> 22%
where the time goes in v4:
time: 238 us
  Pallas kernels  83 us (35%)
  waiting for transfers between devices  74.1 us (31%)
  starting transfers between devices  28.7 us (12%)
  local copies, waits for them, and re-layouts  20.7 us (9%)
  matrix products  15.3 us (6%)
  other arithmetic  14.6 us (6%)
    ppermute x32, waiting for transfers between devices, send(): return lax.ppermute(x, 'dp', perm)  74.1 us
    ppermute x32, starting transfers between devices, send(): return lax.ppermute(x, 'dp', perm)  28.7 us
    pallas_call x4, Pallas kernels, eliminate_blocks(): pl.pallas_call(functools.partial(factor_body, blocks), in_specs=vmem(1),...  27 us
    pallas_call x1, Pallas kernels, stage(): pl.pallas_call(stage_body, grid_spec=pltpu.PrefetchScalarGridSpec(num_sca...  23.6 us
    pallas_call x3, Pallas kernels, place(): pl.pallas_call(functools.partial(place_body, len(chunks)), grid=(landmark...  17 us
    unnamed x49, local copies, waits for them, and re-layouts  14.2 us
    pallas_call x2, Pallas kernels, pieces(): pl.pallas_call(pieces_body, in_specs=[pl.BlockSpec(memory_space=pltpu.SME...  10.9 us
    dot_general x5, matrix products, highest(): lax.dot_general(a, b, (((0,), (0,)), ((), ())), precision=lax.Precision.H...  7.95 us
  transfers between devices with their start and end apart: 32, of which 10 were waited for; matrix products, arithmetic and copies ran while one was open for 15% of the time, Pallas kernels for 22%

profile of v4, /device:TPU:0, one launch (start us, length us, event | category | flops | bytes accessed | tf_op | source)
XLA Modules:
  0.0 237.5 jit_solution(12925529725189361772)
XLA Ops:
  1.3 4.4 %pack.1 = (bf16[256,512]{1,0:T(8,128)(2,1)}, f32[2048,128]{1,0:T(8,128)S(1)}) custom-call(s32[1]{0:T(128)} %bitcast.7.at_ref, s32[1,2048]{1,0:T(1,128)S(1)} %bitcast.48, bf16[1024,512]{1,0:T(8,128)(2,1)} %fps_ref.1), custom_call_target="tpu_custom_call" | custom-call | tf_op jit(solution)/shard_map/pack/pallas_call | solution.py:375
  5.7 4.0 %collective-permute-start = (bf16[256,512]{1,0:T(8,128)(2,1)}, bf16[256,512]{1,0:T(8,128)(2,1)S(1)}, u32[]{:S(2)}, u32[]{:S(2)}) collective-permute-start(bf16[256,512]{1,0:T(8,128)(2,1)} %get-tuple-element.21.refs_0_), channel_id=1, source_target_pairs={{0,8},{1,9},{2,10},{3,11},{4,12},{5,13},{6,14},{7,15},{8,0},{9,1},... | collective-permute-start | bytes 786440 | tf_op jit(solution)/shard_map/ppermute | solution.py:95
  16.2 5.8 %collective-permute-done.refs_6_ = bf16[256,512]{1,0:T(8,128)(2,1)S(1)} collective-permute-done((bf16[256,512]{1,0:T(8,128)(2,1)}, bf16[256,512]{1,0:T(8,128)(2,1)S(1)}, u32[]{:S(2)}, u32[]{:S(2)}) %collective-permute-start) | collective-permute-done | bytes 262176 | tf_op jit(solution)/shard_map/ppermute | solution.py:95
  26.7 4.2 %collective-permute-done.1.refs_2_ = bf16[256,512]{1,0:T(8,128)(2,1)S(1)} collective-permute-done((bf16[256,512]{1,0:T(8,128)(2,1)}, bf16[256,512]{1,0:T(8,128)(2,1)S(1)}, u32[]{:S(2)}, u32[]{:S(2)}) %collective-permute-start.1) | collective-permute-done | bytes 262176 | tf_op jit(solution)/shard_map/ppermute | solution.py:95
  33.5 3.8 %collective-permute-done.8.refs_4_ = bf16[256,512]{1,0:T(8,128)(2,1)} collective-permute-done((bf16[256,512]{1,0:T(8,128)(2,1)}, bf16[256,512]{1,0:T(8,128)(2,1)}, u32[]{:S(2)}, u32[]{:S(2)}) %collective-permute-start.8) | collective-permute-done | bytes 262176 | tf_op jit(solution)/shard_map/ppermute | solution.py:95
  41.6 7.3 %place.3.refs_6_ = bf16[2048,512]{1,0:T(8,128)(2,1)S(1)} custom-call(s32[8]{0:T(128)S(1)} %broadcast_multiply_fusion.2.base_ref, f32[2048,128]{1,0:T(8,128)S(1)} %get-tuple-element.20.slots_ref, bf16[256,512]{1,0:T(8,128)(2,1)} %get-tuple-element.21.refs_0_, bf16[256,512]{1,0:T(8,128)(2,1)} %collective-permute-done.10.refs_1_, ...), custom_call_target="tpu_custom_call" | custom-call | tf_op jit(solution)/shard_map/place/pallas_call | solution.py:415
  49.4 6.0 %place.4.refs_2_ = bf16[2048,512]{1,0:T(8,128)(2,1)S(1)} custom-call(s32[6]{0:T(128)S(1)} %broadcast_multiply_fusion.3.base_ref, f32[2048,128]{1,0:T(8,128)S(1)} %get-tuple-element.20.slots_ref, bf16[256,512]{1,0:T(8,128)(2,1)} %collective-permute-done.5.refs_0_, bf16[256,512]{1,0:T(8,128)(2,1)} %collective-permute-done.6.refs_1_, ...), custom_call_target="tpu_custom_call" | custom-call | tf_op jit(solution)/shard_map/place/pallas_call | solution.py:415
  58.1 3.7 %place.5.land_ref = bf16[2048,512]{1,0:T(8,128)(2,1)S(1)} custom-call(s32[2]{0:T(128)S(1)} %add_multiply_fusion.base_ref, f32[2048,128]{1,0:T(8,128)S(1)} %get-tuple-element.20.slots_ref, bf16[256,512]{1,0:T(8,128)(2,1)} %collective-permute-done.2.refs_0_, bf16[256,512]{1,0:T(8,128)(2,1)S(1)} %collective-permute-done.3.refs_1_, ...), custom_call_target="tpu_custom_call" | custom-call | tf_op jit(solution)/shard_map/place/pallas_call | solution.py:415
  61.8 23.6 %stage.1 = (bf16[2048,2048]{1,0:T(8,128)(2,1)S(1)}, f32[8,128,128]{2,1,0:T(8,128)S(1)}, bf16[128,1792]{1,0:T(8,128)(2,1)S(1)}, f32[152,256]{1,0:T(8,128)S(1)}, f...) custom-call(s32[1]{0:T(128)} %bitcast.4.core_ref, bf16[2048,512]{1,0:T(8,128)(2,1)S(1)} %place.5.land_ref, ...), custom_call_target="tpu_custom_call" | custom-call | tf_op jit(solution)/shard_map/stage/pallas_call | solution.py:213
  86.5 5.5 %pieces.2 = (f32[256,1920]{1,0:T(8,128)S(1)}, bf16[256,1920]{1,0:T(8,128)(2,1)}) custom-call(s32[4]{0:T(128)S(1)} %get-tuple-element.47.at_ref, bf16[2048,2048]{1,0:T(8,128)(2,1)S(1)} %get-tuple-element.22.ct_ref, f32[1,2048]{1,0:T(1,128)S(1)} %get-tuple-element.23.lead_ref, f32[2048,128]{1,0:T(8,128)S(1)} %get-tuple-element.24.column_ref, ...), custom_call_target="tpu_custom_call" | custom-call | tf_op jit(solution)/shard_map/pieces/pallas_call | solution.py:271
  94.8 5.5 %pieces.3 = (f32[256,1920]{1,0:T(8,128)S(1)}, bf16[256,1920]{1,0:T(8,128)(2,1)}) custom-call(s32[4]{0:T(128)S(1)} %get-tuple-element.48.at_ref, bf16[2048,2048]{1,0:T(8,128)(2,1)S(1)} %get-tuple-element.22.ct_ref, f32[1,2048]{1,0:T(1,128)S(1)} %get-tuple-element.23.lead_ref, f32[2048,128]{1,0:T(8,128)S(1)} %get-tuple-element.24.column_ref, ...), custom_call_target="tpu_custom_call" | custom-call | tf_op jit(solution)/shard_map/pieces/pallas_call | solution.py:271
  110.6 5.5 %collective-permute-done.26 = bf16[64,1792]{0,1:T(8,128)(2,1)} collective-permute-done((bf16[64,1792]{0,1:T(8,128)(2,1)S(1)}, bf16[64,1792]{0,1:T(8,128)(2,1)}, u32[]{:S(2)}, u32[]{:S(2)}) %collective-permute-start.26) | collective-permute-done | bytes 229408 | tf_op jit(solution)/shard_map/ppermute | solution.py:95
  117.7 3.3 %collective-permute-start.27 = (bf16[32,1792]{0,1:T(8,128)(2,1)S(1)}, bf16[32,1792]{0,1:T(8,128)(2,1)S(1)}, u32[]{:S(2)}, u32[]{:S(2)}) collective-permute-start(bf16[32,1792]{0,1:T(8,128)(2,1)S(1)} %dynamic-slice_convert_fusion), channel_id=1, source_target_pairs={{0,8},{1,9},{2,10},{3,11},{4,12},{5,13},{6,14},{7,15},{8,0},{9,1},... | collective-permute-start | bytes 344072 | tf_op jit(solution)/shard_map/ppermute | solution.py:95
  121.1 17.0 %collective-permute-done.27 = bf16[32,1792]{0,1:T(8,128)(2,1)S(1)} collective-permute-done((bf16[32,1792]{0,1:T(8,128)(2,1)S(1)}, bf16[32,1792]{0,1:T(8,128)(2,1)S(1)}, u32[]{:S(2)}, u32[]{:S(2)}) %collective-permute-start.27) | collective-permute-done | bytes 114720 | tf_op jit(solution)/shard_map/ppermute | solution.py:95
  140.1 8.5 %collective-permute-done.28 = bf16[32,1792]{0,1:T(8,128)(2,1)S(1)} collective-permute-done((bf16[32,1792]{0,1:T(8,128)(2,1)S(1)}, bf16[32,1792]{0,1:T(8,128)(2,1)S(1)}, u32[]{:S(2)}, u32[]{:S(2)}) %collective-permute-start.28) | collective-permute-done | bytes 114720 | tf_op jit(solution)/shard_map/ppermute | solution.py:95
  148.6 2.7 %collective-permute-start.29 = (bf16[32,1792]{0,1:T(8,128)(2,1)S(1)}, bf16[32,1792]{0,1:T(8,128)(2,1)}, u32[]{:S(2)}, u32[]{:S(2)}) collective-permute-start(bf16[32,1792]{0,1:T(8,128)(2,1)S(1)} %add_convert_fusion), channel_id=1, source_target_pairs={{0,8},{1,9},{2,10},{3,11},{4,12},{5,13},{6,14},{7,15},{8,0},{9,1},... | collective-permute-start | bytes 344072 | tf_op jit(solution)/shard_map/ppermute | solution.py:95
  158.3 12.6 %collective-permute-done.29 = bf16[32,1792]{0,1:T(8,128)(2,1)} collective-permute-done((bf16[32,1792]{0,1:T(8,128)(2,1)S(1)}, bf16[32,1792]{0,1:T(8,128)(2,1)}, u32[]{:S(2)}, u32[]{:S(2)}) %collective-permute-start.29) | collective-permute-done | bytes 114720 | tf_op jit(solution)/shard_map/ppermute | solution.py:95
  170.8 2.7 %dynamic-slice_maximum_fusion = bf16[64,1792]{0,1:T(8,128)(2,1)} fusion(s32[]{:T(128)S(6)} %select_n.73, bf16[32,1792]{0,1:T(8,128)(2,1)S(1)} %add_convert_fusion, bf16[32,1792]{0,1:T(8,128)(2,1)} %collective-permute-done.29), kind=kLoop, calls=%fused_computation.41 | loop fusion | flops 688128 | bytes 458756 | tf_op jit(solution)/shard_map/concatenate | solution.py:526
  173.9 12.2 %collective-permute-done.30 = bf16[64,1792]{0,1:T(8,128)(2,1)} collective-permute-done((bf16[64,1792]{0,1:T(8,128)(2,1)}, bf16[64,1792]{0,1:T(8,128)(2,1)}, u32[]{:S(2)}, u32[]{:S(2)}) %collective-permute-start.30) | collective-permute-done | bytes 229408 | tf_op jit(solution)/shard_map/ppermute | solution.py:95
  186.2 2.6 %fusion.11 = f32[128,1792]{0,1:T(8,128)S(1)} fusion(bf16[2048,512]{1,0:T(8,128)(2,1)S(1)} %place.5.land_ref, f32[128,1792]{0,1:T(8,128)} %fusion.39, s32[]{:T(128)S(6)} %select_n.74, bf16[64,1792]{0,1:T(8,128)(2,1)} %dynamic-slice_maximum_fusion, bf16[64,1792]{0,1:T(8,128)(2,1)} %collective-permute-done.30, f32[1792]{0:T(1024)S(1)} %slice.125, ...), kind=kOutput, calls=%fused_computation.20 | convolution fusion | flops 237633536 | bytes 4268552 | tf_op jit(solution)/shard_map/dot_general | solution.py:23
  195.5 7.1 %factor.4.state_ref = f32[256,512]{1,0:T(8,128)S(1)} custom-call(f32[256,512]{1,0:T(8,128)S(1)} %pad_maximum_fusion.2.state_ref), custom_call_target="tpu_custom_call" | custom-call | tf_op jit(solution)/shard_map/factor/pallas_call | solution.py:328
  206.4 6.8 %factor.5.state_ref = f32[256,512]{1,0:T(8,128)S(1)} custom-call(f32[256,512]{1,0:T(8,128)S(1)} %factor.4.state_ref), custom_call_target="tpu_custom_call" | custom-call | tf_op jit(solution)/shard_map/factor/pallas_call | solution.py:328
  213.2 6.8 %factor.6.state_ref = f32[256,512]{1,0:T(8,128)S(1)} custom-call(f32[256,512]{1,0:T(8,128)S(1)} %factor.5.state_ref), custom_call_target="tpu_custom_call" | custom-call | tf_op jit(solution)/shard_map/factor/pallas_call | solution.py:328
  220.4 6.3 %factor.7 = f32[256,512]{1,0:T(8,128)S(1)} custom-call(f32[256,512]{1,0:T(8,128)S(1)} %factor.6.state_ref), custom_call_target="tpu_custom_call" | custom-call | tf_op jit(solution)/shard_map/factor/pallas_call | solution.py:328
  (160 shorter events, 68.4 us)
Async XLA Ops:
  5.7 16.3 %collective-permute-start = (bf16[256,512]{1,0:T(8,128)(2,1)}, bf16[256,512]{1,0:T(8,128)(2,1)S(1)}, u32[]{:S(2)}, u32[]{:S(2)}) collective-permute-start(bf16[256,512]{1,0:T(8,128)(2,1)} %get-tuple-element.21.refs_0_), channel_id=1, source_target_pairs={{0,8},{1,9},{2,10},{3,11},{4,12},{5,13},{6,14},{7,15},{8,0},{9,1},... | collective-permute-start | bytes 786440 | tf_op jit(solution)/shard_map/ppermute | solution.py:95
  9.8 13.0 %collective-permute-start.4 = (bf16[256,512]{1,0:T(8,128)(2,1)}, bf16[256,512]{1,0:T(8,128)(2,1)}, u32[]{:S(2)}, u32[]{:S(2)}) collective-permute-start(bf16[256,512]{1,0:T(8,128)(2,1)} %get-tuple-element.21.refs_0_), channel_id=1, source_target_pairs={{0,4},{1,5},{2,6},{3,7},{4,0},{5,1},{6,2},{7,3},{8,12},{9,13},{10,... | collective-permute-start | bytes 786440 | tf_op jit(solution)/shard_map/ppermute | solution.py:95
  11.3 12.4 %collective-permute-start.10 = (bf16[256,512]{1,0:T(8,128)(2,1)}, bf16[256,512]{1,0:T(8,128)(2,1)}, u32[]{:S(2)}, u32[]{:S(2)}) collective-permute-start(bf16[256,512]{1,0:T(8,128)(2,1)} %get-tuple-element.21.refs_0_), channel_id=1, source_target_pairs={{0,1},{1,0},{2,3},{3,2},{4,5},{5,4},{6,7},{7,6},{8,9},{9,8},{10,11... | collective-permute-start | bytes 786440 | tf_op jit(solution)/shard_map/ppermute | solution.py:95
  11.3 14.8 %collective-permute-start.11 = (bf16[256,512]{1,0:T(8,128)(2,1)}, bf16[256,512]{1,0:T(8,128)(2,1)}, u32[]{:S(2)}, u32[]{:S(2)}) collective-permute-start(bf16[256,512]{1,0:T(8,128)(2,1)} %get-tuple-element.21.refs_0_), channel_id=1, source_target_pairs={{0,2},{1,3},{2,0},{3,1},{4,6},{5,7},{6,4},{7,5},{8,10},{9,11},{10,... | collective-permute-start | bytes 786440 | tf_op jit(solution)/shard_map/ppermute | solution.py:95
  12.9 42.6 %collective-permute-start.15 = (bf16[1024,512]{1,0:T(8,128)(2,1)}, bf16[1024,512]{1,0:T(8,128)(2,1)}, u32[]{:S(2)}, u32[]{:S(2)}) collective-permute-start(bf16[1024,512]{1,0:T(8,128)(2,1)} %fps_ref.1), channel_id=1, source_target_pairs={{0,1},{1,0},{2,3},{3,2},{4,5},{5,4},{6,7},{7,6},{8,9},{9,8},{10,11... | collective-permute-start | bytes 3145736 | tf_op jit(solution)/shard_map/ppermute | solution.py:95
  26.1 11.2 %collective-permute-start.8 = (bf16[256,512]{1,0:T(8,128)(2,1)}, bf16[256,512]{1,0:T(8,128)(2,1)}, u32[]{:S(2)}, u32[]{:S(2)}) collective-permute-start(bf16[256,512]{1,0:T(8,128)(2,1)} %copy-done.6), channel_id=1, source_target_pairs={{0,2},{1,3},{2,0},{3,1},{4,6},{5,7},{6,4},{7,5},{8,10},{9,11},{10,... | collective-permute-start | bytes 786440 | tf_op jit(solution)/shard_map/ppermute | solution.py:95
  26.7 12.2 %collective-permute-start.13 = (bf16[256,512]{1,0:T(8,128)(2,1)}, bf16[256,512]{1,0:T(8,128)(2,1)}, u32[]{:S(2)}, u32[]{:S(2)}) collective-permute-start(bf16[256,512]{1,0:T(8,128)(2,1)} %collective-permute-done.4.refs_4_), channel_id=1, source_target_pairs={{0,1},{1,0},{2,3},{3,2},{4,5},{5,4},{6,7},{7,6},{8,9},{9,8},{10,11... | collective-permute-start | bytes 786440 | tf_op jit(solution)/shard_map/ppermute | solution.py:95
  37.3 11.5 %collective-permute-start.2 = (bf16[256,512]{1,0:T(8,128)(2,1)S(1)}, bf16[256,512]{1,0:T(8,128)(2,1)}, u32[]{:S(2)}, u32[]{:S(2)}) collective-permute-start(bf16[256,512]{1,0:T(8,128)(2,1)S(1)} %collective-permute-done.1.refs_2_), channel_id=1, source_target_pairs={{0,2},{1,3},{2,0},{3,1},{4,6},{5,7},{6,4},{7,5},{8,10},{9,11},{10,... | collective-permute-start | bytes 786440 | tf_op jit(solution)/shard_map/ppermute | solution.py:95
  38.9 10.5 %collective-permute-start.7 = (bf16[256,512]{1,0:T(8,128)(2,1)S(1)}, bf16[256,512]{1,0:T(8,128)(2,1)}, u32[]{:S(2)}, u32[]{:S(2)}) collective-permute-start(bf16[256,512]{1,0:T(8,128)(2,1)S(1)} %collective-permute-done.1.refs_2_), channel_id=1, source_target_pairs={{0,1},{1,0},{2,3},{3,2},{4,5},{5,4},{6,7},{7,6},{8,9},{9,8},{10,11... | collective-permute-start | bytes 786440 | tf_op jit(solution)/shard_map/ppermute | solution.py:95
  38.9 10.5 %collective-permute-start.6 = (bf16[256,512]{1,0:T(8,128)(2,1)}, bf16[256,512]{1,0:T(8,128)(2,1)}, u32[]{:S(2)}, u32[]{:S(2)}) collective-permute-start(bf16[256,512]{1,0:T(8,128)(2,1)} %collective-permute-done.5.refs_0_), channel_id=1, source_target_pairs={{0,1},{1,0},{2,3},{3,2},{4,5},{5,4},{6,7},{7,6},{8,9},{9,8},{10,11... | collective-permute-start | bytes 786440 | tf_op jit(solution)/shard_map/ppermute | solution.py:95
  85.4 22.5 %collective-permute-start.22 = (f32[152,256]{1,0:T(8,128)S(1)}, f32[152,256]{1,0:T(8,128)}, u32[]{:S(2)}, u32[]{:S(2)}) collective-permute-start(f32[152,256]{1,0:T(8,128)S(1)} %get-tuple-element.30), channel_id=1, source_target_pairs={{0,2},{1,3},{2,0},{3,1},{4,6},{5,7},{6,4},{7,5},{8,10},{9,11},{10,... | collective-permute-start | bytes 466952 | tf_op jit(solution)/shard_map/ppermute | solution.py:95
  93.3 97.6 %collective-permute-start.17 = (bf16[256,1920]{1,0:T(8,128)(2,1)}, bf16[256,1920]{1,0:T(8,128)(2,1)}, u32[]{:S(2)}, u32[]{:S(2)}) collective-permute-start(bf16[256,1920]{1,0:T(8,128)(2,1)} %get-tuple-element.27), channel_id=1, source_target_pairs={{0,2},{1,3},{2,0},{3,1},{4,6},{5,7},{6,4},{7,5},{8,10},{9,11},{10,... | collective-permute-start | bytes 2949128 | tf_op jit(solution)/shard_map/ppermute | solution.py:95
  101.5 87.3 %collective-permute-start.19 = (bf16[256,1920]{1,0:T(8,128)(2,1)}, bf16[256,1920]{1,0:T(8,128)(2,1)}, u32[]{:S(2)}, u32[]{:S(2)}) collective-permute-start(bf16[256,1920]{1,0:T(8,128)(2,1)} %get-tuple-element.29), channel_id=1, source_target_pairs={{0,2},{1,3},{2,0},{3,1},{4,6},{5,7},{6,4},{7,5},{8,10},{9,11},{10,... | collective-permute-start | bytes 2949128 | tf_op jit(solution)/shard_map/ppermute | solution.py:95
  102.5 13.6 %collective-permute-start.26 = (bf16[64,1792]{0,1:T(8,128)(2,1)S(1)}, bf16[64,1792]{0,1:T(8,128)(2,1)}, u32[]{:S(2)}, u32[]{:S(2)}) collective-permute-start(bf16[64,1792]{0,1:T(8,128)(2,1)S(1)} %constant_dynamic-slice_fusion), channel_id=1, source_target_pairs={{0,4},{1,5},{2,6},{3,7},{4,0},{5,1},{6,2},{7,3},{8,12},{9,13},{10,... | collective-permute-start | bytes 688136 | tf_op jit(solution)/shard_map/ppermute | solution.py:95
  109.6 11.4 %collective-permute-start.23 = (f32[176,256]{1,0:T(8,128)S(1)}, f32[176,256]{1,0:T(8,128)S(1)}, u32[]{:S(2)}, u32[]{:S(2)}) collective-permute-start(f32[176,256]{1,0:T(8,128)S(1)} %pad_maximum_fusion.5), channel_id=1, source_target_pairs={{0,4},{1,5},{2,6},{3,7},{4,0},{5,1},{6,2},{7,3},{8,12},{9,13},{10,... | collective-permute-start | bytes 540680 | tf_op jit(solution)/shard_map/ppermute | solution.py:95
  117.7 20.4 %collective-permute-start.27 = (bf16[32,1792]{0,1:T(8,128)(2,1)S(1)}, bf16[32,1792]{0,1:T(8,128)(2,1)S(1)}, u32[]{:S(2)}, u32[]{:S(2)}) collective-permute-start(bf16[32,1792]{0,1:T(8,128)(2,1)S(1)} %dynamic-slice_convert_fusion), channel_id=1, source_target_pairs={{0,8},{1,9},{2,10},{3,11},{4,12},{5,13},{6,14},{7,15},{8,0},{9,1},... | collective-permute-start | bytes 344072 | tf_op jit(solution)/shard_map/ppermute | solution.py:95
  140.0 11.3 %collective-permute-start.24 = (f32[224,256]{1,0:T(8,128)S(1)}, f32[224,256]{1,0:T(8,128)S(1)}, u32[]{:S(2)}, u32[]{:S(2)}) collective-permute-start(f32[224,256]{1,0:T(8,128)S(1)} %pad_maximum_fusion.3), channel_id=1, source_target_pairs={{0,8},{1,9},{2,10},{3,11},{4,12},{5,13},{6,14},{7,15},{8,0},{9,1},... | collective-permute-start | bytes 688136 | tf_op jit(solution)/shard_map/ppermute | solution.py:95
  148.6 22.2 %collective-permute-start.29 = (bf16[32,1792]{0,1:T(8,128)(2,1)S(1)}, bf16[32,1792]{0,1:T(8,128)(2,1)}, u32[]{:S(2)}, u32[]{:S(2)}) collective-permute-start(bf16[32,1792]{0,1:T(8,128)(2,1)S(1)} %add_convert_fusion), channel_id=1, source_target_pairs={{0,8},{1,9},{2,10},{3,11},{4,12},{5,13},{6,14},{7,15},{8,0},{9,1},... | collective-permute-start | bytes 344072 | tf_op jit(solution)/shard_map/ppermute | solution.py:95
  156.2 17.3 %collective-permute-start.25 = (f32[128,256]{1,0:T(8,128)S(1)}, f32[128,256]{1,0:T(8,128)S(1)}, u32[]{:S(2)}, u32[]{:S(2)}) collective-permute-start(f32[128,256]{1,0:T(8,128)S(1)} %fusion.28), channel_id=1, source_target_pairs={{0,1},{1,0},{2,3},{3,2},{4,5},{5,4},{6,7},{7,6},{8,9},{9,8},{10,11... | collective-permute-start | bytes 393224 | tf_op jit(solution)/shard_map/ppermute | solution.py:95
  173.6 12.6 %collective-permute-start.30 = (bf16[64,1792]{0,1:T(8,128)(2,1)}, bf16[64,1792]{0,1:T(8,128)(2,1)}, u32[]{:S(2)}, u32[]{:S(2)}) collective-permute-start(bf16[64,1792]{0,1:T(8,128)(2,1)} %dynamic-slice_maximum_fusion), channel_id=1, source_target_pairs={{0,4},{1,5},{2,6},{3,7},{4,0},{5,1},{6,2},{7,3},{8,12},{9,13},{10,... | collective-permute-start | bytes 688136 | tf_op jit(solution)/shard_map/ppermute | solution.py:95
  188.7 31.3 %collective-permute-start.31 = (f32[128,1792]{0,1:T(8,128)S(1)}, f32[128,1792]{0,1:T(8,128)S(1)}, u32[]{:S(2)}, u32[]{:S(2)}) collective-permute-start(f32[128,1792]{0,1:T(8,128)S(1)} %fusion.11), channel_id=1, source_target_pairs={{0,1},{1,0},{2,3},{3,2},{4,5},{5,4},{6,7},{7,6},{8,9},{9,8},{10,11... | collective-permute-start | bytes 2752520 | tf_op jit(solution)/shard_map/ppermute | solution.py:95
  190.5 14.1 %collective-permute-start.20 = (bf16[128,1920]{1,0:T(8,128)(2,1)S(1)}, bf16[128,1920]{1,0:T(8,128)(2,1)S(1)}, u32[]{:S(2)}, u32[]{:S(2)}) collective-permute-start(bf16[128,1920]{1,0:T(8,128)(2,1)S(1)} %slice.175), channel_id=1, source_target_pairs={{0,4},{1,5},{2,6},{3,7},{4,0},{5,1},{6,2},{7,3},{8,12},{9,13},{10,... | collective-permute-start | bytes 1474568 | tf_op jit(solution)/shard_map/ppermute | solution.py:95
  193.7 37.2 %collective-permute-start.18 = (bf16[128,1920]{1,0:T(8,128)(2,1)}, bf16[128,1920]{1,0:T(8,128)(2,1)}, u32[]{:S(2)}, u32[]{:S(2)}) collective-permute-start(bf16[128,1920]{1,0:T(8,128)(2,1)} %slice.176), channel_id=1, source_target_pairs={{0,4},{1,5},{2,6},{3,7},{4,0},{5,1},{6,2},{7,3},{8,12},{9,13},{10,... | collective-permute-start | bytes 1474568 | tf_op jit(solution)/shard_map/ppermute | solution.py:95
  205.4 25.5 %collective-permute-start.21 = (bf16[128,1920]{1,0:T(8,128)(2,1)}, bf16[128,1920]{1,0:T(8,128)(2,1)}, u32[]{:S(2)}, u32[]{:S(2)}) collective-permute-start(bf16[128,1920]{1,0:T(8,128)(2,1)} %fusion.14), channel_id=1, source_target_pairs={{0,8},{1,9},{2,10},{3,11},{4,12},{5,13},{6,14},{7,15},{8,0},{9,1},... | collective-permute-start | bytes 1474568 | tf_op jit(solution)/shard_map/ppermute | solution.py:95
  (30 other events, 183.2 us)

commit v5 on v4

--- a/solution.py
+++ b/solution.py
@@ -179,7 +179,7 @@
             if j < TILE // LANES:
                 message_ref[:LANES, cols] = rest
             else:
-                rest_ref[:, slice(cols.start - TILE, cols.stop - TILE)] = rest.astype(jnp.bfloat16)
+                rest_ref[:, slice(cols.start - TILE, cols.stop - TILE)] = rest
         message_ref[LANES:, :] = jnp.zeros((message_ref.shape[0] - LANES, TILE), jnp.float32)
         for j in range(lead.shape[1] // TILE):
             cols = slice(j * TILE, (j + 1) * TILE)
@@ -205,7 +205,7 @@
 
     outs = [
         ((steps, LANES, LANES), f32),
-        ((LANES, landmarks - TILE), bf16),
+        ((LANES, landmarks - TILE), f32),
         ((LANES + STATS, TILE), f32),
         ((1, landmarks), f32),
         ((landmarks, LANES), f32),
@@ -439,11 +439,14 @@
     held[10] = send(held[8], ROW)
     held[14] = send(held[12], ROW)
     result = None
-    for masks in ((0, 2, 4, 8), (6, 12, 10), (14,)):
+    for masks in ((0, 2, 4, 8), (6, 12, 10, 14)):
         owners, chunks = [], []
         for m in masks:
+            chunk = held[m]
+            if m in (6, 10, 14):
+                chunk = after(chunk, result)
             owners += [position ^ m, position ^ m ^ 1]
-            chunks += [held[m], send(held[m], CORE)]
+            chunks += [chunk, send(chunk, CORE)]
         result = place(owners, chunks, slots, result)
     return result
 
@@ -478,32 +481,24 @@
             starts += [there + row * 2 * share, there + (1 - row) * 2 * share]
         return pieces(starts, ct, lead, column, rhs_part)
 
+    def merge(x, y):
+        return jnp.concatenate([x[:share] + y[:share], x[share:], y[share:]], axis=0)
+
+    planes = [[2 * j + c for j in range(8)] for c in range(2)]
+    part = lax.psum(rest_rows, "dp", axis_index_groups=planes)
+    message_row = send(message, ROW)
     mine_32, theirs_32 = gram_rows((3, 2), ct)
     other_32 = send(theirs_32, ROW)
-
-    def halves(x, high):
-        return lax.dynamic_slice_in_dim(x, high * (x.shape[0] // 2), x.shape[0] // 2, 0)
-
-    near, far = layer % 2, layer // 2
-    message_row = send(message, ROW)
-    other_near = send(halves(rest_rows, 1 - near), NEAR)
-
-    mine_10, theirs_10 = gram_rows((1, 0), ct)
+    message = merge(message, after(message_row, mine_32))
+    message_near = send(message, NEAR)
+    mine_10, theirs_10 = gram_rows((1, 0), after(ct, message))
     other_10 = send(theirs_10, ROW)
-
-    def merge(x, y):
-        return jnp.concatenate([x[:share] + y[:share], x[share:], y[share:]], axis=0)
-
-    message = merge(message, after(message_row, mine_10))
-    message = merge(message, send(message, NEAR))
-    part = halves(rest_rows, near).astype(f32) + other_near.astype(f32)
-    part_bf = part.astype(bf16)
+    message = merge(message, after(message_near, mine_10))
     message_far = send(message, FAR)
-    part = halves(part, far) + send(halves(part_bf, 1 - far), FAR).astype(f32)
-    part = part.astype(bf16)
-    message = merge(message, message_far)
-    part = (part.astype(f32) + send(part, ROW).astype(f32)).astype(bf16)
-    part_far = send(part, FAR)
+    sums_32 = mine_32 + after(other_32, message).astype(f32)
+    three = sums_32[:share].astype(bf16)
+    other_two = send(three, NEAR)
+    message = merge(message, after(message_far, three))
 
     stats = message[share:].reshape(8, STATS, TILE)
     means = stats[:, :8].reshape(8, landmarks)
@@ -532,23 +527,17 @@
     corner = both_blocks(system_part(message[:share], core * share, panel_cols))
     state = jnp.concatenate([corner, jnp.eye(width, dtype=f32)], axis=1)
 
-    sums_32 = mine_32 + other_32.astype(f32)
-    three = sums_32[:share].astype(bf16)
-    other_two = send(three, NEAR)
     calls = [(b, b + 1) for b in range(0, width // CHOL, 2)]
-    state = eliminate_blocks(after(state, three, part_far), calls[0])
-    part = in_order(part, part_far, far)
-    part_near = send(part, NEAR)
-    two = (sums_32[share:] + other_two.astype(f32)).astype(bf16)
-    state = eliminate_blocks(after(state, two, part), calls[1])
+    state = eliminate_blocks(state, calls[0])
+    two = (sums_32[share:] + after(other_two, state).astype(f32)).astype(bf16)
     got_two = send(two, FAR)
-    sums_10 = mine_10 + other_10.astype(f32)
+    state = eliminate_blocks(after(state, two), calls[1])
+    sums_10 = mine_10 + after(other_10, state).astype(f32)
     one = sums_10[:share].astype(bf16)
     got_one = send(one, NEAR)
     state = eliminate_blocks(after(state, one), calls[2])
-    part = in_order(part, part_near, near)
-    block = both_blocks(system_part(part.astype(f32), core * share, other_cols))
-    state = eliminate_blocks(after(state, block), calls[3])
+    state = eliminate_blocks(state, calls[3])
+    block = both_blocks(system_part(after(part, state), core * share, other_cols))
     panel_rows = jnp.concatenate([corner, block], axis=1)
     factor = exact_dot(state[:, width:], panel_rows)
 

time: 238 us -> 213 us (0.89)
  waiting for transfers between devices: 74.1 us -> 38.6 us
  between operations: 1.19 us -> 14.6 us
  local copies, waits for them, and re-layouts: 20.7 us -> 24.7 us
  starting transfers between devices: 28.7 us -> 24.8 us
  Pallas kernels: 83 us -> 80.5 us
    ppermute x32 -> x27, waiting for transfers between devices: 74.1 us -> 23.3 us  [send(): return lax.ppermute(x, 'dp', perm)]
    psum x0 -> x1, waiting for transfers between devices: none -> 15.2 us  [local_16(): part = lax.psum(rest_rows, 'dp', axis_index_groups=planes)]
    ppermute x32 -> x27, starting transfers between devices: 28.7 us -> 24.8 us  [send(): return lax.ppermute(x, 'dp', perm)]
    concatenate x3 -> x2, other arithmetic: 3.29 us -> 0.54 us  [in_order(): jnp.concatenate([x, other, x], axis=0)]
    pallas_call x3 -> x2, Pallas kernels: 17 us -> 14.5 us  [place(): pl.pallas_call(functools.partial(place_body, len(chunks)), grid=(landmark...]
    unnamed x49 -> x55, local copies, waits for them, and re-layouts: 14.2 us -> 14 us
  transfers between devices with their start and end apart: 32 -> 28, of which waited for: 10 -> 8; matrix products, arithmetic and copies ran while one was open for 15% -> 17% of each run, Pallas kernels for 22% -> 22%
where the time goes in v5:
time: 213 us; the launch traced here: 211 us
  Pallas kernels  80.5 us (38%)
  waiting for transfers between devices  38.6 us (18%)
  starting transfers between devices  24.8 us (12%)
  local copies, waits for them, and re-layouts  24.7 us (12%)
  between operations  14.6 us (7%)
  matrix products  14.4 us (7%)
  other arithmetic  13.1 us (6%)
    pallas_call x4, Pallas kernels, eliminate_blocks(): pl.pallas_call(functools.partial(factor_body, blocks), in_specs=vmem(1),...  27.1 us
    ppermute x27, starting transfers between devices, send(): return lax.ppermute(x, 'dp', perm)  24.8 us
    pallas_call x1, Pallas kernels, stage(): pl.pallas_call(stage_body, grid_spec=pltpu.PrefetchScalarGridSpec(num_sca...  23.6 us
    ppermute x27, waiting for transfers between devices, send(): return lax.ppermute(x, 'dp', perm)  23.3 us
    psum x1, waiting for transfers between devices, local_16(): part = lax.psum(rest_rows, 'dp', axis_index_groups=planes)  15.2 us
    pallas_call x2, Pallas kernels, place(): pl.pallas_call(functools.partial(place_body, len(chunks)), grid=(landmark...  14.5 us
    unnamed x55, local copies, waits for them, and re-layouts  14 us
    pallas_call x2, Pallas kernels, pieces(): pl.pallas_call(pieces_body, in_specs=[pl.BlockSpec(memory_space=pltpu.SME...  11 us
  transfers between devices with their start and end apart: 28, of which 8 were waited for; matrix products, arithmetic and copies ran while one was open for 17% of the time, Pallas kernels for 22%

profile of v5, /device:TPU:0, one launch (start us, length us, event | category | flops | bytes accessed | tf_op | source)
XLA Modules:
  0.0 210.6 jit_solution(11520668211944457132)
XLA Ops:
  7.9 4.4 %pack.1 = (bf16[256,512]{1,0:T(8,128)(2,1)}, f32[2048,128]{1,0:T(8,128)S(1)}) custom-call(s32[1]{0:T(128)} %bitcast.13.at_ref, s32[1,2048]{1,0:T(1,128)S(1)} %bitcast.48, bf16[1024,512]{1,0:T(8,128)(2,1)} %fps_ref.1), custom_call_target="tpu_custom_call" | custom-call | tf_op jit(solution)/shard_map/pack/pallas_call | solution.py:375
  12.3 4.0 %collective-permute-start.6 = (bf16[256,512]{1,0:T(8,128)(2,1)}, bf16[256,512]{1,0:T(8,128)(2,1)}, u32[]{:S(2)}, u32[]{:S(2)}) collective-permute-start(bf16[256,512]{1,0:T(8,128)(2,1)} %get-tuple-element.29.refs_0_), channel_id=1, source_target_pairs={{0,8},{1,9},{2,10},{3,11},{4,12},{5,13},{6,14},{7,15},{8,0},{9,1},... | collective-permute-start | bytes 786440 | tf_op jit(solution)/shard_map/ppermute | solution.py:95
  23.1 5.5 %collective-permute-done.6.refs_6_ = bf16[256,512]{1,0:T(8,128)(2,1)} collective-permute-done((bf16[256,512]{1,0:T(8,128)(2,1)}, bf16[256,512]{1,0:T(8,128)(2,1)}, u32[]{:S(2)}, u32[]{:S(2)}) %collective-permute-start.6) | collective-permute-done | bytes 262176 | tf_op jit(solution)/shard_map/ppermute | solution.py:95
  33.4 4.4 %collective-permute-done.9.refs_2_ = bf16[256,512]{1,0:T(8,128)(2,1)} collective-permute-done((bf16[256,512]{1,0:T(8,128)(2,1)}, bf16[256,512]{1,0:T(8,128)(2,1)}, u32[]{:S(2)}, u32[]{:S(2)}) %collective-permute-start.9) | collective-permute-done | bytes 262176 | tf_op jit(solution)/shard_map/ppermute | solution.py:95
  40.5 7.3 %place.2.refs_8_ = bf16[2048,512]{1,0:T(8,128)(2,1)S(1)} custom-call(s32[8]{0:T(128)S(1)} %broadcast_multiply_fusion.2.base_ref, f32[2048,128]{1,0:T(8,128)S(1)} %get-tuple-element.28.slots_ref, bf16[256,512]{1,0:T(8,128)(2,1)} %get-tuple-element.29.refs_0_, bf16[256,512]{1,0:T(8,128)(2,1)} %collective-permute-done.2.refs_1_, ...), custom_call_target="tpu_custom_call" | custom-call | tf_op jit(solution)/shard_map/place/pallas_call | solution.py:415
  48.5 2.9 %collective-permute-done.13.refs_6_ = bf16[256,512]{1,0:T(8,128)(2,1)} collective-permute-done((bf16[256,512]{1,0:T(8,128)(2,1)}, bf16[256,512]{1,0:T(8,128)(2,1)}, u32[]{:S(2)}, u32[]{:S(2)}) %collective-permute-start.13) | collective-permute-done | bytes 262176 | tf_op jit(solution)/shard_map/ppermute | solution.py:95
  54.1 7.2 %place.3.land_ref = bf16[2048,512]{1,0:T(8,128)(2,1)S(1)} custom-call(s32[8]{0:T(128)S(1)} %broadcast_multiply_fusion.3.base_ref, f32[2048,128]{1,0:T(8,128)S(1)} %get-tuple-element.28.slots_ref, bf16[256,512]{1,0:T(8,128)(2,1)} %collective-permute-done.1.refs_0_, bf16[256,512]{1,0:T(8,128)(2,1)S(1)} %collective-permute-done.8.refs_1_, ...), custom_call_target="tpu_custom_call" | custom-call | tf_op jit(solution)/shard_map/place/pallas_call | solution.py:415
  61.2 23.6 %stage.1 = (bf16[2048,2048]{1,0:T(8,128)(2,1)S(1)}, f32[8,128,128]{2,1,0:T(8,128)S(1)}, f32[128,1792]{1,0:T(8,128)S(1)}, f32[152,256]{1,0:T(8,128)S(1)}, f32[1,2048]{1,0:T(1,128)S(1)}, /*index=5*/f32[2048,128]{1,0:T(8,128)S(1)}) custom-call(s32[1]{0:T(128)} %bitcast.4.core_ref, bf16[2048,512]{1,0:T(8,128)(2,1)S(1)} %place.3.land_ref, ...), custom_call_target="tpu_custom_call" | custom-call | tf_op jit(solution)/shard_map/stage/pallas_call | solution.py:213
  87.8 5.5 %pieces.2 = (f32[256,1920]{1,0:T(8,128)S(1)}, bf16[256,1920]{1,0:T(8,128)(2,1)}) custom-call(s32[4]{0:T(128)S(1)} %get-tuple-element.64.at_ref, bf16[2048,2048]{1,0:T(8,128)(2,1)S(1)} %get-tuple-element.40.ct_ref, f32[1,2048]{1,0:T(1,128)S(1)} %get-tuple-element.35.lead_ref, f32[2048,128]{1,0:T(8,128)S(1)} %get-tuple-element.36.column_ref, ...), custom_call_target="tpu_custom_call" | custom-call | tf_op jit(solution)/shard_map/pieces/pallas_call | solution.py:271
  95.1 2.4 %copy.9 = f32[128,1792]{0,1:T(8,128)} copy(f32[128,1792]{1,0:T(8,128)} %copy-done.10) | data formatting | bytes 1835008 | tf_op jit(solution)/shard_map/stage/pallas_call | solution.py:213
  102.7 2.5 %copy.17 = f32[128,1792]{1,0:T(8,128)} copy(f32[128,1792]{0,1:T(8,128)} %subtract_divide_fusion) | data formatting | bytes 1835008 | tf_op jit(solution)/shard_map/div | solution.py:27
  105.2 3.4 %copy-done.1 = bf16[2048,2048]{1,0:T(8,128)(2,1)S(1)} copy-done((bf16[2048,2048]{1,0:T(8,128)(2,1)S(1)}, bf16[2048,2048]{1,0:T(8,128)(2,1)}, u32[]{:S(2)}) %copy-start.1) | copy-done | bytes 8388632
  109.6 5.5 %pieces.3 = (f32[256,1920]{1,0:T(8,128)S(1)}, bf16[256,1920]{1,0:T(8,128)(2,1)}) custom-call(s32[4]{0:T(128)S(1)} %get-tuple-element.63.at_ref, bf16[2048,2048]{1,0:T(8,128)(2,1)S(1)} %copy-done.1, f32[1,2048]{1,0:T(1,128)S(1)} %get-tuple-element.35.lead_ref, f32[2048,128]{1,0:T(8,128)S(1)} %get-tuple-element.36.column_ref, f32[8,128,128]{2,1,0:T(8,128)S(1)} %copy-done.5), custom_call_target="tpu_custom_call" | custom-call | tf_op jit(solution)/shard_map/pieces/pallas_call | solution.py:271
  118.4 2.1 collective-permute-start.20
  120.5 2.4 %collective-permute-done.21 = bf16[256,1920]{1,0:T(8,128)(2,1)} collective-permute-done((bf16[256,1920]{1,0:T(8,128)(2,1)}, bf16[256,1920]{1,0:T(8,128)(2,1)}, u32[]{:S(2)}, u32[]{:S(2)}) %collective-permute-start.21) | collective-permute-done | bytes 983072 | tf_op jit(solution)/shard_map/ppermute | solution.py:95
  125.7 6.4 %collective-permute-done.20 = f32[224,256]{1,0:T(8,128)S(1)} collective-permute-done((f32[224,256]{1,0:T(8,128)S(1)}, f32[224,256]{1,0:T(8,128)S(1)}, u32[]{:S(2)}, u32[]{:S(2)}) %collective-permute-start.20) | collective-permute-done | bytes 229408 | tf_op jit(solution)/shard_map/ppermute | solution.py:95
  137.5 7.1 %factor.4.state_ref = f32[256,512]{1,0:T(8,128)S(1)} custom-call(f32[256,512]{1,0:T(8,128)S(1)} %pad_maximum_fusion.2.state_ref), custom_call_target="tpu_custom_call" | custom-call | tf_op jit(solution)/shard_map/factor/pallas_call | solution.py:328
  148.1 6.9 %factor.5.state_ref = f32[256,512]{1,0:T(8,128)S(1)} custom-call(f32[256,512]{1,0:T(8,128)S(1)} %factor.4.state_ref), custom_call_target="tpu_custom_call" | custom-call | tf_op jit(solution)/shard_map/factor/pallas_call | solution.py:328
  158.0 3.1 %collective-permute-start.25 = (bf16[128,1920]{1,0:T(8,128)(2,1)}, bf16[128,1920]{1,0:T(8,128)(2,1)}, u32[]{:S(2)}, u32[]{:S(2)}) collective-permute-start(bf16[128,1920]{1,0:T(8,128)(2,1)} %fusion.16), channel_id=1, source_target_pairs={{0,8},{1,9},{2,10},{3,11},{4,12},{5,13},{6,14},{7,15},{8,0},{9,1},... | collective-permute-start | bytes 1474568 | tf_op jit(solution)/shard_map/ppermute | solution.py:95
  161.1 6.8 %factor.6.state_ref = f32[256,512]{1,0:T(8,128)S(1)} custom-call(f32[256,512]{1,0:T(8,128)S(1)} %factor.5.state_ref), custom_call_target="tpu_custom_call" | custom-call | tf_op jit(solution)/shard_map/factor/pallas_call | solution.py:328
  167.9 6.3 %factor.7 = f32[256,512]{1,0:T(8,128)S(1)} custom-call(f32[256,512]{1,0:T(8,128)S(1)} %factor.6.state_ref), custom_call_target="tpu_custom_call" | custom-call | tf_op jit(solution)/shard_map/factor/pallas_call | solution.py:328
  174.2 15.2 %all-reduce.2.cloned.1.call-done = f32[128,1792]{0,1:T(8,128)} async-done(((f32[128,1792]{0,1:T(8,128)}), f32[128,1792]{0,1:T(8,128)}) %all-reduce.2.cloned.1.call-update) | async-done | bytes 917520 | tf_op jit(solution)/shard_map/psum | solution.py:488
  189.4 2.8 %fusion = f32[128,1792]{0,1:T(8,128)S(1)} fusion(f32[128,1792]{0,1:T(8,128)} %all-reduce.2.cloned.1.call-done, f32[8,2048]{1,0:T(8,128)S(1)} %broadcast_multiply_fusion, f32[8,2048]{1,0:T(8,128)S(1)} %get-tuple-element.59, s32[]{:T(128)S(6)} %select_n.39, f32[8,2048]{1,0:T(8,128)S(1)} %get-tuple-element.58, f32[8,2048]{1,0:T(8,128)S(1)} %bitcast.52), kind=kOutput, calls=%fused_computation.8 | convolution fusion | flops 44529664 | bytes 2097156 | tf_op jit(solution)/shard_map/dot_general | solution.py:99
  200.7 3.1 %convolution_subtract_fusion = f32[128,2048]{1,0:T(8,128)} fusion(f32[256,2048]{1,0:T(8,128)S(1)} %fusion.1, f32[128,1792]{1,0:T(8,128)S(1)} %fusion.18, f32[128,256]{1,0:T(8,128)} %fusion.31, s32[]{:T(128)S(6)} %select_n.41), kind=kOutput, calls=%fused_computation.9 | convolution fusion | flops 805830656 | bytes 4325380 | tf_op jit(solution)/shard_map/dot_general | solution.py:99
  (151 shorter events, 55.2 us)
Async XLA Ops:
  7.2 182.3 %all-reduce.2.cloned.1.call-start = ((), (), s32[]{:S(2)}) async-start(), calls=%async_computation | async-start | bytes 1835008 | tf_op jit(solution)/shard_map/psum | solution.py:488
  12.3 16.4 %collective-permute-start.6 = (bf16[256,512]{1,0:T(8,128)(2,1)}, bf16[256,512]{1,0:T(8,128)(2,1)}, u32[]{:S(2)}, u32[]{:S(2)}) collective-permute-start(bf16[256,512]{1,0:T(8,128)(2,1)} %get-tuple-element.29.refs_0_), channel_id=1, source_target_pairs={{0,8},{1,9},{2,10},{3,11},{4,12},{5,13},{6,14},{7,15},{8,0},{9,1},... | collective-permute-start | bytes 786440 | tf_op jit(solution)/shard_map/ppermute | solution.py:95
  16.3 12.4 %collective-permute-start = (bf16[256,512]{1,0:T(8,128)(2,1)}, bf16[256,512]{1,0:T(8,128)(2,1)S(1)}, u32[]{:S(2)}, u32[]{:S(2)}) collective-permute-start(bf16[256,512]{1,0:T(8,128)(2,1)} %get-tuple-element.29.refs_0_), channel_id=1, source_target_pairs={{0,4},{1,5},{2,6},{3,7},{4,0},{5,1},{6,2},{7,3},{8,12},{9,13},{10,... | collective-permute-start | bytes 786440 | tf_op jit(solution)/shard_map/ppermute | solution.py:95
  17.9 11.3 %collective-permute-start.3 = (bf16[256,512]{1,0:T(8,128)(2,1)}, bf16[256,512]{1,0:T(8,128)(2,1)}, u32[]{:S(2)}, u32[]{:S(2)}) collective-permute-start(bf16[256,512]{1,0:T(8,128)(2,1)} %get-tuple-element.29.refs_0_), channel_id=1, source_target_pairs={{0,2},{1,3},{2,0},{3,1},{4,6},{5,7},{6,4},{7,5},{8,10},{9,11},{10,... | collective-permute-start | bytes 786440 | tf_op jit(solution)/shard_map/ppermute | solution.py:95
  19.4 10.8 %collective-permute-start.2 = (bf16[256,512]{1,0:T(8,128)(2,1)}, bf16[256,512]{1,0:T(8,128)(2,1)}, u32[]{:S(2)}, u32[]{:S(2)}) collective-permute-start(bf16[256,512]{1,0:T(8,128)(2,1)} %get-tuple-element.29.refs_0_), channel_id=1, source_target_pairs={{0,1},{1,0},{2,3},{3,2},{4,5},{5,4},{6,7},{7,6},{8,9},{9,8},{10,11... | collective-permute-start | bytes 786440 | tf_op jit(solution)/shard_map/ppermute | solution.py:95
  19.4 32.0 %collective-permute-start.15 = (bf16[1024,512]{1,0:T(8,128)(2,1)}, bf16[1024,512]{1,0:T(8,128)(2,1)}, u32[]{:S(2)}, u32[]{:S(2)}) collective-permute-start(bf16[1024,512]{1,0:T(8,128)(2,1)} %fps_ref.1), channel_id=1, source_target_pairs={{0,1},{1,0},{2,3},{3,2},{4,5},{5,4},{6,7},{7,6},{8,9},{9,8},{10,11... | collective-permute-start | bytes 3145736 | tf_op jit(solution)/shard_map/ppermute | solution.py:95
  28.8 4.1 %collective-permute-start.7 = (bf16[256,512]{1,0:T(8,128)(2,1)}, bf16[256,512]{1,0:T(8,128)(2,1)}, u32[]{:S(2)}, u32[]{:S(2)}) collective-permute-start(bf16[256,512]{1,0:T(8,128)(2,1)} %collective-permute-done.6.refs_6_), channel_id=1, source_target_pairs={{0,1},{1,0},{2,3},{3,2},{4,5},{5,4},{6,7},{7,6},{8,9},{9,8},{10,11... | collective-permute-start | bytes 786440 | tf_op jit(solution)/shard_map/ppermute | solution.py:95
  29.2 8.6 %collective-permute-start.9 = (bf16[256,512]{1,0:T(8,128)(2,1)}, bf16[256,512]{1,0:T(8,128)(2,1)}, u32[]{:S(2)}, u32[]{:S(2)}) collective-permute-start(bf16[256,512]{1,0:T(8,128)(2,1)} %collective-permute-done.6.refs_6_), channel_id=1, source_target_pairs={{0,4},{1,5},{2,6},{3,7},{4,0},{5,1},{6,2},{7,3},{8,12},{9,13},{10,... | collective-permute-start | bytes 786440 | tf_op jit(solution)/shard_map/ppermute | solution.py:95
  31.3 16.6 %collective-permute-start.11 = (bf16[256,512]{1,0:T(8,128)(2,1)}, bf16[256,512]{1,0:T(8,128)(2,1)}, u32[]{:S(2)}, u32[]{:S(2)}) collective-permute-start(bf16[256,512]{1,0:T(8,128)(2,1)} %collective-permute-done.6.refs_6_), channel_id=1, source_target_pairs={{0,2},{1,3},{2,0},{3,1},{4,6},{5,7},{6,4},{7,5},{8,10},{9,11},{10,... | collective-permute-start | bytes 786440 | tf_op jit(solution)/shard_map/ppermute | solution.py:95
  32.9 15.1 %collective-permute-start.1 = (bf16[256,512]{1,0:T(8,128)(2,1)S(1)}, bf16[256,512]{1,0:T(8,128)(2,1)}, u32[]{:S(2)}, u32[]{:S(2)}) collective-permute-start(bf16[256,512]{1,0:T(8,128)(2,1)S(1)} %collective-permute-done.refs_4_), channel_id=1, source_target_pairs={{0,2},{1,3},{2,0},{3,1},{4,6},{5,7},{6,4},{7,5},{8,10},{9,11},{10,... | collective-permute-start | bytes 786440 | tf_op jit(solution)/shard_map/ppermute | solution.py:95
  33.4 7.1 %collective-permute-start.4 = (bf16[256,512]{1,0:T(8,128)(2,1)}, bf16[256,512]{1,0:T(8,128)(2,1)}, u32[]{:S(2)}, u32[]{:S(2)}) collective-permute-start(bf16[256,512]{1,0:T(8,128)(2,1)} %collective-permute-done.3.refs_2_), channel_id=1, source_target_pairs={{0,1},{1,0},{2,3},{3,2},{4,5},{5,4},{6,7},{7,6},{8,9},{9,8},{10,11... | collective-permute-start | bytes 786440 | tf_op jit(solution)/shard_map/ppermute | solution.py:95
  37.8 13.6 %collective-permute-start.13 = (bf16[256,512]{1,0:T(8,128)(2,1)}, bf16[256,512]{1,0:T(8,128)(2,1)}, u32[]{:S(2)}, u32[]{:S(2)}) collective-permute-start(bf16[256,512]{1,0:T(8,128)(2,1)} %collective-permute-done.9.refs_2_), channel_id=1, source_target_pairs={{0,2},{1,3},{2,0},{3,1},{4,6},{5,7},{6,4},{7,5},{8,10},{9,11},{10,... | collective-permute-start | bytes 786440 | tf_op jit(solution)/shard_map/ppermute | solution.py:95
  47.9 5.3 %collective-permute-start.12 = (bf16[256,512]{1,0:T(8,128)(2,1)}, bf16[256,512]{1,0:T(8,128)(2,1)S(1)}, u32[]{:S(2)}, u32[]{:S(2)}) collective-permute-start(bf16[256,512]{1,0:T(8,128)(2,1)} %collective-permute-done.11.refs_4_), channel_id=1, source_target_pairs={{0,1},{1,0},{2,3},{3,2},{4,5},{5,4},{6,7},{7,6},{8,9},{9,8},{10,11... | collective-permute-start | bytes 786440 | tf_op jit(solution)/shard_map/ppermute | solution.py:95
  48.0 5.3 %collective-permute-start.8 = (bf16[256,512]{1,0:T(8,128)(2,1)}, bf16[256,512]{1,0:T(8,128)(2,1)S(1)}, u32[]{:S(2)}, u32[]{:S(2)}) collective-permute-start(bf16[256,512]{1,0:T(8,128)(2,1)} %collective-permute-done.1.refs_0_), channel_id=1, source_target_pairs={{0,1},{1,0},{2,3},{3,2},{4,5},{5,4},{6,7},{7,6},{8,9},{9,8},{10,11... | collective-permute-start | bytes 786440 | tf_op jit(solution)/shard_map/ppermute | solution.py:95
  48.5 4.8 %collective-permute-start.10 = (bf16[256,512]{1,0:T(8,128)(2,1)}, bf16[256,512]{1,0:T(8,128)(2,1)S(1)}, u32[]{:S(2)}, u32[]{:S(2)}) collective-permute-start(bf16[256,512]{1,0:T(8,128)(2,1)} %collective-permute-done.9.refs_2_), channel_id=1, source_target_pairs={{0,1},{1,0},{2,3},{3,2},{4,5},{5,4},{6,7},{7,6},{8,9},{9,8},{10,11... | collective-permute-start | bytes 786440 | tf_op jit(solution)/shard_map/ppermute | solution.py:95
  85.8 12.0 %collective-permute-start.17 = (f32[152,256]{1,0:T(8,128)S(1)}, f32[152,256]{1,0:T(8,128)}, u32[]{:S(2)}, u32[]{:S(2)}) collective-permute-start(f32[152,256]{1,0:T(8,128)S(1)} %get-tuple-element.34), channel_id=1, source_target_pairs={{0,2},{1,3},{2,0},{3,1},{4,6},{5,7},{6,4},{7,5},{8,10},{9,11},{10,... | collective-permute-start | bytes 466952 | tf_op jit(solution)/shard_map/ppermute | solution.py:95
  94.6 28.2 %collective-permute-start.21 = (bf16[256,1920]{1,0:T(8,128)(2,1)}, bf16[256,1920]{1,0:T(8,128)(2,1)}, u32[]{:S(2)}, u32[]{:S(2)}) collective-permute-start(bf16[256,1920]{1,0:T(8,128)(2,1)} %get-tuple-element.44), channel_id=1, source_target_pairs={{0,2},{1,3},{2,0},{3,1},{4,6},{5,7},{6,4},{7,5},{8,10},{9,11},{10,... | collective-permute-start | bytes 2949128 | tf_op jit(solution)/shard_map/ppermute | solution.py:95
  100.1 16.5 %collective-permute-start.19 = (f32[176,256]{1,0:T(8,128)}, f32[176,256]{1,0:T(8,128)}, u32[]{:S(2)}, u32[]{:S(2)}) collective-permute-start(f32[176,256]{1,0:T(8,128)} %pad_maximum_fusion.5), channel_id=1, source_target_pairs={{0,4},{1,5},{2,6},{3,7},{4,0},{5,1},{6,2},{7,3},{8,12},{9,13},{10,... | collective-permute-start | bytes 540680 | tf_op jit(solution)/shard_map/ppermute | solution.py:95
  115.1 39.9 %collective-permute-start.18 = (bf16[256,1920]{1,0:T(8,128)(2,1)}, bf16[256,1920]{1,0:T(8,128)(2,1)}, u32[]{:S(2)}, u32[]{:S(2)}) collective-permute-start(bf16[256,1920]{1,0:T(8,128)(2,1)} %get-tuple-element.42), channel_id=1, source_target_pairs={{0,2},{1,3},{2,0},{3,1},{4,6},{5,7},{6,4},{7,5},{8,10},{9,11},{10,... | collective-permute-start | bytes 2949128 | tf_op jit(solution)/shard_map/ppermute | solution.py:95
  118.4 13.7 %collective-permute-start.20 = (f32[224,256]{1,0:T(8,128)S(1)}, f32[224,256]{1,0:T(8,128)S(1)}, u32[]{:S(2)}, u32[]{:S(2)}) collective-permute-start(f32[224,256]{1,0:T(8,128)S(1)} %pad_maximum_fusion.3), channel_id=1, source_target_pairs={{0,8},{1,9},{2,10},{3,11},{4,12},{5,13},{6,14},{7,15},{8,0},{9,1},... | collective-permute-start | bytes 688136 | tf_op jit(solution)/shard_map/ppermute | solution.py:95
  132.2 14.0 %collective-permute-start.23 = (bf16[128,1920]{1,0:T(8,128)(2,1)}, bf16[128,1920]{1,0:T(8,128)(2,1)}, u32[]{:S(2)}, u32[]{:S(2)}) collective-permute-start(bf16[128,1920]{1,0:T(8,128)(2,1)} %slice.166), channel_id=1, source_target_pairs={{0,4},{1,5},{2,6},{3,7},{4,0},{5,1},{6,2},{7,3},{8,12},{9,13},{10,... | collective-permute-start | bytes 1474568 | tf_op jit(solution)/shard_map/ppermute | solution.py:95
  157.3 36.0 %collective-permute-start.24 = (bf16[128,1920]{1,0:T(8,128)(2,1)}, bf16[128,1920]{1,0:T(8,128)(2,1)}, u32[]{:S(2)}, u32[]{:S(2)}) collective-permute-start(bf16[128,1920]{1,0:T(8,128)(2,1)} %slice.165), channel_id=1, source_target_pairs={{0,4},{1,5},{2,6},{3,7},{4,0},{5,1},{6,2},{7,3},{8,12},{9,13},{10,... | collective-permute-start | bytes 1474568 | tf_op jit(solution)/shard_map/ppermute | solution.py:95
  158.0 35.3 %collective-permute-start.25 = (bf16[128,1920]{1,0:T(8,128)(2,1)}, bf16[128,1920]{1,0:T(8,128)(2,1)}, u32[]{:S(2)}, u32[]{:S(2)}) collective-permute-start(bf16[128,1920]{1,0:T(8,128)(2,1)} %fusion.16), channel_id=1, source_target_pairs={{0,8},{1,9},{2,10},{3,11},{4,12},{5,13},{6,14},{7,15},{8,0},{9,1},... | collective-permute-start | bytes 1474568 | tf_op jit(solution)/shard_map/ppermute | solution.py:95
  193.0 3.3 %collective-permute-start.26 = (f32[128,1792]{0,1:T(8,128)S(1)}, f32[128,1792]{0,1:T(8,128)S(1)}, u32[]{:S(2)}, u32[]{:S(2)}) collective-permute-start(f32[128,1792]{0,1:T(8,128)S(1)} %fusion.12), channel_id=1, source_target_pairs={{0,1},{1,0},{2,3},{3,2},{4,5},{5,4},{6,7},{7,6},{8,9},{9,8},{10,11... | collective-permute-start | bytes 2752520 | tf_op jit(solution)/shard_map/ppermute | solution.py:95
  (29 other events, 169.9 us)
Sparse Core Ops, SparseCore 0:
  97.7 91.6 all-reduce.1

commit v6 on v5

--- a/solution.py
+++ b/solution.py
@@ -89,6 +89,7 @@
 LANES = 128
 TILE = 256
 MIB = 2**20
+LITTLE = pl.CostEstimate(flops=1, transcendentals=0, bytes_accessed=1)
 
 
 def send(x, perm):
@@ -128,7 +129,7 @@
 def stage_body(
     core_ref, land_ref, fps_ref, norms_ref, tgs_ref,
     ct_ref, rhs_ref, rest_ref, message_ref, lead_ref, column_ref,
-    cent_ref, first_ref, left_ref, low_ref, mean_ref,
+    cent_ref, first_ref, left_ref, mean_ref,
 ):
     step = pl.program_id(0)
     rows = fps_ref.shape[0]
@@ -146,9 +147,10 @@
     mean = total * (1.0 / rows)
     for n in range(0, rows, TILE):
         cent = cent_ref[:, n : n + TILE] - mean
-        high = cent.astype(jnp.bfloat16)
-        ct_ref[:, n : n + TILE] = high
-        low_ref[:, n : n + TILE] = (cent - high.astype(jnp.float32)).astype(jnp.bfloat16)
+        cent_ref[:, n : n + TILE] = cent
+        ct_ref[:, n : n + TILE] = cent.astype(jnp.bfloat16)
+    own = cent_ref[pl.ds(block, LANES), :]
+    low = (own - ct_ref[pl.ds(block, LANES), :].astype(jnp.float32)).astype(jnp.bfloat16)
     mean_ref[:, pl.ds(base, TILE)] = jnp.broadcast_to(mean, (TILE, LANES)).T[:1, :]
 
     @pl.when(step == 0)
@@ -158,8 +160,9 @@
 
     both = dot_nt(left_ref[...], ct_ref[...])
     first_ref[:, pl.ds(base, TILE)] = both[:LANES, :]
-    cent_ref[:LANES, :TILE] = both[LANES:, :] + dot_nt(left_ref[LANES:, :], low_ref[...])
-    rhs_ref[step] = cent_ref[:LANES, pl.ds(block, LANES)].T
+    cent_ref[:LANES, :TILE] = both[LANES:, :]
+    high_part = cent_ref[:LANES, pl.ds(block, LANES)]
+    rhs_ref[step] = (high_part + dot_nt(left_ref[LANES:, :], low)).T
 
     @pl.when(step == pl.num_programs(0) - 1)
     def _():
@@ -227,7 +230,6 @@
                 pltpu.VMEM((TILE, rows), f32),
                 pltpu.VMEM((LANES, landmarks), f32),
                 pltpu.VMEM((2 * LANES, rows), bf16),
-                pltpu.VMEM((TILE, rows), bf16),
                 pltpu.VMEM((1, landmarks), f32),
             ],
         ),
@@ -278,6 +280,7 @@
         ],
         scratch_shapes=[pltpu.VMEM((2 * shape[0], ct.shape[1]), jnp.bfloat16)],
         compiler_params=pltpu.CompilerParams(vmem_limit_bytes=28 * MIB),
+        cost_estimate=LITTLE,
         name="pieces",
     )(jnp.stack(starts).astype(jnp.int32), ct, lead, column, rhs_part)
 
@@ -331,8 +334,49 @@
         out_specs=vmem(1)[0],
         out_shape=jax.ShapeDtypeStruct(state.shape, jnp.float32),
         compiler_params=pltpu.CompilerParams(vmem_limit_bytes=28 * MIB),
+        cost_estimate=LITTLE,
         name="factor",
     )(state)
+
+
+def finish_body(
+    scale, at_ref, state_ref, corner_ref, sums_ref, added_ref, rest_ref,
+    panel_ref, trailing_ref, factor_ref, own_ref,
+):
+    width = corner_ref.shape[0]
+    start = pl.multiple_of(at_ref[0], LANES)
+    inverse = state_ref[:, width:]
+    own_ref[:, :width] = corner_ref[...]
+    factor_ref[:, :width] = exact_dot(inverse, corner_ref[...])
+    for lo in range(0, rest_ref.shape[1], TILE):
+        cols = slice(lo, lo + TILE)
+        rows = sums_ref[:, cols].astype(jnp.float32) * scale + added_ref[:, cols]
+        own_ref[:, lo + width : lo + width + TILE] = rows
+        factor_ref[:, lo + width : lo + width + TILE] = exact_dot(inverse, rows)
+    panel = factor_ref[:, pl.ds(start, LANES)].T
+    panel_ref[...] = panel
+    first = own_ref[:, pl.ds(start, LANES)].T
+    trailing_ref[:, :width] = first - exact_dot(panel, factor_ref[:, :width])
+    for lo in range(0, rest_ref.shape[1], TILE):
+        here = slice(lo + width, lo + width + TILE)
+        trailing_ref[:, here] = rest_ref[:, lo : lo + TILE] - exact_dot(panel, factor_ref[:, here])
+
+
+def finish(scale, start, state, corner, sums, added, rest):
+    width, landmarks = corner.shape[0], rest.shape[1] + corner.shape[0]
+    f32 = jnp.float32
+    return pl.pallas_call(
+        functools.partial(finish_body, scale),
+        in_specs=[pl.BlockSpec(memory_space=pltpu.SMEM)] + vmem(5),
+        out_specs=vmem(2),
+        out_shape=[
+            jax.ShapeDtypeStruct((LANES, width), f32),
+            jax.ShapeDtypeStruct((LANES, landmarks), f32),
+        ],
+        scratch_shapes=[pltpu.VMEM((width, landmarks), f32), pltpu.VMEM((width, landmarks), f32)],
+        compiler_params=pltpu.CompilerParams(vmem_limit_bytes=28 * MIB),
+        name="finish",
+    )(jnp.reshape(start, (1,)), state, corner, sums, added, rest)
 
 
 def pack_body(at_ref, index_ref, fps_ref, packed_ref, slots_ref, key_ref, pick_ref):
@@ -508,10 +552,10 @@
     left_terms = jnp.concatenate([shift * chip_rows, leads], axis=0)
     right_terms = jnp.concatenate([shift, leads * lead_weights], axis=0)
 
-    def system_part(sums, start, cols):
+    def added_part(start, cols):
         rows_fps = lax.dynamic_slice_in_dim(landmark_fps, start, share, 0)
         terms = lax.dynamic_slice_in_dim(left_terms, start, share, 1)
-        return (sums + highest(terms, right_terms[:, cols])) * scale + tanimoto(
+        return highest(terms, right_terms[:, cols]) * scale + tanimoto(
             rows_fps, landmark_fps[cols], norms[cols]
         )
 
@@ -524,7 +568,7 @@
     def both_blocks(block):
         return in_order(block, send(block, CORE), core)
 
-    corner = both_blocks(system_part(message[:share], core * share, panel_cols))
+    corner = both_blocks(message[:share] * scale + added_part(core * share, panel_cols))
     state = jnp.concatenate([corner, jnp.eye(width, dtype=f32)], axis=1)
 
     calls = [(b, b + 1) for b in range(0, width // CHOL, 2)]
@@ -537,22 +581,17 @@
     got_one = send(one, NEAR)
     state = eliminate_blocks(after(state, one), calls[2])
     state = eliminate_blocks(state, calls[3])
-    block = both_blocks(system_part(after(part, state), core * share, other_cols))
-    panel_rows = jnp.concatenate([corner, block], axis=1)
-    factor = exact_dot(state[:, width:], panel_rows)
-
+    start = position * share
     own = sums_10[share:] + got_one.astype(f32) + got_two.astype(f32)
-    start = position * share
-    rest = system_part(own[:, : landmarks - width], start, other_cols)
+    rest = own[:, : landmarks - width] * scale + added_part(start, other_cols)
     own_shift = lax.dynamic_slice_in_dim(shift, start, share, 1)
     rhs = (own[:, landmarks - width :] + highest(own_shift, target_sums)) / math.sqrt(
         ridge_weight * total_rows
     )
-    own_panel = lax.dynamic_slice_in_dim(panel_rows, start, share, 1)
-    own_factor = lax.dynamic_slice_in_dim(factor, start, share, 1)
-    system_rows = jnp.concatenate([own_panel.T, rest], axis=1)
-    trailing = system_rows - highest(own_factor, factor)
-    return (rhs, own_factor.T, trailing)
+    added = both_blocks(added_part(core * share, other_cols))
+    sums = both_blocks(after(part, state, added))
+    panel, trailing = finish(scale, start, state, corner, sums, added, rest)
+    return (rhs, panel, trailing)
 
 
 def solution(mesh):

time: 213 us -> 207 us (0.972)
  matrix products: 14.4 us -> 5.83 us
  waiting for transfers between devices: 38.6 us -> 44.1 us
  Pallas kernels: 80.5 us -> 77.4 us
  other arithmetic: 13.1 us -> 16 us
    pallas_call x1, Pallas kernels: 23.6 us -> 17.6 us  [stage(): pl.pallas_call(stage_body, grid_spec=pltpu.PrefetchScalarGridSpec(num_sca...]
    dot_general x5 -> x4, matrix products: 9.03 us -> 4.02 us  [highest(): lax.dot_general(a, b, (((0,), (0,)), ((), ())), precision=lax.Precision.H...]
    unnamed x55 -> x62, local copies, waits for them, and re-layouts: 14 us -> 18.7 us
    ppermute x27 -> x28, waiting for transfers between devices: 23.3 us -> 27.8 us  [send(): return lax.ppermute(x, 'dp', perm)]
    pallas_call x0 -> x1, Pallas kernels: none -> 4.09 us  [finish(): pl.pallas_call(functools.partial(finish_body, scale), in_specs=[pl.BlockS...]
    div x1 -> x0, local copies, waits for them, and re-layouts: 2.54 us -> none  [tanimoto(): inner_prod / (row_norms[:, None] + landmark_norms[None, :] - inner_prod)]
    pallas_call x1 -> x0, local copies, waits for them, and re-layouts: 2.44 us -> none  [stage(): pl.pallas_call(stage_body, grid_spec=pltpu.PrefetchScalarGridSpec(num_sca...]
    ppermute x27 -> x28, starting transfers between devices: 24.8 us -> 22.9 us  [send(): return lax.ppermute(x, 'dp', perm)]
  transfers between devices with their start and end apart: 28 -> 29, of which waited for: 8 -> 8; matrix products, arithmetic and copies ran while one was open for 17% -> 15% of each run, Pallas kernels for 22% -> 22%
where the time goes in v6:
time: 207 us; the launch traced here: 206 us
  Pallas kernels  77.4 us (37%)
  waiting for transfers between devices  44.1 us (21%)
  local copies, waits for them, and re-layouts  25 us (12%)
  starting transfers between devices  22.9 us (11%)
  other arithmetic  16 us (8%)
  between operations  14.6 us (7%)
  matrix products  5.83 us (3%)
    ppermute x28, waiting for transfers between devices, send(): return lax.ppermute(x, 'dp', perm)  27.8 us
    pallas_call x4, Pallas kernels, eliminate_blocks(): pl.pallas_call(functools.partial(factor_body, blocks), in_specs=vmem(1),...  27 us
    ppermute x28, starting transfers between devices, send(): return lax.ppermute(x, 'dp', perm)  22.9 us
    unnamed x62, local copies, waits for them, and re-layouts  18.7 us
    pallas_call x1, Pallas kernels, stage(): pl.pallas_call(stage_body, grid_spec=pltpu.PrefetchScalarGridSpec(num_sca...  17.6 us
    psum x1, waiting for transfers between devices, local_16(): part = lax.psum(rest_rows, 'dp', axis_index_groups=planes)  16.3 us
    pallas_call x2, Pallas kernels, place(): pl.pallas_call(functools.partial(place_body, len(chunks)), grid=(landmark...  14.1 us
    pallas_call x2, Pallas kernels, pieces(): pl.pallas_call(pieces_body, in_specs=[pl.BlockSpec(memory_space=pltpu.SME...  10.9 us
  transfers between devices with their start and end apart: 29, of which 8 were waited for; matrix products, arithmetic and copies ran while one was open for 15% of the time, Pallas kernels for 22%

profile of v6, /device:TPU:0, one launch (start us, length us, event | category | flops | bytes accessed | tf_op | source)
XLA Modules:
  0.0 206.0 jit_solution(7237244089559137143)
XLA Ops:
  7.9 3.7 %pack.1 = (bf16[256,512]{1,0:T(8,128)(2,1)S(1)}, f32[2048,128]{1,0:T(8,128)S(1)}) custom-call(s32[1]{0:T(128)} %bitcast.13.at_ref, s32[1,2048]{1,0:T(1,128)S(1)} %bitcast.44, bf16[1024,512]{1,0:T(8,128)(2,1)} %fps_ref.1), custom_call_target="tpu_custom_call" | custom-call | tf_op jit(solution)/shard_map/pack/pallas_call | solution.py:419
  11.6 4.1 %collective-permute-start.6 = (bf16[256,512]{1,0:T(8,128)(2,1)S(1)}, bf16[256,512]{1,0:T(8,128)(2,1)}, u32[]{:S(2)}, u32[]{:S(2)}) collective-permute-start(bf16[256,512]{1,0:T(8,128)(2,1)S(1)} %get-tuple-element.31.refs_0_), channel_id=1, source_target_pairs={{0,8},{1,9},{2,10},{3,11},{4,12},{5,13},{6,14},{7,15},{8,0},{9,1},... | collective-permute-start | bytes 786440 | tf_op jit(solution)/shard_map/ppermute | solution.py:96
  21.2 6.7 %collective-permute-done.6.refs_6_ = bf16[256,512]{1,0:T(8,128)(2,1)} collective-permute-done((bf16[256,512]{1,0:T(8,128)(2,1)S(1)}, bf16[256,512]{1,0:T(8,128)(2,1)}, u32[]{:S(2)}, u32[]{:S(2)}) %collective-permute-start.6) | collective-permute-done | bytes 262176 | tf_op jit(solution)/shard_map/ppermute | solution.py:96
  34.0 3.0 %collective-permute-done.9.refs_2_ = bf16[256,512]{1,0:T(8,128)(2,1)} collective-permute-done((bf16[256,512]{1,0:T(8,128)(2,1)}, bf16[256,512]{1,0:T(8,128)(2,1)}, u32[]{:S(2)}, u32[]{:S(2)}) %collective-permute-start.9) | collective-permute-done | bytes 262176 | tf_op jit(solution)/shard_map/ppermute | solution.py:96
  44.8 6.9 %place.2.refs_8_ = bf16[2048,512]{1,0:T(8,128)(2,1)S(1)} custom-call(s32[8]{0:T(128)S(1)} %broadcast_multiply_fusion.2.base_ref, f32[2048,128]{1,0:T(8,128)S(1)} %get-tuple-element.30.slots_ref, bf16[256,512]{1,0:T(8,128)(2,1)S(1)} %copy-done.13, bf16[256,512]{1,0:T(8,128)(2,1)S(1)} %copy-done.15, bf16[256,512]{1,0:T(8,128)(2,1)} %collective-permute-done.3.refs_2_, ...), custom_call_target="tpu_custom_call" | custom-call | tf_op jit(solution)/shard_map/place/pallas_call | solution.py:459
  55.5 7.2 %place.3.land_ref = bf16[2048,512]{1,0:T(8,128)(2,1)S(1)} custom-call(s32[8]{0:T(128)S(1)} %broadcast_multiply_fusion.3.base_ref, f32[2048,128]{1,0:T(8,128)S(1)} %get-tuple-element.30.slots_ref, bf16[256,512]{1,0:T(8,128)(2,1)} %collective-permute-done.1.refs_0_, bf16[256,512]{1,0:T(8,128)(2,1)S(1)} %collective-permute-done.8.refs_1_, ...), custom_call_target="tpu_custom_call" | custom-call | tf_op jit(solution)/shard_map/place/pallas_call | solution.py:459
  62.6 17.6 %stage.1 = (bf16[2048,2048]{1,0:T(8,128)(2,1)S(1)}, f32[8,128,128]{2,1,0:T(8,128)S(1)}, f32[128,1792]{1,0:T(8,128)S(1)}, f32[152,256]{1,0:T(8,128)S(1)}, f32[1,2048]{1,0:T(1,128)S(1)}, /*index=5*/f32[2048,128]{1,0:T(8,128)S(1)}) custom-call(s32[1]{0:T(128)} %bitcast.4.core_ref, bf16[2048,512]{1,0:T(8,128)(2,1)S(1)} %place.3.land_ref, ...), custom_call_target="tpu_custom_call" | custom-call | tf_op jit(solution)/shard_map/stage/pallas_call | solution.py:216
  81.8 5.5 %pieces.2 = (f32[256,1920]{1,0:T(8,128)S(1)}, bf16[256,1920]{1,0:T(8,128)(2,1)}) custom-call(s32[4]{0:T(128)S(1)} %get-tuple-element.65.at_ref, bf16[2048,2048]{1,0:T(8,128)(2,1)S(1)} %get-tuple-element.42.ct_ref, f32[1,2048]{1,0:T(1,128)S(1)} %get-tuple-element.37.lead_ref, f32[2048,128]{1,0:T(8,128)S(1)} %get-tuple-element.38.column_ref, ...), custom_call_target="tpu_custom_call" | custom-call | flops 1 | bytes 1 | tf_op jit(solution)/shard_map/pieces/pallas_call | solution.py:273
  95.3 3.4 %copy-done.1 = bf16[2048,2048]{1,0:T(8,128)(2,1)S(1)} copy-done((bf16[2048,2048]{1,0:T(8,128)(2,1)S(1)}, bf16[2048,2048]{1,0:T(8,128)(2,1)}, u32[]{:S(2)}) %copy-start.1) | copy-done | bytes 8388632
  99.7 5.5 %pieces.3 = (f32[256,1920]{1,0:T(8,128)S(1)}, bf16[256,1920]{1,0:T(8,128)(2,1)}) custom-call(s32[4]{0:T(128)S(1)} %get-tuple-element.64.at_ref, bf16[2048,2048]{1,0:T(8,128)(2,1)S(1)} %copy-done.1, f32[1,2048]{1,0:T(1,128)S(1)} %get-tuple-element.37.lead_ref, f32[2048,128]{1,0:T(8,128)S(1)} %get-tuple-element.38.column_ref, f32[8,128,128]{2,1,0:T(8,128)S(1)} %copy-done.6), custom_call_target="tpu_custom_call" | custom-call | flops 1 | bytes 1 | tf_op jit(solution)/shard_map/pieces/pallas_call | solution.py:273
  107.5 2.6 %collective-permute-start.20 = (f32[224,256]{1,0:T(8,128)S(1)}, f32[224,256]{1,0:T(8,128)S(1)}, u32[]{:S(2)}, u32[]{:S(2)}) collective-permute-start(f32[224,256]{1,0:T(8,128)S(1)} %pad_maximum_fusion.1), channel_id=1, source_target_pairs={{0,8},{1,9},{2,10},{3,11},{4,12},{5,13},{6,14},{7,15},{8,0},{9,1},... | collective-permute-start | bytes 688136 | tf_op jit(solution)/shard_map/ppermute | solution.py:96
  110.0 6.8 %collective-permute-done.21 = bf16[256,1920]{1,0:T(8,128)(2,1)} collective-permute-done((bf16[256,1920]{1,0:T(8,128)(2,1)}, bf16[256,1920]{1,0:T(8,128)(2,1)}, u32[]{:S(2)}, u32[]{:S(2)}) %collective-permute-start.21) | collective-permute-done | bytes 983072 | tf_op jit(solution)/shard_map/ppermute | solution.py:96
  119.7 5.5 %collective-permute-done.20 = f32[224,256]{1,0:T(8,128)S(1)} collective-permute-done((f32[224,256]{1,0:T(8,128)S(1)}, f32[224,256]{1,0:T(8,128)S(1)}, u32[]{:S(2)}, u32[]{:S(2)}) %collective-permute-start.20) | collective-permute-done | bytes 229408 | tf_op jit(solution)/shard_map/ppermute | solution.py:96
  129.0 7.1 %factor.4.state_ref = f32[256,512]{1,0:T(8,128)S(1)} custom-call(f32[256,512]{1,0:T(8,128)S(1)} %pad_maximum_fusion.state_ref), custom_call_target="tpu_custom_call" | custom-call | flops 1 | bytes 1 | tf_op jit(solution)/shard_map/factor/pallas_call | solution.py:331
  136.1 5.2 %collective-permute-done.23 = bf16[128,1920]{1,0:T(8,128)(2,1)} collective-permute-done((bf16[128,1920]{1,0:T(8,128)(2,1)}, bf16[128,1920]{1,0:T(8,128)(2,1)}, u32[]{:S(2)}, u32[]{:S(2)}) %collective-permute-start.23) | collective-permute-done | bytes 491552 | tf_op jit(solution)/shard_map/ppermute | solution.py:96
  141.3 1.9 fusion.22
  143.2 6.8 %factor.5.state_ref = f32[256,512]{1,0:T(8,128)S(1)} custom-call(f32[256,512]{1,0:T(8,128)S(1)} %factor.4.state_ref), custom_call_target="tpu_custom_call" | custom-call | flops 1 | bytes 1 | tf_op jit(solution)/shard_map/factor/pallas_call | solution.py:331
  150.0 2.7 %convert_add_fusion = f32[256,1920]{1,0:T(8,128)} fusion(f32[256,1920]{1,0:T(8,128)S(1)} %copy-done.8, bf16[256,1920]{1,0:T(8,128)(2,1)} %collective-permute-done.18), kind=kLoop, calls=%fused_computation.10 | loop fusion | flops 983040 | bytes 4915200 | tf_op jit(solution)/shard_map/add | solution.py:579
  152.7 2.3 %slice.162 = bf16[128,1920]{1,0:T(8,128)(2,1)} slice(f32[256,1920]{1,0:T(8,128)} %convert_add_fusion), slice={[0:128], [0:1920]} | slice | bytes 983040 | tf_op jit(solution)/shard_map/slice | solution.py:580
  158.7 6.8 %factor.6.state_ref = f32[256,512]{1,0:T(8,128)S(1)} custom-call(f32[256,512]{1,0:T(8,128)S(1)} %factor.5.state_ref), custom_call_target="tpu_custom_call" | custom-call | flops 1 | bytes 1 | tf_op jit(solution)/shard_map/factor/pallas_call | solution.py:331
  165.5 6.3 %factor.7.state_ref = f32[256,512]{1,0:T(8,128)S(1)} custom-call(f32[256,512]{1,0:T(8,128)S(1)} %factor.6.state_ref), custom_call_target="tpu_custom_call" | custom-call | flops 1 | bytes 1 | tf_op jit(solution)/shard_map/factor/pallas_call | solution.py:331
  171.8 1.9 fusion.3.added_ref
  173.7 16.3 %all-reduce.2.cloned.1.call-done = f32[128,1792]{1,0:T(8,128)} async-done(((f32[128,1792]{1,0:T(8,128)}), f32[128,1792]{1,0:T(8,128)}) %all-reduce.2.cloned.1.call-update) | async-done | bytes 917520 | tf_op jit(solution)/shard_map/psum | solution.py:532
  195.0 4.1 %finish.1 = (f32[128,256]{1,0:T(8,128)}, f32[128,2048]{1,0:T(8,128)}) custom-call(s32[1]{0:T(128)} %bitcast.31.at_ref, f32[256,512]{1,0:T(8,128)S(1)} %factor.7.state_ref, f32[256,256]{1,0:T(8,128)S(1)} %fusion.24.corner_ref, f32[256,1792]{1,0:T(8,128)S(1)} %fusion.1.sums_ref, f32[256,1792]{1,0:T(8,128)S(1)} %copy-done.4, f32[128,1792]{1,0:T(8,128)S(1)} %fusion.13.rest_ref), custom_call_target="tpu_custom_call" | custom-call | tf_op jit(solution)/shard_map/finish/pallas_call | solution.py:368
  (154 shorter events, 51.7 us)
Async XLA Ops:
  7.2 182.8 %all-reduce.2.cloned.1.call-start = ((), (), s32[]{:S(2)}) async-start(), calls=%async_computation | async-start | bytes 1835008 | tf_op jit(solution)/shard_map/psum | solution.py:532
  11.6 16.2 %collective-permute-start.6 = (bf16[256,512]{1,0:T(8,128)(2,1)S(1)}, bf16[256,512]{1,0:T(8,128)(2,1)}, u32[]{:S(2)}, u32[]{:S(2)}) collective-permute-start(bf16[256,512]{1,0:T(8,128)(2,1)S(1)} %get-tuple-element.31.refs_0_), channel_id=1, source_target_pairs={{0,8},{1,9},{2,10},{3,11},{4,12},{5,13},{6,14},{7,15},{8,0},{9,1},... | collective-permute-start | bytes 786440 | tf_op jit(solution)/shard_map/ppermute | solution.py:96
  15.7 12.2 %collective-permute-start = (bf16[256,512]{1,0:T(8,128)(2,1)S(1)}, bf16[256,512]{1,0:T(8,128)(2,1)S(1)}, u32[]{:S(2)}, u32[]{:S(2)}) collective-permute-start(bf16[256,512]{1,0:T(8,128)(2,1)S(1)} %get-tuple-element.31.refs_0_), channel_id=1, source_target_pairs={{0,4},{1,5},{2,6},{3,7},{4,0},{5,1},{6,2},{7,3},{8,12},{9,13},{10,... | collective-permute-start | bytes 786440 | tf_op jit(solution)/shard_map/ppermute | solution.py:96
  17.3 11.1 %collective-permute-start.3 = (bf16[256,512]{1,0:T(8,128)(2,1)S(1)}, bf16[256,512]{1,0:T(8,128)(2,1)}, u32[]{:S(2)}, u32[]{:S(2)}) collective-permute-start(bf16[256,512]{1,0:T(8,128)(2,1)S(1)} %get-tuple-element.31.refs_0_), channel_id=1, source_target_pairs={{0,2},{1,3},{2,0},{3,1},{4,6},{5,7},{6,4},{7,5},{8,10},{9,11},{10,... | collective-permute-start | bytes 786440 | tf_op jit(solution)/shard_map/ppermute | solution.py:96
  18.8 10.6 %collective-permute-start.2 = (bf16[256,512]{1,0:T(8,128)(2,1)S(1)}, bf16[256,512]{1,0:T(8,128)(2,1)S(1)}, u32[]{:S(2)}, u32[]{:S(2)}) collective-permute-start(bf16[256,512]{1,0:T(8,128)(2,1)S(1)} %get-tuple-element.31.refs_0_), channel_id=1, source_target_pairs={{0,1},{1,0},{2,3},{3,2},{4,5},{5,4},{6,7},{7,6},{8,9},{9,8},{10,11... | collective-permute-start | bytes 786440 | tf_op jit(solution)/shard_map/ppermute | solution.py:96
  18.8 34.0 %collective-permute-start.15 = (bf16[1024,512]{1,0:T(8,128)(2,1)}, bf16[1024,512]{1,0:T(8,128)(2,1)}, u32[]{:S(2)}, u32[]{:S(2)}) collective-permute-start(bf16[1024,512]{1,0:T(8,128)(2,1)} %fps_ref.1), channel_id=1, source_target_pairs={{0,1},{1,0},{2,3},{3,2},{4,5},{5,4},{6,7},{7,6},{8,9},{9,8},{10,11... | collective-permute-start | bytes 3145736 | tf_op jit(solution)/shard_map/ppermute | solution.py:96
  27.9 4.1 %collective-permute-start.7 = (bf16[256,512]{1,0:T(8,128)(2,1)}, bf16[256,512]{1,0:T(8,128)(2,1)S(1)}, u32[]{:S(2)}, u32[]{:S(2)}) collective-permute-start(bf16[256,512]{1,0:T(8,128)(2,1)} %collective-permute-done.6.refs_6_), channel_id=1, source_target_pairs={{0,1},{1,0},{2,3},{3,2},{4,5},{5,4},{6,7},{7,6},{8,9},{9,8},{10,11... | collective-permute-start | bytes 786440 | tf_op jit(solution)/shard_map/ppermute | solution.py:96
  28.4 8.6 %collective-permute-start.9 = (bf16[256,512]{1,0:T(8,128)(2,1)}, bf16[256,512]{1,0:T(8,128)(2,1)}, u32[]{:S(2)}, u32[]{:S(2)}) collective-permute-start(bf16[256,512]{1,0:T(8,128)(2,1)} %collective-permute-done.6.refs_6_), channel_id=1, source_target_pairs={{0,4},{1,5},{2,6},{3,7},{4,0},{5,1},{6,2},{7,3},{8,12},{9,13},{10,... | collective-permute-start | bytes 786440 | tf_op jit(solution)/shard_map/ppermute | solution.py:96
  30.1 3.1 %collective-permute-start.5 = (bf16[256,512]{1,0:T(8,128)(2,1)S(1)}, bf16[256,512]{1,0:T(8,128)(2,1)S(1)}, u32[]{:S(2)}, u32[]{:S(2)}) collective-permute-start(bf16[256,512]{1,0:T(8,128)(2,1)S(1)} %collective-permute-done.refs_4_), channel_id=1, source_target_pairs={{0,1},{1,0},{2,3},{3,2},{4,5},{5,4},{6,7},{7,6},{8,9},{9,8},{10,11... | collective-permute-start | bytes 786440 | tf_op jit(solution)/shard_map/ppermute | solution.py:96
  30.5 21.2 %collective-permute-start.11 = (bf16[256,512]{1,0:T(8,128)(2,1)}, bf16[256,512]{1,0:T(8,128)(2,1)}, u32[]{:S(2)}, u32[]{:S(2)}) collective-permute-start(bf16[256,512]{1,0:T(8,128)(2,1)} %collective-permute-done.6.refs_6_), channel_id=1, source_target_pairs={{0,2},{1,3},{2,0},{3,1},{4,6},{5,7},{6,4},{7,5},{8,10},{9,11},{10,... | collective-permute-start | bytes 786440 | tf_op jit(solution)/shard_map/ppermute | solution.py:96
  32.8 19.0 %collective-permute-start.1 = (bf16[256,512]{1,0:T(8,128)(2,1)S(1)}, bf16[256,512]{1,0:T(8,128)(2,1)}, u32[]{:S(2)}, u32[]{:S(2)}) collective-permute-start(bf16[256,512]{1,0:T(8,128)(2,1)S(1)} %collective-permute-done.refs_4_), channel_id=1, source_target_pairs={{0,2},{1,3},{2,0},{3,1},{4,6},{5,7},{6,4},{7,5},{8,10},{9,11},{10,... | collective-permute-start | bytes 786440 | tf_op jit(solution)/shard_map/ppermute | solution.py:96
  34.0 7.0 %collective-permute-start.4 = (bf16[256,512]{1,0:T(8,128)(2,1)}, bf16[256,512]{1,0:T(8,128)(2,1)}, u32[]{:S(2)}, u32[]{:S(2)}) collective-permute-start(bf16[256,512]{1,0:T(8,128)(2,1)} %collective-permute-done.3.refs_2_), channel_id=1, source_target_pairs={{0,1},{1,0},{2,3},{3,2},{4,5},{5,4},{6,7},{7,6},{8,9},{9,8},{10,11... | collective-permute-start | bytes 786440 | tf_op jit(solution)/shard_map/ppermute | solution.py:96
  37.0 15.4 %collective-permute-start.13 = (bf16[256,512]{1,0:T(8,128)(2,1)}, bf16[256,512]{1,0:T(8,128)(2,1)}, u32[]{:S(2)}, u32[]{:S(2)}) collective-permute-start(bf16[256,512]{1,0:T(8,128)(2,1)} %collective-permute-done.9.refs_2_), channel_id=1, source_target_pairs={{0,2},{1,3},{2,0},{3,1},{4,6},{5,7},{6,4},{7,5},{8,10},{9,11},{10,... | collective-permute-start | bytes 786440 | tf_op jit(solution)/shard_map/ppermute | solution.py:96
  52.4 3.1 %collective-permute-start.14 = (bf16[256,512]{1,0:T(8,128)(2,1)}, bf16[256,512]{1,0:T(8,128)(2,1)S(1)}, u32[]{:S(2)}, u32[]{:S(2)}) collective-permute-start(bf16[256,512]{1,0:T(8,128)(2,1)} %collective-permute-done.13.refs_6_), channel_id=1, source_target_pairs={{0,1},{1,0},{2,3},{3,2},{4,5},{5,4},{6,7},{7,6},{8,9},{9,8},{10,11... | collective-permute-start | bytes 786440 | tf_op jit(solution)/shard_map/ppermute | solution.py:96
  81.2 9.6 %collective-permute-start.17 = (f32[152,256]{1,0:T(8,128)S(1)}, f32[152,256]{1,0:T(8,128)}, u32[]{:S(2)}, u32[]{:S(2)}) collective-permute-start(f32[152,256]{1,0:T(8,128)S(1)} %get-tuple-element.36), channel_id=1, source_target_pairs={{0,2},{1,3},{2,0},{3,1},{4,6},{5,7},{6,4},{7,5},{8,10},{9,11},{10,... | collective-permute-start | bytes 466952 | tf_op jit(solution)/shard_map/ppermute | solution.py:96
  88.5 28.3 %collective-permute-start.21 = (bf16[256,1920]{1,0:T(8,128)(2,1)}, bf16[256,1920]{1,0:T(8,128)(2,1)}, u32[]{:S(2)}, u32[]{:S(2)}) collective-permute-start(bf16[256,1920]{1,0:T(8,128)(2,1)} %get-tuple-element.46), channel_id=1, source_target_pairs={{0,2},{1,3},{2,0},{3,1},{4,6},{5,7},{6,4},{7,5},{8,10},{9,11},{10,... | collective-permute-start | bytes 2949128 | tf_op jit(solution)/shard_map/ppermute | solution.py:96
  93.1 12.5 %collective-permute-start.19 = (f32[176,256]{1,0:T(8,128)}, f32[176,256]{1,0:T(8,128)}, u32[]{:S(2)}, u32[]{:S(2)}) collective-permute-start(f32[176,256]{1,0:T(8,128)} %pad_maximum_fusion.3), channel_id=1, source_target_pairs={{0,4},{1,5},{2,6},{3,7},{4,0},{5,1},{6,2},{7,3},{8,12},{9,13},{10,... | collective-permute-start | bytes 540680 | tf_op jit(solution)/shard_map/ppermute | solution.py:96
  105.2 44.8 %collective-permute-start.18 = (bf16[256,1920]{1,0:T(8,128)(2,1)}, bf16[256,1920]{1,0:T(8,128)(2,1)}, u32[]{:S(2)}, u32[]{:S(2)}) collective-permute-start(bf16[256,1920]{1,0:T(8,128)(2,1)} %get-tuple-element.44), channel_id=1, source_target_pairs={{0,2},{1,3},{2,0},{3,1},{4,6},{5,7},{6,4},{7,5},{8,10},{9,11},{10,... | collective-permute-start | bytes 2949128 | tf_op jit(solution)/shard_map/ppermute | solution.py:96
  107.5 17.7 %collective-permute-start.20 = (f32[224,256]{1,0:T(8,128)S(1)}, f32[224,256]{1,0:T(8,128)S(1)}, u32[]{:S(2)}, u32[]{:S(2)}) collective-permute-start(f32[224,256]{1,0:T(8,128)S(1)} %pad_maximum_fusion.1), channel_id=1, source_target_pairs={{0,8},{1,9},{2,10},{3,11},{4,12},{5,13},{6,14},{7,15},{8,0},{9,1},... | collective-permute-start | bytes 688136 | tf_op jit(solution)/shard_map/ppermute | solution.py:96
  125.3 16.0 %collective-permute-start.23 = (bf16[128,1920]{1,0:T(8,128)(2,1)}, bf16[128,1920]{1,0:T(8,128)(2,1)}, u32[]{:S(2)}, u32[]{:S(2)}) collective-permute-start(bf16[128,1920]{1,0:T(8,128)(2,1)} %slice.163), channel_id=1, source_target_pairs={{0,4},{1,5},{2,6},{3,7},{4,0},{5,1},{6,2},{7,3},{8,12},{9,13},{10,... | collective-permute-start | bytes 1474568 | tf_op jit(solution)/shard_map/ppermute | solution.py:96
  128.7 43.1 %collective-permute-start.26 = (f32[128,1792]{1,0:T(8,128)S(1)}, f32[128,1792]{1,0:T(8,128)S(1)}, u32[]{:S(2)}, u32[]{:S(2)}) collective-permute-start(f32[128,1792]{1,0:T(8,128)S(1)} %fusion.18), channel_id=1, source_target_pairs={{0,1},{1,0},{2,3},{3,2},{4,5},{5,4},{6,7},{7,6},{8,9},{9,8},{10,11... | collective-permute-start | bytes 2752520 | tf_op jit(solution)/shard_map/ppermute | solution.py:96
  155.0 35.0 %collective-permute-start.24 = (bf16[128,1920]{1,0:T(8,128)(2,1)}, bf16[128,1920]{1,0:T(8,128)(2,1)}, u32[]{:S(2)}, u32[]{:S(2)}) collective-permute-start(bf16[128,1920]{1,0:T(8,128)(2,1)} %slice.162), channel_id=1, source_target_pairs={{0,4},{1,5},{2,6},{3,7},{4,0},{5,1},{6,2},{7,3},{8,12},{9,13},{10,... | collective-permute-start | bytes 1474568 | tf_op jit(solution)/shard_map/ppermute | solution.py:96
  155.1 34.9 %collective-permute-start.25 = (bf16[128,1920]{1,0:T(8,128)(2,1)}, bf16[128,1920]{1,0:T(8,128)(2,1)}, u32[]{:S(2)}, u32[]{:S(2)}) collective-permute-start(bf16[128,1920]{1,0:T(8,128)(2,1)} %fusion.22), channel_id=1, source_target_pairs={{0,8},{1,9},{2,10},{3,11},{4,12},{5,13},{6,14},{7,15},{8,0},{9,1},... | collective-permute-start | bytes 1474568 | tf_op jit(solution)/shard_map/ppermute | solution.py:96
  190.0 3.5 %collective-permute-start.27 = (f32[128,1792]{1,0:T(8,128)}, f32[128,1792]{1,0:T(8,128)S(1)}, u32[]{:S(2)}, u32[]{:S(2)}) collective-permute-start(f32[128,1792]{1,0:T(8,128)} %all-reduce.2.cloned.1.call-done), channel_id=1, source_target_pairs={{0,1},{1,0},{2,3},{3,2},{4,5},{5,4},{6,7},{7,6},{8,9},{9,8},{10,11... | collective-permute-start | bytes 2752520 | tf_op jit(solution)/shard_map/ppermute | solution.py:96
  (34 other events, 169.7 us)
Sparse Core Ops, SparseCore 0:
  95.2 94.7 all-reduce.1

commit v7 on v6

--- a/solution.py
+++ b/solution.py
@@ -483,11 +483,11 @@
     held[10] = send(held[8], ROW)
     held[14] = send(held[12], ROW)
     result = None
-    for masks in ((0, 2, 4, 8), (6, 12, 10, 14)):
+    for masks in ((0, 2, 4, 8, 6, 12), (10, 14)):
         owners, chunks = [], []
         for m in masks:
             chunk = held[m]
-            if m in (6, 10, 14):
+            if m in (10, 14):
                 chunk = after(chunk, result)
             owners += [position ^ m, position ^ m ^ 1]
             chunks += [chunk, send(chunk, CORE)]

time: 207 us -> 208 us (level)
  waiting for transfers between devices: 44.1 us -> 48.8 us
  local copies, waits for them, and re-layouts: 25 us -> 21.6 us
    ppermute x28, waiting for transfers between devices: 27.8 us -> 31.7 us  [send(): return lax.ppermute(x, 'dp', perm)]
    unnamed x62, local copies, waits for them, and re-layouts: 18.7 us -> 16.4 us
  transfers between devices with their start and end apart: 29 -> 29, of which waited for: 8 -> 10; matrix products, arithmetic and copies ran while one was open for 15% -> 13% of each run, Pallas kernels for 22% -> 23%
where the time goes in v7:
time: 208 us; the launch traced here: 207 us
  Pallas kernels  77.7 us (37%)
  waiting for transfers between devices  48.8 us (23%)
  starting transfers between devices  23.4 us (11%)
  local copies, waits for them, and re-layouts  21.6 us (10%)
  other arithmetic  14.7 us (7%)
  between operations  14.6 us (7%)
  matrix products  5.82 us (3%)
    ppermute x28, waiting for transfers between devices, send(): return lax.ppermute(x, 'dp', perm)  31.7 us
    pallas_call x4, Pallas kernels, eliminate_blocks(): pl.pallas_call(functools.partial(factor_body, blocks), in_specs=vmem(1),...  27 us
    ppermute x28, starting transfers between devices, send(): return lax.ppermute(x, 'dp', perm)  23.4 us
    pallas_call x1, Pallas kernels, stage(): pl.pallas_call(stage_body, grid_spec=pltpu.PrefetchScalarGridSpec(num_sca...  17.6 us
    psum x1, waiting for transfers between devices, local_16(): part = lax.psum(rest_rows, 'dp', axis_index_groups=planes)  17.1 us
    unnamed x62, local copies, waits for them, and re-layouts  16.4 us
    pallas_call x2, Pallas kernels, place(): pl.pallas_call(functools.partial(place_body, len(chunks)), grid=(landmark...  14.3 us
    pallas_call x2, Pallas kernels, pieces(): pl.pallas_call(pieces_body, in_specs=[pl.BlockSpec(memory_space=pltpu.SME...  10.9 us
  transfers between devices with their start and end apart: 29, of which 10 were waited for; matrix products, arithmetic and copies ran while one was open for 13% of the time, Pallas kernels for 23%

profile of v7, /device:TPU:0, one launch (start us, length us, event | category | flops | bytes accessed | tf_op | source)
XLA Modules:
  0.0 206.7 jit_solution(11188779002130078801)
XLA Ops:
  7.9 3.7 %pack.1 = (bf16[256,512]{1,0:T(8,128)(2,1)S(1)}, f32[2048,128]{1,0:T(8,128)S(1)}) custom-call(s32[1]{0:T(128)} %bitcast.9.at_ref, s32[1,2048]{1,0:T(1,128)S(1)} %bitcast.44, bf16[1024,512]{1,0:T(8,128)(2,1)} %fps_ref.1), custom_call_target="tpu_custom_call" | custom-call | tf_op jit(solution)/shard_map/pack/pallas_call | solution.py:419
  11.6 4.1 %collective-permute-start = (bf16[256,512]{1,0:T(8,128)(2,1)S(1)}, bf16[256,512]{1,0:T(8,128)(2,1)S(1)}, u32[]{:S(2)}, u32[]{:S(2)}) collective-permute-start(bf16[256,512]{1,0:T(8,128)(2,1)S(1)} %get-tuple-element.30.refs_0_), channel_id=1, source_target_pairs={{0,8},{1,9},{2,10},{3,11},{4,12},{5,13},{6,14},{7,15},{8,0},{9,1},... | collective-permute-start | bytes 786440 | tf_op jit(solution)/shard_map/ppermute | solution.py:96
  20.1 7.6 %collective-permute-done.refs_6_ = bf16[256,512]{1,0:T(8,128)(2,1)S(1)} collective-permute-done((bf16[256,512]{1,0:T(8,128)(2,1)S(1)}, bf16[256,512]{1,0:T(8,128)(2,1)S(1)}, u32[]{:S(2)}, u32[]{:S(2)}) %collective-permute-start) | collective-permute-done | bytes 262176 | tf_op jit(solution)/shard_map/ppermute | solution.py:96
  32.0 4.5 %collective-permute-done.10.refs_10_ = bf16[256,512]{1,0:T(8,128)(2,1)S(1)} collective-permute-done((bf16[256,512]{1,0:T(8,128)(2,1)S(1)}, bf16[256,512]{1,0:T(8,128)(2,1)S(1)}, u32[]{:S(2)}, u32[]{:S(2)}) %collective-permute-start.10) | collective-permute-done | bytes 262176 | tf_op jit(solution)/shard_map/ppermute | solution.py:96
  46.1 9.5 %place.2.refs_4_ = bf16[2048,512]{1,0:T(8,128)(2,1)S(1)} custom-call(s32[12]{0:T(128)S(1)} %broadcast_multiply_fusion.2.base_ref, f32[2048,128]{1,0:T(8,128)S(1)} %get-tuple-element.29.slots_ref, bf16[256,512]{1,0:T(8,128)(2,1)S(1)} %copy-done.13, bf16[256,512]{1,0:T(8,128)(2,1)S(1)} %copy-done.15, bf16[256,512]{1,0:T(8,128)(2,1)} %collective-permute-done.3.refs_2_, ...), custom_call_target="tpu_custom_call" | custom-call | tf_op jit(solution)/shard_map/place/pallas_call | solution.py:459
  58.9 4.8 %place.3.land_ref = bf16[2048,512]{1,0:T(8,128)(2,1)S(1)} custom-call(s32[4]{0:T(128)S(1)} %add_multiply_fusion.base_ref, f32[2048,128]{1,0:T(8,128)S(1)} %get-tuple-element.29.slots_ref, bf16[256,512]{1,0:T(8,128)(2,1)} %collective-permute-done.1.refs_0_, bf16[256,512]{1,0:T(8,128)(2,1)S(1)} %collective-permute-done.12.refs_1_, ...), custom_call_target="tpu_custom_call" | custom-call | tf_op jit(solution)/shard_map/place/pallas_call | solution.py:459
  63.7 17.6 %stage.1 = (bf16[2048,2048]{1,0:T(8,128)(2,1)S(1)}, f32[8,128,128]{2,1,0:T(8,128)S(1)}, f32[128,1792]{1,0:T(8,128)S(1)}, f32[152,256]{1,0:T(8,128)S(1)}, f32[1,2048]{1,0:T(1,128)S(1)}, /*index=5*/f32[2048,128]{1,0:T(8,128)S(1)}) custom-call(s32[1]{0:T(128)} %bitcast.4.core_ref, bf16[2048,512]{1,0:T(8,128)(2,1)S(1)} %place.3.land_ref, ...), custom_call_target="tpu_custom_call" | custom-call | tf_op jit(solution)/shard_map/stage/pallas_call | solution.py:216
  83.9 5.5 %pieces.2 = (f32[256,1920]{1,0:T(8,128)S(1)}, bf16[256,1920]{1,0:T(8,128)(2,1)}) custom-call(s32[4]{0:T(128)S(1)} %get-tuple-element.63.at_ref, bf16[2048,2048]{1,0:T(8,128)(2,1)S(1)} %get-tuple-element.40.ct_ref, f32[1,2048]{1,0:T(1,128)S(1)} %get-tuple-element.35.lead_ref, f32[2048,128]{1,0:T(8,128)S(1)} %get-tuple-element.36.column_ref, ...), custom_call_target="tpu_custom_call" | custom-call | flops 1 | bytes 1 | tf_op jit(solution)/shard_map/pieces/pallas_call | solution.py:273
  95.5 3.4 %copy-done.1 = bf16[2048,2048]{1,0:T(8,128)(2,1)S(1)} copy-done((bf16[2048,2048]{1,0:T(8,128)(2,1)S(1)}, bf16[2048,2048]{1,0:T(8,128)(2,1)}, u32[]{:S(2)}) %copy-start.1) | copy-done | bytes 8388632
  99.9 5.5 %pieces.3 = (f32[256,1920]{1,0:T(8,128)S(1)}, bf16[256,1920]{1,0:T(8,128)(2,1)}) custom-call(s32[4]{0:T(128)S(1)} %get-tuple-element.62.at_ref, bf16[2048,2048]{1,0:T(8,128)(2,1)S(1)} %copy-done.1, f32[1,2048]{1,0:T(1,128)S(1)} %get-tuple-element.35.lead_ref, f32[2048,128]{1,0:T(8,128)S(1)} %get-tuple-element.36.column_ref, f32[8,128,128]{2,1,0:T(8,128)S(1)} %copy-done.6), custom_call_target="tpu_custom_call" | custom-call | flops 1 | bytes 1 | tf_op jit(solution)/shard_map/pieces/pallas_call | solution.py:273
  108.7 3.0 %collective-permute-start.20 = (f32[224,256]{1,0:T(8,128)S(1)}, f32[224,256]{1,0:T(8,128)S(1)}, u32[]{:S(2)}, u32[]{:S(2)}) collective-permute-start(f32[224,256]{1,0:T(8,128)S(1)} %pad_maximum_fusion.1), channel_id=1, source_target_pairs={{0,8},{1,9},{2,10},{3,11},{4,12},{5,13},{6,14},{7,15},{8,0},{9,1},... | collective-permute-start | bytes 688136 | tf_op jit(solution)/shard_map/ppermute | solution.py:96
  111.7 7.2 %collective-permute-done.21 = bf16[256,1920]{1,0:T(8,128)(2,1)} collective-permute-done((bf16[256,1920]{1,0:T(8,128)(2,1)}, bf16[256,1920]{1,0:T(8,128)(2,1)}, u32[]{:S(2)}, u32[]{:S(2)}) %collective-permute-start.21) | collective-permute-done | bytes 983072 | tf_op jit(solution)/shard_map/ppermute | solution.py:96
  121.8 5.1 %collective-permute-done.20 = f32[224,256]{1,0:T(8,128)S(1)} collective-permute-done((f32[224,256]{1,0:T(8,128)S(1)}, f32[224,256]{1,0:T(8,128)S(1)}, u32[]{:S(2)}, u32[]{:S(2)}) %collective-permute-start.20) | collective-permute-done | bytes 229408 | tf_op jit(solution)/shard_map/ppermute | solution.py:96
  130.7 7.1 %factor.4.state_ref = f32[256,512]{1,0:T(8,128)S(1)} custom-call(f32[256,512]{1,0:T(8,128)S(1)} %pad_maximum_fusion.state_ref), custom_call_target="tpu_custom_call" | custom-call | flops 1 | bytes 1 | tf_op jit(solution)/shard_map/factor/pallas_call | solution.py:331
  137.8 5.1 %collective-permute-done.23 = bf16[128,1920]{1,0:T(8,128)(2,1)} collective-permute-done((bf16[128,1920]{1,0:T(8,128)(2,1)}, bf16[128,1920]{1,0:T(8,128)(2,1)}, u32[]{:S(2)}, u32[]{:S(2)}) %collective-permute-start.23) | collective-permute-done | bytes 491552 | tf_op jit(solution)/shard_map/ppermute | solution.py:96
  142.9 1.9 fusion.19
  144.8 6.8 %factor.5.state_ref = f32[256,512]{1,0:T(8,128)S(1)} custom-call(f32[256,512]{1,0:T(8,128)S(1)} %factor.4.state_ref), custom_call_target="tpu_custom_call" | custom-call | flops 1 | bytes 1 | tf_op jit(solution)/shard_map/factor/pallas_call | solution.py:331
  154.5 2.2 %collective-permute-start.25 = (bf16[128,1920]{1,0:T(8,128)(2,1)}, bf16[128,1920]{1,0:T(8,128)(2,1)}, u32[]{:S(2)}, u32[]{:S(2)}) collective-permute-start(bf16[128,1920]{1,0:T(8,128)(2,1)} %fusion.19), channel_id=1, source_target_pairs={{0,8},{1,9},{2,10},{3,11},{4,12},{5,13},{6,14},{7,15},{8,0},{9,1},... | collective-permute-start | bytes 1474568 | tf_op jit(solution)/shard_map/ppermute | solution.py:96
  156.7 1.8 convolution_multiply_fusion
  158.6 6.8 %factor.6.state_ref = f32[256,512]{1,0:T(8,128)S(1)} custom-call(f32[256,512]{1,0:T(8,128)S(1)} %factor.5.state_ref), custom_call_target="tpu_custom_call" | custom-call | flops 1 | bytes 1 | tf_op jit(solution)/shard_map/factor/pallas_call | solution.py:331
  165.4 6.3 %factor.7.state_ref = f32[256,512]{1,0:T(8,128)S(1)} custom-call(f32[256,512]{1,0:T(8,128)S(1)} %factor.6.state_ref), custom_call_target="tpu_custom_call" | custom-call | flops 1 | bytes 1 | tf_op jit(solution)/shard_map/factor/pallas_call | solution.py:331
  171.7 1.9 fusion.3.added_ref
  173.6 17.1 %all-reduce.2.cloned.1.call-done = f32[128,1792]{1,0:T(8,128)} async-done(((f32[128,1792]{1,0:T(8,128)}), f32[128,1792]{1,0:T(8,128)}) %all-reduce.2.cloned.1.call-update) | async-done | bytes 917520 | tf_op jit(solution)/shard_map/psum | solution.py:532
  195.7 4.1 %finish.1 = (f32[128,256]{1,0:T(8,128)}, f32[128,2048]{1,0:T(8,128)}) custom-call(s32[1]{0:T(128)} %bitcast.31.at_ref, f32[256,512]{1,0:T(8,128)S(1)} %factor.7.state_ref, f32[256,256]{1,0:T(8,128)S(1)} %fusion.24.corner_ref, f32[256,1792]{1,0:T(8,128)S(1)} %fusion.1.sums_ref, f32[256,1792]{1,0:T(8,128)S(1)} %copy-done.4, f32[128,1792]{1,0:T(8,128)S(1)} %fusion.20.rest_ref), custom_call_target="tpu_custom_call" | custom-call | tf_op jit(solution)/shard_map/finish/pallas_call | solution.py:368
  (153 shorter events, 49.3 us)
Async XLA Ops:
  7.2 183.6 %all-reduce.2.cloned.1.call-start = ((), (), s32[]{:S(2)}) async-start(), calls=%async_computation | async-start | bytes 1835008 | tf_op jit(solution)/shard_map/psum | solution.py:532
  11.6 16.1 %collective-permute-start = (bf16[256,512]{1,0:T(8,128)(2,1)S(1)}, bf16[256,512]{1,0:T(8,128)(2,1)S(1)}, u32[]{:S(2)}, u32[]{:S(2)}) collective-permute-start(bf16[256,512]{1,0:T(8,128)(2,1)S(1)} %get-tuple-element.30.refs_0_), channel_id=1, source_target_pairs={{0,8},{1,9},{2,10},{3,11},{4,12},{5,13},{6,14},{7,15},{8,0},{9,1},... | collective-permute-start | bytes 786440 | tf_op jit(solution)/shard_map/ppermute | solution.py:96
  15.7 12.3 %collective-permute-start.5 = (bf16[256,512]{1,0:T(8,128)(2,1)S(1)}, bf16[256,512]{1,0:T(8,128)(2,1)}, u32[]{:S(2)}, u32[]{:S(2)}) collective-permute-start(bf16[256,512]{1,0:T(8,128)(2,1)S(1)} %get-tuple-element.30.refs_0_), channel_id=1, source_target_pairs={{0,4},{1,5},{2,6},{3,7},{4,0},{5,1},{6,2},{7,3},{8,12},{9,13},{10,... | collective-permute-start | bytes 786440 | tf_op jit(solution)/shard_map/ppermute | solution.py:96
  17.3 39.0 %collective-permute-start.15 = (bf16[1024,512]{1,0:T(8,128)(2,1)}, bf16[1024,512]{1,0:T(8,128)(2,1)}, u32[]{:S(2)}, u32[]{:S(2)}) collective-permute-start(bf16[1024,512]{1,0:T(8,128)(2,1)} %fps_ref.1), channel_id=1, source_target_pairs={{0,1},{1,0},{2,3},{3,2},{4,5},{5,4},{6,7},{7,6},{8,9},{9,8},{10,11... | collective-permute-start | bytes 3145736 | tf_op jit(solution)/shard_map/ppermute | solution.py:96
  17.3 12.2 %collective-permute-start.3 = (bf16[256,512]{1,0:T(8,128)(2,1)S(1)}, bf16[256,512]{1,0:T(8,128)(2,1)}, u32[]{:S(2)}, u32[]{:S(2)}) collective-permute-start(bf16[256,512]{1,0:T(8,128)(2,1)S(1)} %get-tuple-element.30.refs_0_), channel_id=1, source_target_pairs={{0,2},{1,3},{2,0},{3,1},{4,6},{5,7},{6,4},{7,5},{8,10},{9,11},{10,... | collective-permute-start | bytes 786440 | tf_op jit(solution)/shard_map/ppermute | solution.py:96
  18.8 10.7 %collective-permute-start.2 = (bf16[256,512]{1,0:T(8,128)(2,1)S(1)}, bf16[256,512]{1,0:T(8,128)(2,1)S(1)}, u32[]{:S(2)}, u32[]{:S(2)}) collective-permute-start(bf16[256,512]{1,0:T(8,128)(2,1)S(1)} %get-tuple-element.30.refs_0_), channel_id=1, source_target_pairs={{0,1},{1,0},{2,3},{3,2},{4,5},{5,4},{6,7},{7,6},{8,9},{9,8},{10,11... | collective-permute-start | bytes 786440 | tf_op jit(solution)/shard_map/ppermute | solution.py:96
  27.7 4.0 %collective-permute-start.16 = (bf16[1024,128]{0,1:T(8,128)(2,1)S(1)}, bf16[1024,128]{0,1:T(8,128)(2,1)S(1)}, u32[]{:S(2)}, u32[]{:S(2)}) collective-permute-start(bf16[1024,128]{0,1:T(8,128)(2,1)S(1)} %copy.7), channel_id=1, source_target_pairs={{0,1},{1,0},{2,3},{3,2},{4,5},{5,4},{6,7},{7,6},{8,9},{9,8},{10,11... | collective-permute-start | bytes 786440 | tf_op jit(solution)/shard_map/ppermute | solution.py:96
  28.1 8.4 %collective-permute-start.10 = (bf16[256,512]{1,0:T(8,128)(2,1)S(1)}, bf16[256,512]{1,0:T(8,128)(2,1)S(1)}, u32[]{:S(2)}, u32[]{:S(2)}) collective-permute-start(bf16[256,512]{1,0:T(8,128)(2,1)S(1)} %collective-permute-done.refs_6_), channel_id=1, source_target_pairs={{0,4},{1,5},{2,6},{3,7},{4,0},{5,1},{6,2},{7,3},{8,12},{9,13},{10,... | collective-permute-start | bytes 786440 | tf_op jit(solution)/shard_map/ppermute | solution.py:96
  29.5 11.3 %collective-permute-start.7 = (bf16[256,512]{1,0:T(8,128)(2,1)S(1)}, bf16[256,512]{1,0:T(8,128)(2,1)}, u32[]{:S(2)}, u32[]{:S(2)}) collective-permute-start(bf16[256,512]{1,0:T(8,128)(2,1)S(1)} %collective-permute-done.refs_6_), channel_id=1, source_target_pairs={{0,1},{1,0},{2,3},{3,2},{4,5},{5,4},{6,7},{7,6},{8,9},{9,8},{10,11... | collective-permute-start | bytes 786440 | tf_op jit(solution)/shard_map/ppermute | solution.py:96
  30.2 9.0 %collective-permute-start.8 = (bf16[256,512]{1,0:T(8,128)(2,1)}, bf16[256,512]{1,0:T(8,128)(2,1)}, u32[]{:S(2)}, u32[]{:S(2)}) collective-permute-start(bf16[256,512]{1,0:T(8,128)(2,1)} %collective-permute-done.5.refs_4_), channel_id=1, source_target_pairs={{0,2},{1,3},{2,0},{3,1},{4,6},{5,7},{6,4},{7,5},{8,10},{9,11},{10,... | collective-permute-start | bytes 786440 | tf_op jit(solution)/shard_map/ppermute | solution.py:96
  31.8 9.0 %collective-permute-start.6 = (bf16[256,512]{1,0:T(8,128)(2,1)}, bf16[256,512]{1,0:T(8,128)(2,1)}, u32[]{:S(2)}, u32[]{:S(2)}) collective-permute-start(bf16[256,512]{1,0:T(8,128)(2,1)} %collective-permute-done.5.refs_4_), channel_id=1, source_target_pairs={{0,1},{1,0},{2,3},{3,2},{4,5},{5,4},{6,7},{7,6},{8,9},{9,8},{10,11... | collective-permute-start | bytes 786440 | tf_op jit(solution)/shard_map/ppermute | solution.py:96
  37.2 4.2 %collective-permute-start.4 = (bf16[256,512]{1,0:T(8,128)(2,1)}, bf16[256,512]{1,0:T(8,128)(2,1)}, u32[]{:S(2)}, u32[]{:S(2)}) collective-permute-start(bf16[256,512]{1,0:T(8,128)(2,1)} %collective-permute-done.3.refs_2_), channel_id=1, source_target_pairs={{0,1},{1,0},{2,3},{3,2},{4,5},{5,4},{6,7},{7,6},{8,9},{9,8},{10,11... | collective-permute-start | bytes 786440 | tf_op jit(solution)/shard_map/ppermute | solution.py:96
  39.3 16.6 %collective-permute-start.1 = (bf16[256,512]{1,0:T(8,128)(2,1)S(1)}, bf16[256,512]{1,0:T(8,128)(2,1)}, u32[]{:S(2)}, u32[]{:S(2)}) collective-permute-start(bf16[256,512]{1,0:T(8,128)(2,1)S(1)} %collective-permute-done.refs_6_), channel_id=1, source_target_pairs={{0,2},{1,3},{2,0},{3,1},{4,6},{5,7},{6,4},{7,5},{8,10},{9,11},{10,... | collective-permute-start | bytes 786440 | tf_op jit(solution)/shard_map/ppermute | solution.py:96
  40.8 14.9 %collective-permute-start.13 = (bf16[256,512]{1,0:T(8,128)(2,1)}, bf16[256,512]{1,0:T(8,128)(2,1)}, u32[]{:S(2)}, u32[]{:S(2)}) collective-permute-start(bf16[256,512]{1,0:T(8,128)(2,1)} %copy-done.16), channel_id=1, source_target_pairs={{0,2},{1,3},{2,0},{3,1},{4,6},{5,7},{6,4},{7,5},{8,10},{9,11},{10,... | collective-permute-start | bytes 786440 | tf_op jit(solution)/shard_map/ppermute | solution.py:96
  82.3 9.6 %collective-permute-start.17 = (f32[152,256]{1,0:T(8,128)S(1)}, f32[152,256]{1,0:T(8,128)}, u32[]{:S(2)}, u32[]{:S(2)}) collective-permute-start(f32[152,256]{1,0:T(8,128)S(1)} %get-tuple-element.34), channel_id=1, source_target_pairs={{0,2},{1,3},{2,0},{3,1},{4,6},{5,7},{6,4},{7,5},{8,10},{9,11},{10,... | collective-permute-start | bytes 466952 | tf_op jit(solution)/shard_map/ppermute | solution.py:96
  90.6 28.3 %collective-permute-start.21 = (bf16[256,1920]{1,0:T(8,128)(2,1)}, bf16[256,1920]{1,0:T(8,128)(2,1)}, u32[]{:S(2)}, u32[]{:S(2)}) collective-permute-start(bf16[256,1920]{1,0:T(8,128)(2,1)} %get-tuple-element.44), channel_id=1, source_target_pairs={{0,2},{1,3},{2,0},{3,1},{4,6},{5,7},{6,4},{7,5},{8,10},{9,11},{10,... | collective-permute-start | bytes 2949128 | tf_op jit(solution)/shard_map/ppermute | solution.py:96
  94.2 12.7 %collective-permute-start.19 = (f32[176,256]{1,0:T(8,128)}, f32[176,256]{1,0:T(8,128)}, u32[]{:S(2)}, u32[]{:S(2)}) collective-permute-start(f32[176,256]{1,0:T(8,128)} %pad_maximum_fusion.3), channel_id=1, source_target_pairs={{0,4},{1,5},{2,6},{3,7},{4,0},{5,1},{6,2},{7,3},{8,12},{9,13},{10,... | collective-permute-start | bytes 540680 | tf_op jit(solution)/shard_map/ppermute | solution.py:96
  105.4 46.3 %collective-permute-start.18 = (bf16[256,1920]{1,0:T(8,128)(2,1)}, bf16[256,1920]{1,0:T(8,128)(2,1)}, u32[]{:S(2)}, u32[]{:S(2)}) collective-permute-start(bf16[256,1920]{1,0:T(8,128)(2,1)} %get-tuple-element.42), channel_id=1, source_target_pairs={{0,2},{1,3},{2,0},{3,1},{4,6},{5,7},{6,4},{7,5},{8,10},{9,11},{10,... | collective-permute-start | bytes 2949128 | tf_op jit(solution)/shard_map/ppermute | solution.py:96
  108.7 18.3 %collective-permute-start.20 = (f32[224,256]{1,0:T(8,128)S(1)}, f32[224,256]{1,0:T(8,128)S(1)}, u32[]{:S(2)}, u32[]{:S(2)}) collective-permute-start(f32[224,256]{1,0:T(8,128)S(1)} %pad_maximum_fusion.1), channel_id=1, source_target_pairs={{0,8},{1,9},{2,10},{3,11},{4,12},{5,13},{6,14},{7,15},{8,0},{9,1},... | collective-permute-start | bytes 688136 | tf_op jit(solution)/shard_map/ppermute | solution.py:96
  127.0 15.9 %collective-permute-start.23 = (bf16[128,1920]{1,0:T(8,128)(2,1)}, bf16[128,1920]{1,0:T(8,128)(2,1)}, u32[]{:S(2)}, u32[]{:S(2)}) collective-permute-start(bf16[128,1920]{1,0:T(8,128)(2,1)} %slice.163), channel_id=1, source_target_pairs={{0,4},{1,5},{2,6},{3,7},{4,0},{5,1},{6,2},{7,3},{8,12},{9,13},{10,... | collective-permute-start | bytes 1474568 | tf_op jit(solution)/shard_map/ppermute | solution.py:96
  130.5 41.2 %collective-permute-start.26 = (f32[128,1792]{1,0:T(8,128)S(1)}, f32[128,1792]{1,0:T(8,128)S(1)}, u32[]{:S(2)}, u32[]{:S(2)}) collective-permute-start(f32[128,1792]{1,0:T(8,128)S(1)} %fusion.15), channel_id=1, source_target_pairs={{0,1},{1,0},{2,3},{3,2},{4,5},{5,4},{6,7},{7,6},{8,9},{9,8},{10,11... | collective-permute-start | bytes 2752520 | tf_op jit(solution)/shard_map/ppermute | solution.py:96
  154.3 36.4 %collective-permute-start.24 = (bf16[128,1920]{1,0:T(8,128)(2,1)}, bf16[128,1920]{1,0:T(8,128)(2,1)}, u32[]{:S(2)}, u32[]{:S(2)}) collective-permute-start(bf16[128,1920]{1,0:T(8,128)(2,1)} %slice.162), channel_id=1, source_target_pairs={{0,4},{1,5},{2,6},{3,7},{4,0},{5,1},{6,2},{7,3},{8,12},{9,13},{10,... | collective-permute-start | bytes 1474568 | tf_op jit(solution)/shard_map/ppermute | solution.py:96
  154.5 36.3 %collective-permute-start.25 = (bf16[128,1920]{1,0:T(8,128)(2,1)}, bf16[128,1920]{1,0:T(8,128)(2,1)}, u32[]{:S(2)}, u32[]{:S(2)}) collective-permute-start(bf16[128,1920]{1,0:T(8,128)(2,1)} %fusion.19), channel_id=1, source_target_pairs={{0,8},{1,9},{2,10},{3,11},{4,12},{5,13},{6,14},{7,15},{8,0},{9,1},... | collective-permute-start | bytes 1474568 | tf_op jit(solution)/shard_map/ppermute | solution.py:96
  190.7 3.5 %collective-permute-start.27 = (f32[128,1792]{1,0:T(8,128)}, f32[128,1792]{1,0:T(8,128)S(1)}, u32[]{:S(2)}, u32[]{:S(2)}) collective-permute-start(f32[128,1792]{1,0:T(8,128)} %all-reduce.2.cloned.1.call-done), channel_id=1, source_target_pairs={{0,1},{1,0},{2,3},{3,2},{4,5},{5,4},{6,7},{7,6},{8,9},{9,8},{10,11... | collective-permute-start | bytes 2752520 | tf_op jit(solution)/shard_map/ppermute | solution.py:96
  (34 other events, 187.3 us)
Sparse Core Ops, SparseCore 0:
  95.4 95.2 all-reduce.1
